TPU v7x, 256 devices: a whole 4x4x8 slice. The times are simulated.
256 devices in a mesh: ctx: 32 (over z, x), head: 8 (over y, core).
Axes of the slice: x: 4, y: 4, z: 8, core: 2. Of those that a mesh axis runs over, the one named last changes fastest.
Arguments:
- lin_query: bfloat16 [12288, 8192], P('ctx', 'head'), may hold values from -4 to 4
- lin_key: bfloat16 [12288, 8192], P('ctx', 'head'), may hold values from -4 to 4
- lin_value: bfloat16 [12288, 8192], P('ctx', 'head'), may hold values from -400 to 400
- lin_gate: bfloat16 [12288, 8192], P('ctx', 'head'), may hold values from -8 to 8
- lin_decay: float32 [12288, 64], P('ctx', 'head'), may hold values from -1 to 0
- norm_gain: float32 [8192], P('head'), may hold values from 0.25 to 1.75
- soft_query: bfloat16 [12288, 8192], P('ctx', 'head'), may hold values from -6.5 to 6.5
- soft_key: bfloat16 [12288, 1024], P('ctx', 'head'), may hold values from -6.5 to 6.5
- soft_value: bfloat16 [12288, 1024], P('ctx', 'head'), may hold values from -6 to 6
- starts: int32 [4], replicated, may hold values from 1 to 9408, as said below
- lengths: int32 [4], replicated, may hold values from 1536 to 3072, as said below
Outputs:
- lin_out: bfloat16 [12288, 8192], P('ctx', 'head')
- soft_out: bfloat16 [12288, 8192], P('ctx', 'head')
Inputs may be any that keep to these rules, and one draw needn't show every extreme that they name: `starts`: sequence s begins 1 to min(384, 192) positions after s * 3072; sequences 1 and 2 begin at the same offset, no sequence runs into the next, and the last one ends at the pack's end. `lengths`: sequence 1 has length 3072 in every draw.
All inputs are finite; a program needn't handle non-finite values.
Results may differ from a plain program's by a relative error of at most 0.012.
Values may be sent and summed in bfloat16 or wider, within the bound.
No kernel may reach another device: no remote copies, remote signals or barrier semaphores. Data moves between devices by JAX's collectives and lax.ppermute only.
A program may use at most 128 MiB of HBM per device.

v0:
```python
import functools
import jax
import jax.numpy as jnp
from jax import lax
from jax.experimental import pallas as pl
from jax.experimental.pallas import tpu as pltpu
from jax.sharding import PartitionSpec as P


T = 384
D = 128
H = 8
SPAN = 8
NEG = -1e30
GROUP = 2
EPS = 1e-06
GONE = -1e5
ROW = 4
PAIR = H // ROW
EXTRA = 16
HI = lax.Precision.HIGHEST
F32 = jnp.float32
BF16 = jnp.bfloat16
NT = (((1,), (1,)), ((), ()))
TN = (((0,), (0,)), ((), ()))


def iota(shape, axis):
    return lax.broadcasted_iota(jnp.int32, shape, axis)


def marks(starts, lengths):
    device = lax.axis_index("ctx")
    room = device // SPAN
    place = device % SPAN
    first = device * T
    at_start = place == 0
    bound = jnp.where(at_start, starts[room] - first, 0)
    earlier = jnp.maximum(room - 1, 0)
    end_prev = jnp.where(at_start & (room > 0), starts[earlier] + lengths[earlier] - first, 0)
    end_cur = starts[room] + lengths[room] - first
    return room, place, bound, end_prev, end_cur


def valid_rows(shape, bound, end_prev, end_cur):
    rows = iota(shape, 0)
    return rows < jnp.where(rows < bound, end_prev, end_cur)


def state_kernel(starts, lengths, key, value, dec_t, soft_key, soft_value, s0, s1, s2, s3, cum,
                 cum_t, both, pack, rest):
    both[:, 0:D] = soft_key[...]
    both[:, D:2 * D] = soft_value[...]
    _, place, bound, _, end_cur = marks(starts, lengths)
    lower = (iota((T, T), 1) <= iota((T, T), 0)).astype(F32)
    dec = dec_t[...]
    col = lax.dot_general(lower, dec, NT, precision=HI, preferred_element_type=F32)
    cum[...] = col
    cum_t[...] = lax.dot_general(dec, lower, NT, precision=HI, preferred_element_type=F32)
    rows = iota((T, 1), 0)
    keep = (rows >= bound) & (rows < end_cur)
    last = col[T - 1:T, :]
    to_end = jnp.where(keep, jnp.exp(last - col), 0.0)
    total = jnp.where(place == 0, GONE, last)
    for h in range(H):
        part = slice(h * D, (h + 1) * D)
        scaled = (key[:, part].astype(F32) * to_end[:, h:h + 1]).astype(BF16)
        state = lax.dot_general(scaled, value[:, part], TN, preferred_element_type=F32)
        pack[h // PAIR, (h % PAIR) * D:(h % PAIR + 1) * D, :] = state.astype(BF16)
    at = iota((EXTRA, D), 0)
    for w in range(ROW):
        table = jnp.zeros((EXTRA, D), F32)
        for j in range(PAIR):
            one = jnp.broadcast_to(total[:, w * PAIR + j:w * PAIR + j + 1], (EXTRA, D))
            a = one.astype(BF16).astype(F32)
            b = (one - a).astype(BF16).astype(F32)
            c = one - a - b
            for i, x in enumerate((a, b, c)):
                table = jnp.where(at == 3 * j + i, x, table)
        rest[w] = table.astype(BF16)
    x = place % ROW
    for step, out in enumerate((s0, s1, s2, s3)):
        w = (x + step) % ROW
        out[0:PAIR * D, :] = pack[w]
        out[PAIR * D:PAIR * D + EXTRA, :] = rest[w]


def log_decays(ref):
    table = ref[PAIR * D:PAIR * D + EXTRA, :].astype(F32)
    return [table[3 * j:3 * j + 1] + table[3 * j + 1:3 * j + 2] + table[3 * j + 2:3 * j + 3]
            for j in range(PAIR)]


def gather_row(own, r1, r2, r3, states, logs):
    x = (lax.axis_index("ctx") % SPAN) % ROW
    for step, ref in enumerate((own, r1, r2, r3)):
        w = (x - step + ROW) % ROW
        states[w] = ref[0:PAIR * D, :].astype(F32)
        for j, one in enumerate(log_decays(ref)):
            logs[w, 8 * j:8 * j + 8, :] = jnp.broadcast_to(one, (8, D))


def row_kernel(own, r1, r2, r3, out, states, logs):
    gather_row(own, r1, r2, r3, states, logs)
    at = iota((EXTRA, D), 0)
    table = jnp.zeros((EXTRA, D), F32)
    for j in range(PAIR):
        part = slice(j * D, (j + 1) * D)
        c = [logs[w, 8 * j:8 * j + 1, :] for w in range(ROW)]
        total = (states[3, part, :] + jnp.exp(c[3]) * states[2, part, :]
                 + jnp.exp(c[3] + c[2]) * states[1, part, :]
                 + jnp.exp(c[3] + c[2] + c[1]) * states[0, part, :])
        out[part, :] = total.astype(BF16)
        one = jnp.broadcast_to(c[0] + c[1] + c[2] + c[3], (EXTRA, D))
        a = one.astype(BF16).astype(F32)
        b = (one - a).astype(BF16).astype(F32)
        for i, x in enumerate((a, b, one - a - b)):
            table = jnp.where(at == 3 * j + i, x, table)
    out[PAIR * D:PAIR * D + EXTRA, :] = table.astype(BF16)


def prefix_kernel(own, r1, r2, r3, z1, z2, p0, p1, p2, p3, states, logs, ready):
    gather_row(own, r1, r2, r3, states, logs)
    decay = log_decays(z1)
    for j in range(PAIR):
        part = slice(j * D, (j + 1) * D)
        c = [logs[w, 8 * j:8 * j + 1, :] for w in range(ROW)]
        state = (z1[part, :].astype(F32) + jnp.exp(decay[j]) * z2[part, :].astype(F32))
        ready[0, part, :] = state.astype(BF16)
        state1 = states[0, part, :]
        ready[1, part, :] = (state1 + jnp.exp(c[0]) * state).astype(BF16)
        state2 = states[1, part, :] + jnp.exp(c[1]) * state1
        ready[2, part, :] = (state2 + jnp.exp(c[0] + c[1]) * state).astype(BF16)
        state3 = states[2, part, :] + jnp.exp(c[2]) * state2
        ready[3, part, :] = (state3 + jnp.exp(c[0] + c[1] + c[2]) * state).astype(BF16)
    x = (lax.axis_index("ctx") % SPAN) % ROW
    for step, out in enumerate((p0, p1, p2, p3)):
        out[...] = ready[(x + step) % ROW]


def intra_kernel(starts, lengths, query, key, value, cum, cum_t, out, bias):
    _, _, bound, _, _ = marks(starts, lengths)
    t = iota((T, T), 0)
    i = iota((T, T), 1)
    seen = (i <= t) & ((i >= bound) | (t < bound))
    bias[...] = jnp.where(seen, 0.0, NEG)
    for h in range(H):
        lanes = slice(h * D, (h + 1) * D)
        for r in range(T // D):
            part = slice(r * D, (r + 1) * D)
            wide = (r + 1) * D
            scores = lax.dot_general(query[part, lanes], key[0:wide, lanes], NT,
                                     preferred_element_type=F32)
            gap = (cum[part, h:h + 1] - cum_t[h:h + 1, 0:wide]) + bias[part, 0:wide]
            weights = (scores * jnp.exp(gap)).astype(BF16)
            out[part, lanes] = jnp.dot(weights, value[0:wide, lanes], preferred_element_type=F32)


def carry_kernel(starts, lengths, query, intra, p0, p1, p2, p3, cum, out, squares, states):
    _, place, bound, end_prev, end_cur = marks(starts, lengths)
    x = place % ROW
    for step, ref in enumerate((p0, p1, p2, p3)):
        states[(x - step + ROW) % ROW] = ref[...]
    rows = iota((T, 1), 0)
    valid = rows < jnp.where(rows < bound, end_prev, end_cur)
    enters = (rows < jnp.where(place > 0, T, bound)) & valid
    enter = jnp.where(enters, jnp.exp(cum[...]), 0.0)
    live = jnp.where(valid, 1.0, 0.0)
    acc = jnp.zeros((T, D), F32)
    for h in range(H):
        lanes = slice(h * D, (h + 1) * D)
        state = states[h // PAIR, (h % PAIR) * D:(h % PAIR + 1) * D, :]
        carried = jnp.dot(query[:, lanes], state, preferred_element_type=F32)
        heads = intra[:, lanes] * live + enter[:, h:h + 1] * carried
        out[:, lanes] = heads
        acc += heads * heads
    squares[...] = lax.dot_general(jnp.ones((8, D), F32), acc, NT, precision=HI,
                                   preferred_element_type=F32)


def norm_kernel(heads, gate, gain, squares, others, out, *, features):
    pick = (iota((8, D), 0) == 0).astype(F32)
    sums = lax.dot_general(squares[...] + others[...], pick, TN, precision=HI,
                           preferred_element_type=F32)
    scale = lax.rsqrt(sums * (1.0 / features) + EPS)
    for h in range(heads.shape[1] // D):
        lanes = slice(h * D, (h + 1) * D)
        gated = jax.nn.sigmoid(gate[:, lanes].astype(F32))
        out[:, lanes] = (heads[:, lanes] * scale * gain[:, lanes] * gated).astype(BF16)


def soft_kernel(starts, lengths, query, own, f1, f2, f3, f4, f5, f6, f7, f8, out,
                keys, values, asks, top, acc):
    room, place, bound, end_prev, end_cur = marks(starts, lengths)
    tail = place == 0
    count = jnp.where(tail, jnp.where(room > 0, SPAN, 0), place)
    begin_room = jnp.where(tail, jnp.maximum(room - 1, 0), room)
    begin = starts[begin_room] - begin_room * SPAN * T
    factor = (D ** -0.5) * 1.4426950408889634
    ones = jnp.ones((T, D), BF16)
    for m, ref in enumerate((own, f1, f2, f3, f4, f5, f6, f7, f8)):
        @pl.when(m <= count)
        def _():
            keys[m] = ref[:, 0:D]
            values[m, :, 0:D] = ref[:, D:2 * D]
            values[m, :, D:2 * D] = ones

    for h in range(H):
        asks[h] = query[:, h * D:(h + 1) * D]

    def attend(m, size, hidden, fresh=False):
        k = keys[m]
        v = values[m]
        span = GROUP if size == T else 1
        many = span * size

        def ask(h):
            return lax.dot_general(asks[h:h + span, 0:size, :].reshape(many, D), k, NT,
                                   preferred_element_type=F32)

        heads = range(0, H, span)
        ahead = ask(0)
        for h in heads:
            x = ahead
            if h + span < H:
                ahead = ask(h + span)
            if hidden is not None:
                x = (x.reshape(span, size, T) + hidden[None]).reshape(many, T)
            parts = [x[:, j * D:(j + 1) * D] for j in range(T // D)]
            best = functools.reduce(jnp.maximum, parts)
            peak = jnp.broadcast_to(jnp.max(best, axis=1, keepdims=True), (many, D)) * factor
            if not fresh:
                old = top[h:h + span, 0:size, :].reshape(many, D)
                peak = jnp.maximum(old, peak)
                shrink = jnp.exp2(old - peak)
            top[h:h + span, 0:size, :] = peak.reshape(span, size, D)
            p = jnp.concatenate([jnp.exp2(y * factor - peak).astype(BF16) for y in parts], axis=1)
            mixed = jnp.dot(p, v, preferred_element_type=F32)
            if not fresh:
                kept = acc[h:h + span, 0:size, :].reshape(many, 2 * D)
                mixed = mixed + kept * jnp.concatenate([shrink, shrink], axis=1)
            acc[h:h + span, 0:size, :] = mixed.reshape(span, size, 2 * D)

    t = iota((T, T), 0)
    i = iota((T, T), 1)
    seen = (i <= t) & ((i >= bound) | (t < bound))
    attend(0, T, jnp.where(seen, 0.0, NEG), fresh=True)

    @pl.when(place > 0)
    def _():
        def middle(m, _):
            attend(m, T, None)
            return 0

        lax.fori_loop(1, count, middle, 0)
        attend(count, T, jnp.where(iota((1, T), 1) < begin, NEG, 0.0))

    half = T // 2

    @pl.when(tail & (count > 0))
    def _():
        def one(m, _):
            row_ok = iota((half, T), 0) < bound
            first_key = jnp.where(m == count, begin, 0)
            attend(m, half, jnp.where(row_ok & (iota((half, T), 1) >= first_key), 0.0, NEG))
            return 0

        lax.fori_loop(1, count + 1, one, 0)

    valid = valid_rows((T, 1), bound, end_prev, end_cur)
    for h in range(H):
        mixed = acc[h, :, 0:D] / acc[h, :, D:2 * D]
        out[:, h * D:(h + 1) * D] = jnp.where(valid, mixed, 0.0).astype(BF16)


smem = pl.BlockSpec(memory_space=pltpu.SMEM)
vmem = pl.BlockSpec(memory_space=pltpu.VMEM)


def shape(*dims, kind=F32):
    return jax.ShapeDtypeStruct(dims, kind)


def call(kernel, tables, operands, outs, scratch=()):
    return pl.pallas_call(
        kernel, in_specs=[smem] * tables + [vmem] * (len(operands) - tables),
        out_specs=[vmem] * len(outs), out_shape=list(outs), scratch_shapes=list(scratch),
    )(*operands)


def window(distance, rooms):
    pairs = []
    for room in range(rooms):
        base = room * SPAN
        for i in range(base, base + SPAN):
            j = i + distance
            if j <= base + SPAN and j < rooms * SPAN:
                pairs.append((i, j))
    return pairs


def per_device(lin_query, lin_key, lin_value, lin_gate, lin_decay, norm_gain,
               soft_query, soft_key, soft_value, starts, lengths):
    places = lax.axis_size("ctx")
    rooms = places // SPAN
    share = lax.axis_size("head")
    width = H * D
    piece = PAIR * D
    around = [[(i, i - i % ROW + (i + step) % ROW) for i in range(places)] for step in range(ROW)]
    onward = [(i, i + ROW) for i in range(places - ROW)]
    beyond = [(i, i + 2 * ROW) for i in range(places - 2 * ROW) if i // ROW % 2 == 0]

    def send(x, pairs):
        return lax.ppermute(x, "ctx", pairs)

    packed = shape(piece + EXTRA, D, kind=BF16)

    pair = shape(T, 2 * D, kind=BF16)
    *slices, cum, cum_t, kv = call(
        state_kernel, 2,
        (starts, lengths, lin_key, lin_value, lin_decay.T, soft_key, soft_value),
        [packed] * ROW + [shape(T, H), shape(H, T), pair],
        [pltpu.VMEM((ROW, piece, D), BF16), pltpu.VMEM((ROW, EXTRA, D), BF16)])
    row = [slices[0]] + [send(slices[j], around[j]) for j in range(1, ROW)]

    intra, = call(intra_kernel, 2,
                  (starts, lengths, lin_query, lin_key, lin_value, cum, cum_t),
                  [shape(T, width)], [pltpu.VMEM((T, T), F32)])

    table = [pltpu.VMEM((ROW, piece, D), F32), pltpu.VMEM((ROW, 8 * PAIR, D), F32)]
    row_total, = call(row_kernel, 0, row, [packed], table)
    above = send(row_total, onward)
    above2 = send(row_total, beyond)
    ready = call(
        prefix_kernel, 0, (*row, above, above2), [shape(piece, D, kind=BF16)] * ROW,
        table + [pltpu.VMEM((ROW, piece, D), BF16)])
    before = [ready[0]] + [send(ready[j], around[j]) for j in range(1, ROW)]

    far_kv = [send(kv, window(m, rooms)) for m in range(1, SPAN + 1)]

    heads, squares = call(
        carry_kernel, 2, (starts, lengths, lin_query, intra, *before, cum),
        [shape(T, width), shape(8, T)], [pltpu.VMEM((ROW, piece, D), BF16)])
    step = 1
    others = jnp.zeros_like(squares)
    while step < share:
        if step > 1:
            squares = squares + others
        others = lax.ppermute(squares, "head", [(i, i ^ step) for i in range(share)])
        step *= 2

    soft_out, = call(
        soft_kernel, 2, (starts, lengths, soft_query, kv, *far_kv),
        [shape(T, width, kind=BF16)],
        [pltpu.VMEM((SPAN + 1, T, D), BF16), pltpu.VMEM((SPAN + 1, T, 2 * D), BF16),
         pltpu.VMEM((H, T, D), BF16), pltpu.VMEM((H, T, D), F32),
         pltpu.VMEM((H, T, 2 * D), F32)])

    lin_out, = call(
        functools.partial(norm_kernel, features=width * share), 0,
        (heads, lin_gate, norm_gain.reshape(1, width), squares, others),
        [shape(T, width, kind=BF16)])
    return (lin_out, soft_out)


def solution(mesh):
    wide = P("ctx", "head")
    return jax.shard_map(
        per_device, mesh=mesh,
        in_specs=(wide, wide, wide, wide, wide, P("head"), wide, wide, wide, P(), P()),
        out_specs=(wide, wide), check_vma=False,
    )
```

profile of v0, /device:TPU:38, one launch (start us, length us, event | category | flops | bytes accessed | tf_op | source)
XLA Modules:
  0.0 107.6 jit_solution(4691704138265424727)
XLA Ops:
  0.6 3.9 %shard_map.122 = (bf16[272,128]{1,0:T(8,128)(2,1)}, bf16[272,128]{1,0:T(8,128)(2,1)}, bf16[272,128]{1,0:T(8,128)(2,1)}, bf16[272,128]{1,0:T(8,128)(2,1)}, f32[38...) custom-call(s32[4]{0:T(128)} %starts.7, s32[4]{0:T(128)} %lengths.7, bf16[384,1024]{1,0:T(8,128)(2,1)} %key.3, ...), custom_call_target="tpu_custom_call" | custom-call | tf_op jit(solution)/shard_map/pallas_call | solution.py:285
  4.6 0.5 collective-permute-start
  5.0 2.4 %collective-permute-start.1 = (bf16[272,128]{1,0:T(8,128)(2,1)}, bf16[272,128]{1,0:T(8,128)(2,1)S(1)}, u32[]{:S(2)}, u32[]{:S(2)}) collective-permute-start(bf16[272,128]{1,0:T(8,128)(2,1)} %get-tuple-element.19), channel_id=1, source_target_pairs={{0,16},{8,24},{16,0},{24,8},{32,48},{40,56},{48,32},{56,40},{64,80... | collective-permute-start | bytes 208904 | tf_op jit(solution)/shard_map/ppermute | solution.py:314
  7.5 2.0 %collective-permute-done.r1 = bf16[272,128]{1,0:T(8,128)(2,1)S(1)} collective-permute-done((bf16[272,128]{1,0:T(8,128)(2,1)}, bf16[272,128]{1,0:T(8,128)(2,1)S(1)}, u32[]{:S(2)}, u32[]{:S(2)}) %collective-permute-start) | collective-permute-done | bytes 69664 | tf_op jit(solution)/shard_map/ppermute | solution.py:314
  9.4 1.9 %collective-permute-done.1.r2 = bf16[272,128]{1,0:T(8,128)(2,1)S(1)} collective-permute-done((bf16[272,128]{1,0:T(8,128)(2,1)}, bf16[272,128]{1,0:T(8,128)(2,1)S(1)}, u32[]{:S(2)}, u32[]{:S(2)}) %collective-permute-start.1) | collective-permute-done | bytes 69664 | tf_op jit(solution)/shard_map/ppermute | solution.py:314
  11.3 1.8 %collective-permute-done.2.r3 = bf16[272,128]{1,0:T(8,128)(2,1)S(1)} collective-permute-done((bf16[272,128]{1,0:T(8,128)(2,1)}, bf16[272,128]{1,0:T(8,128)(2,1)S(1)}, u32[]{:S(2)}, u32[]{:S(2)}) %collective-permute-start.2) | collective-permute-done | bytes 69664 | tf_op jit(solution)/shard_map/ppermute | solution.py:314
  13.2 0.6 copy-done.2
  13.8 1.7 %shard_map.124 = bf16[272,128]{1,0:T(8,128)(2,1)} custom-call(bf16[272,128]{1,0:T(8,128)(2,1)} %get-tuple-element.17.own, bf16[272,128]{1,0:T(8,128)(2,1)} %copy-done, bf16[272,128]{1,0:T(8,128)(2,1)} %copy-done.1, bf16[272,128]{1,0:T(8,128)(2,1)} %copy-done.2), custom_call_target="tpu_custom_call" | custom-call | tf_op jit(solution)/shard_map/pallas_call | solution.py:285
  15.5 3.8 %collective-permute-start.3 = (bf16[272,128]{1,0:T(8,128)(2,1)}, bf16[272,128]{1,0:T(8,128)(2,1)S(1)}, u32[]{:S(2)}, u32[]{:S(2)}) collective-permute-start(bf16[272,128]{1,0:T(8,128)(2,1)} %shard_map.124), channel_id=1, source_target_pairs={{0,32},{8,40},{16,48},{24,56},{32,64},{40,72},{48,80},{56,88},{64,... | collective-permute-start | bytes 208904 | tf_op jit(solution)/shard_map/ppermute | solution.py:314
  19.4 0.7 collective-permute-start.4
  20.0 8.7 %collective-permute-start.11 = (bf16[384,256]{1,0:T(8,128)(2,1)}, bf16[384,256]{1,0:T(8,128)(2,1)S(1)}, u32[]{:S(2)}, u32[]{:S(2)}) collective-permute-start(bf16[384,256]{1,0:T(8,128)(2,1)} %get-tuple-element.27.own), channel_id=1, source_target_pairs={{0,8},{8,16},{16,24},{24,32},{32,40},{40,48},{48,56},{56,64},{64,7... | collective-permute-start | bytes 589832 | tf_op jit(solution)/shard_map/ppermute | solution.py:314
  28.7 1.3 %collective-permute-start.12 = (bf16[384,256]{1,0:T(8,128)(2,1)}, bf16[384,256]{1,0:T(8,128)(2,1)S(1)}, u32[]{:S(2)}, u32[]{:S(2)}) collective-permute-start(bf16[384,256]{1,0:T(8,128)(2,1)} %get-tuple-element.27.own), channel_id=1, source_target_pairs={{0,16},{8,24},{16,32},{24,40},{32,48},{40,56},{48,64},{64,80},{72,... | collective-permute-start | bytes 589832 | tf_op jit(solution)/shard_map/ppermute | solution.py:314
  30.0 1.3 %collective-permute-start.13 = (bf16[384,256]{1,0:T(8,128)(2,1)}, bf16[384,256]{1,0:T(8,128)(2,1)S(1)}, u32[]{:S(2)}, u32[]{:S(2)}) collective-permute-start(bf16[384,256]{1,0:T(8,128)(2,1)} %get-tuple-element.27.own), channel_id=1, source_target_pairs={{0,24},{8,32},{16,40},{24,48},{32,56},{40,64},{64,88},{72,96},{80,... | collective-permute-start | bytes 589832 | tf_op jit(solution)/shard_map/ppermute | solution.py:314
  31.3 0.0 collective-permute-done.3.z1
  31.3 0.0 collective-permute-done.4.z2
  31.3 0.6 copy-done.12
  32.0 0.6 copy-done.13
  32.6 1.9 %shard_map.125 = (bf16[256,128]{1,0:T(8,128)(2,1)}, bf16[256,128]{1,0:T(8,128)(2,1)}, bf16[256,128]{1,0:T(8,128)(2,1)}, bf16[256,128]{1,0:T(8,128)(2,1)}) custom-call(bf16[272,128]{1,0:T(8,128)(2,1)} %get-tuple-element.17.own, bf16[272,128]{1,0:T(8,128)(2,1)} %copy-done, bf16[272,128]{1,0:T(8,128)(2,1)} %copy-done.1, bf16[272,128]{1,0:T(8,128)(2,1)} %copy-done.2, ...), custom_call_target="tpu_custom_call" | custom-call | tf_op jit(solution)/shard_map/pallas_call | solution.py:285
  34.5 3.9 %collective-permute-start.5 = (bf16[256,128]{1,0:T(8,128)(2,1)}, bf16[256,128]{1,0:T(8,128)(2,1)S(1)}, u32[]{:S(2)}, u32[]{:S(2)}) collective-permute-start(bf16[256,128]{1,0:T(8,128)(2,1)} %get-tuple-element.22), channel_id=1, source_target_pairs={{0,8},{8,16},{16,24},{24,0},{32,40},{40,48},{48,56},{56,32},{64,72... | collective-permute-start | bytes 196616 | tf_op jit(solution)/shard_map/ppermute | solution.py:314
  38.3 3.0 %collective-permute-start.6 = (bf16[256,128]{1,0:T(8,128)(2,1)}, bf16[256,128]{1,0:T(8,128)(2,1)S(1)}, u32[]{:S(2)}, u32[]{:S(2)}) collective-permute-start(bf16[256,128]{1,0:T(8,128)(2,1)} %get-tuple-element.23), channel_id=1, source_target_pairs={{0,16},{8,24},{16,0},{24,8},{32,48},{40,56},{48,32},{56,40},{64,80... | collective-permute-start | bytes 196616 | tf_op jit(solution)/shard_map/ppermute | solution.py:314
  41.3 0.0 collective-permute-done.5.p1
  41.4 2.3 %collective-permute-start.7 = (bf16[256,128]{1,0:T(8,128)(2,1)}, bf16[256,128]{1,0:T(8,128)(2,1)S(1)}, u32[]{:S(2)}, u32[]{:S(2)}) collective-permute-start(bf16[256,128]{1,0:T(8,128)(2,1)} %get-tuple-element.24), channel_id=1, source_target_pairs={{0,24},{8,0},{16,8},{24,16},{32,56},{40,32},{48,40},{56,48},{64,88... | collective-permute-start | bytes 196616 | tf_op jit(solution)/shard_map/ppermute | solution.py:314
  43.7 6.7 %shard_map.123.intra = f32[384,1024]{1,0:T(8,128)} custom-call(s32[4]{0:T(128)} %starts.7, s32[4]{0:T(128)} %lengths.7, bf16[384,1024]{1,0:T(8,128)(2,1)} %query.4, bf16[384,1024]{1,0:T(8,128)(2,1)} %key.3, bf16[384,1024]{1,0:T(8,128)(2,1)} %value.3, f32[384,8]{1,0:T(8,128)} %get-tuple-element.15.cum, f32[8,384]{1,0:T(8,128)} %get-tuple-element.16.cum_t), custom_call_target="tpu_custom_call" | custom-call | tf_op jit(solution)/shard_map/pallas_call | solution.py:285
  50.4 0.0 collective-permute-done.7.p3
  50.5 0.6 copy-done.15
  51.0 0.0 copy-done.16
  51.1 3.6 %shard_map.126 = (f32[384,1024]{1,0:T(8,128)}, f32[8,384]{1,0:T(8,128)}) custom-call(s32[4]{0:T(128)} %starts.7, s32[4]{0:T(128)} %lengths.7, bf16[384,1024]{1,0:T(8,128)(2,1)} %query.4, f32[384,1024]{1,0:T(8,128)} %shard_map.123.intra, bf16[256,128]{1,0:T(8,128)(2,1)} %get-tuple-element.21.p0, bf16[256,128]{1,0:T(8,128)(2,1)} %copy-done.14, ...), custom_call_target="tpu_custom_call" | custom-call | tf_op jit(solution)/shard_map/pallas_call | solution.py:285
  54.7 1.4 %collective-permute-done.8 = f32[8,384]{1,0:T(8,128)S(1)} collective-permute-done((f32[8,384]{1,0:T(8,128)}, f32[8,384]{1,0:T(8,128)S(1)}, u32[]{:S(2)}, u32[]{:S(2)}) %collective-permute-start.8) | collective-permute-done | bytes 12320 | tf_op jit(solution)/shard_map/ppermute | solution.py:349
  56.1 0.7 add.6
  56.8 1.6 %collective-permute-start.9 = (f32[8,384]{1,0:T(8,128)S(1)}, f32[8,384]{1,0:T(8,128)S(1)}, u32[]{:S(2)}, u32[]{:S(2)}) collective-permute-start(f32[8,384]{1,0:T(8,128)S(1)} %add.6), channel_id=1, source_target_pairs={{0,2},{1,3},{2,0},{3,1},{4,6},{5,7},{6,4},{7,5},{8,10},{9,11},{10,... | collective-permute-start | bytes 36872 | tf_op jit(solution)/shard_map/ppermute | solution.py:349
  58.4 1.3 %collective-permute-start.14 = (bf16[384,256]{1,0:T(8,128)(2,1)S(1)}, bf16[384,256]{1,0:T(8,128)(2,1)S(1)}, u32[]{:S(2)}, u32[]{:S(2)}) collective-permute-start(bf16[384,256]{1,0:T(8,128)(2,1)S(1)} %copy-done.3), channel_id=1, source_target_pairs={{0,32},{8,40},{16,48},{24,56},{32,64},{64,96},{72,104},{80,112},{8... | collective-permute-start | bytes 589832 | tf_op jit(solution)/shard_map/ppermute | solution.py:314
  59.7 0.0 collective-permute-done.11.f1
  59.7 1.3 %collective-permute-start.15 = (bf16[384,256]{1,0:T(8,128)(2,1)S(1)}, bf16[384,256]{1,0:T(8,128)(2,1)S(1)}, u32[]{:S(2)}, u32[]{:S(2)}) collective-permute-start(bf16[384,256]{1,0:T(8,128)(2,1)S(1)} %copy-done.3), channel_id=1, source_target_pairs={{0,40},{8,48},{16,56},{24,64},{64,104},{72,112},{80,120},{88,128},... | collective-permute-start | bytes 589832 | tf_op jit(solution)/shard_map/ppermute | solution.py:314
  61.0 0.0 collective-permute-done.12.f2
  61.0 1.3 %collective-permute-start.16 = (bf16[384,256]{1,0:T(8,128)(2,1)S(1)}, bf16[384,256]{1,0:T(8,128)(2,1)S(1)}, u32[]{:S(2)}, u32[]{:S(2)}) collective-permute-start(bf16[384,256]{1,0:T(8,128)(2,1)S(1)} %copy-done.3), channel_id=1, source_target_pairs={{0,48},{8,56},{16,64},{64,112},{72,120},{80,128},{128,176},{136,18... | collective-permute-start | bytes 589832 | tf_op jit(solution)/shard_map/ppermute | solution.py:314
  62.3 1.3 %collective-permute-start.17 = (bf16[384,256]{1,0:T(8,128)(2,1)S(1)}, bf16[384,256]{1,0:T(8,128)(2,1)S(1)}, u32[]{:S(2)}, u32[]{:S(2)}) collective-permute-start(bf16[384,256]{1,0:T(8,128)(2,1)S(1)} %copy-done.3), channel_id=1, source_target_pairs={{0,56},{8,64},{64,120},{72,128},{128,184},{136,192},{192,248},{1,5... | collective-permute-start | bytes 589832 | tf_op jit(solution)/shard_map/ppermute | solution.py:314
  63.6 0.0 collective-permute-done.9
  63.6 0.7 collective-permute-start.18
  64.3 2.9 %collective-permute-done.14.f4 = bf16[384,256]{1,0:T(8,128)(2,1)S(1)} collective-permute-done((bf16[384,256]{1,0:T(8,128)(2,1)S(1)}, bf16[384,256]{1,0:T(8,128)(2,1)S(1)}, u32[]{:S(2)}, u32[]{:S(2)}) %collective-permute-start.14) | collective-permute-done | bytes 196640 | tf_op jit(solution)/shard_map/ppermute | solution.py:314
  67.2 2.9 %collective-permute-start.10 = (f32[8,384]{1,0:T(8,128)S(1)}, f32[8,384]{1,0:T(8,128)S(1)}, u32[]{:S(2)}, u32[]{:S(2)}) collective-permute-start(f32[8,384]{1,0:T(8,128)S(1)} %add.7.squares), channel_id=1, source_target_pairs={{0,4},{1,5},{2,6},{3,7},{4,0},{5,1},{6,2},{7,3},{8,12},{9,13},{10,... | collective-permute-start | bytes 36872 | tf_op jit(solution)/shard_map/ppermute | solution.py:349
  70.1 3.6 %collective-permute-done.15.f5 = bf16[384,256]{1,0:T(8,128)(2,1)S(1)} collective-permute-done((bf16[384,256]{1,0:T(8,128)(2,1)S(1)}, bf16[384,256]{1,0:T(8,128)(2,1)S(1)}, u32[]{:S(2)}, u32[]{:S(2)}) %collective-permute-start.15) | collective-permute-done | bytes 196640 | tf_op jit(solution)/shard_map/ppermute | solution.py:314
  73.7 5.1 %collective-permute-done.16.f6 = bf16[384,256]{1,0:T(8,128)(2,1)S(1)} collective-permute-done((bf16[384,256]{1,0:T(8,128)(2,1)S(1)}, bf16[384,256]{1,0:T(8,128)(2,1)S(1)}, u32[]{:S(2)}, u32[]{:S(2)}) %collective-permute-start.16) | collective-permute-done | bytes 196640 | tf_op jit(solution)/shard_map/ppermute | solution.py:314
  78.8 3.4 %collective-permute-done.17.f7 = bf16[384,256]{1,0:T(8,128)(2,1)S(1)} collective-permute-done((bf16[384,256]{1,0:T(8,128)(2,1)S(1)}, bf16[384,256]{1,0:T(8,128)(2,1)S(1)}, u32[]{:S(2)}, u32[]{:S(2)}) %collective-permute-start.17) | collective-permute-done | bytes 196640 | tf_op jit(solution)/shard_map/ppermute | solution.py:314
  82.2 0.6 copy-done.10
  82.9 0.7 copy-done.11
  83.5 20.2 %shard_map.128 = bf16[384,1024]{1,0:T(8,128)(2,1)} custom-call(s32[4]{0:T(128)} %starts.7, s32[4]{0:T(128)} %lengths.7, bf16[384,1024]{1,0:T(8,128)(2,1)} %query.5, bf16[384,256]{1,0:T(8,128)(2,1)} %get-tuple-element.27.own, bf16[384,256]{1,0:T(8,128)(2,1)} %copy-done.4, bf16[384,256]{1,0:T(8,128)(2,1)} %copy-done.5, bf16[384,256]{1,0:T(8,128)(2,1)} %copy-done.6, ...), custom_call_target="tpu_custom_call" | custom-call | tf_op jit(solution)/shard_map/pallas_call | solution.py:285
  103.7 0.6 copy-done.18
  104.3 3.3 %shard_map.127 = bf16[384,1024]{1,0:T(8,128)(2,1)} custom-call(f32[384,1024]{1,0:T(8,128)} %get-tuple-element.25.heads, bf16[384,1024]{1,0:T(8,128)(2,1)} %gate.1, f32[1,1024]{1,0:T(1,128)} %bitcast.3, f32[8,384]{1,0:T(8,128)} %copy-done.17, f32[8,384]{1,0:T(8,128)} %copy-done.18), custom_call_target="tpu_custom_call" | custom-call | tf_op jit(solution)/shard_map/pallas_call | solution.py:285
  (37 shorter events, 0.1 us)
Async XLA Ops:
  4.6 4.9 %collective-permute-start = (bf16[272,128]{1,0:T(8,128)(2,1)}, bf16[272,128]{1,0:T(8,128)(2,1)S(1)}, u32[]{:S(2)}, u32[]{:S(2)}) collective-permute-start(bf16[272,128]{1,0:T(8,128)(2,1)} %get-tuple-element.18), channel_id=1, source_target_pairs={{0,8},{8,16},{16,24},{24,0},{32,40},{40,48},{48,56},{56,32},{64,72... | collective-permute-start | bytes 208904 | tf_op jit(solution)/shard_map/ppermute | solution.py:314
  5.0 6.3 %collective-permute-start.1 = (bf16[272,128]{1,0:T(8,128)(2,1)}, bf16[272,128]{1,0:T(8,128)(2,1)S(1)}, u32[]{:S(2)}, u32[]{:S(2)}) collective-permute-start(bf16[272,128]{1,0:T(8,128)(2,1)} %get-tuple-element.19), channel_id=1, source_target_pairs={{0,16},{8,24},{16,0},{24,8},{32,48},{40,56},{48,32},{56,40},{64,80... | collective-permute-start | bytes 208904 | tf_op jit(solution)/shard_map/ppermute | solution.py:314
  7.5 5.7 %collective-permute-start.2 = (bf16[272,128]{1,0:T(8,128)(2,1)}, bf16[272,128]{1,0:T(8,128)(2,1)S(1)}, u32[]{:S(2)}, u32[]{:S(2)}) collective-permute-start(bf16[272,128]{1,0:T(8,128)(2,1)} %get-tuple-element.20), channel_id=1, source_target_pairs={{0,24},{8,0},{16,8},{24,16},{32,56},{40,32},{48,40},{56,48},{64,88... | collective-permute-start | bytes 208904 | tf_op jit(solution)/shard_map/ppermute | solution.py:314
  9.4 3.8 %copy-start = (bf16[272,128]{1,0:T(8,128)(2,1)}, bf16[272,128]{1,0:T(8,128)(2,1)S(1)}, u32[]{:S(2)}) copy-start(bf16[272,128]{1,0:T(8,128)(2,1)S(1)} %collective-permute-done.r1) | copy-start | bytes 208900
  11.3 1.9 %copy-start.1 = (bf16[272,128]{1,0:T(8,128)(2,1)}, bf16[272,128]{1,0:T(8,128)(2,1)S(1)}, u32[]{:S(2)}) copy-start(bf16[272,128]{1,0:T(8,128)(2,1)S(1)} %collective-permute-done.1.r2) | copy-start | bytes 208900
  13.2 0.6 copy-start.2
  15.5 15.8 %collective-permute-start.3 = (bf16[272,128]{1,0:T(8,128)(2,1)}, bf16[272,128]{1,0:T(8,128)(2,1)S(1)}, u32[]{:S(2)}, u32[]{:S(2)}) collective-permute-start(bf16[272,128]{1,0:T(8,128)(2,1)} %shard_map.124), channel_id=1, source_target_pairs={{0,32},{8,40},{16,48},{24,56},{32,64},{40,72},{48,80},{56,88},{64,... | collective-permute-start | bytes 208904 | tf_op jit(solution)/shard_map/ppermute | solution.py:314
  19.4 12.0 %collective-permute-start.4 = (bf16[272,128]{1,0:T(8,128)(2,1)}, bf16[272,128]{1,0:T(8,128)(2,1)S(1)}, u32[]{:S(2)}, u32[]{:S(2)}) collective-permute-start(bf16[272,128]{1,0:T(8,128)(2,1)} %shard_map.124), channel_id=1, source_target_pairs={{0,64},{8,72},{16,80},{24,88},{64,128},{72,136},{80,144},{88,152},... | collective-permute-start | bytes 208904 | tf_op jit(solution)/shard_map/ppermute | solution.py:314
  20.0 39.6 %collective-permute-start.11 = (bf16[384,256]{1,0:T(8,128)(2,1)}, bf16[384,256]{1,0:T(8,128)(2,1)S(1)}, u32[]{:S(2)}, u32[]{:S(2)}) collective-permute-start(bf16[384,256]{1,0:T(8,128)(2,1)} %get-tuple-element.27.own), channel_id=1, source_target_pairs={{0,8},{8,16},{16,24},{24,32},{32,40},{40,48},{48,56},{56,64},{64,7... | collective-permute-start | bytes 589832 | tf_op jit(solution)/shard_map/ppermute | solution.py:314
  28.7 32.3 %collective-permute-start.12 = (bf16[384,256]{1,0:T(8,128)(2,1)}, bf16[384,256]{1,0:T(8,128)(2,1)S(1)}, u32[]{:S(2)}, u32[]{:S(2)}) collective-permute-start(bf16[384,256]{1,0:T(8,128)(2,1)} %get-tuple-element.27.own), channel_id=1, source_target_pairs={{0,16},{8,24},{16,32},{24,40},{32,48},{40,56},{48,64},{64,80},{72,... | collective-permute-start | bytes 589832 | tf_op jit(solution)/shard_map/ppermute | solution.py:314
  30.0 32.3 %collective-permute-start.13 = (bf16[384,256]{1,0:T(8,128)(2,1)}, bf16[384,256]{1,0:T(8,128)(2,1)S(1)}, u32[]{:S(2)}, u32[]{:S(2)}) collective-permute-start(bf16[384,256]{1,0:T(8,128)(2,1)} %get-tuple-element.27.own), channel_id=1, source_target_pairs={{0,24},{8,32},{16,40},{24,48},{32,56},{40,64},{64,88},{72,96},{80,... | collective-permute-start | bytes 589832 | tf_op jit(solution)/shard_map/ppermute | solution.py:314
  31.3 0.6 copy-start.12
  32.0 0.6 copy-start.13
  34.5 6.9 %collective-permute-start.5 = (bf16[256,128]{1,0:T(8,128)(2,1)}, bf16[256,128]{1,0:T(8,128)(2,1)S(1)}, u32[]{:S(2)}, u32[]{:S(2)}) collective-permute-start(bf16[256,128]{1,0:T(8,128)(2,1)} %get-tuple-element.22), channel_id=1, source_target_pairs={{0,8},{8,16},{16,24},{24,0},{32,40},{40,48},{48,56},{56,32},{64,72... | collective-permute-start | bytes 196616 | tf_op jit(solution)/shard_map/ppermute | solution.py:314
  38.3 12.1 %collective-permute-start.6 = (bf16[256,128]{1,0:T(8,128)(2,1)}, bf16[256,128]{1,0:T(8,128)(2,1)S(1)}, u32[]{:S(2)}, u32[]{:S(2)}) collective-permute-start(bf16[256,128]{1,0:T(8,128)(2,1)} %get-tuple-element.23), channel_id=1, source_target_pairs={{0,16},{8,24},{16,0},{24,8},{32,48},{40,56},{48,32},{56,40},{64,80... | collective-permute-start | bytes 196616 | tf_op jit(solution)/shard_map/ppermute | solution.py:314
  41.4 9.1 %copy-start.14 = (bf16[256,128]{1,0:T(8,128)(2,1)}, bf16[256,128]{1,0:T(8,128)(2,1)S(1)}, u32[]{:S(2)}) copy-start(bf16[256,128]{1,0:T(8,128)(2,1)S(1)} %collective-permute-done.5.p1) | copy-start | bytes 196612
  41.4 9.1 %collective-permute-start.7 = (bf16[256,128]{1,0:T(8,128)(2,1)}, bf16[256,128]{1,0:T(8,128)(2,1)S(1)}, u32[]{:S(2)}, u32[]{:S(2)}) collective-permute-start(bf16[256,128]{1,0:T(8,128)(2,1)} %get-tuple-element.24), channel_id=1, source_target_pairs={{0,24},{8,0},{16,8},{24,16},{32,56},{40,32},{48,40},{56,48},{64,88... | collective-permute-start | bytes 196616 | tf_op jit(solution)/shard_map/ppermute | solution.py:314
  50.4 8.0 %copy-start.3 = (bf16[384,256]{1,0:T(8,128)(2,1)S(1)}, bf16[384,256]{1,0:T(8,128)(2,1)}, u32[]{:S(2)}) copy-start(bf16[384,256]{1,0:T(8,128)(2,1)} %get-tuple-element.27.own) | copy-start | bytes 589828
  50.4 0.6 copy-start.15
  50.4 0.6 copy-start.16
  54.7 1.4 %collective-permute-start.8 = (f32[8,384]{1,0:T(8,128)}, f32[8,384]{1,0:T(8,128)S(1)}, u32[]{:S(2)}, u32[]{:S(2)}) collective-permute-start(f32[8,384]{1,0:T(8,128)} %get-tuple-element.26), channel_id=1, source_target_pairs={{0,1},{1,0},{2,3},{3,2},{4,5},{5,4},{6,7},{7,6},{8,9},{9,8},{10,11... | collective-permute-start | bytes 36872 | tf_op jit(solution)/shard_map/ppermute | solution.py:349
  56.8 6.8 %collective-permute-start.9 = (f32[8,384]{1,0:T(8,128)S(1)}, f32[8,384]{1,0:T(8,128)S(1)}, u32[]{:S(2)}, u32[]{:S(2)}) collective-permute-start(f32[8,384]{1,0:T(8,128)S(1)} %add.6), channel_id=1, source_target_pairs={{0,2},{1,3},{2,0},{3,1},{4,6},{5,7},{6,4},{7,5},{8,10},{9,11},{10,... | collective-permute-start | bytes 36872 | tf_op jit(solution)/shard_map/ppermute | solution.py:349
  58.4 8.8 %collective-permute-start.14 = (bf16[384,256]{1,0:T(8,128)(2,1)S(1)}, bf16[384,256]{1,0:T(8,128)(2,1)S(1)}, u32[]{:S(2)}, u32[]{:S(2)}) collective-permute-start(bf16[384,256]{1,0:T(8,128)(2,1)S(1)} %copy-done.3), channel_id=1, source_target_pairs={{0,32},{8,40},{16,48},{24,56},{32,64},{64,96},{72,104},{80,112},{8... | collective-permute-start | bytes 589832 | tf_op jit(solution)/shard_map/ppermute | solution.py:314
  59.7 22.5 %copy-start.4 = (bf16[384,256]{1,0:T(8,128)(2,1)}, bf16[384,256]{1,0:T(8,128)(2,1)S(1)}, u32[]{:S(2)}) copy-start(bf16[384,256]{1,0:T(8,128)(2,1)S(1)} %collective-permute-done.11.f1) | copy-start | bytes 589828
  59.7 14.0 %collective-permute-start.15 = (bf16[384,256]{1,0:T(8,128)(2,1)S(1)}, bf16[384,256]{1,0:T(8,128)(2,1)S(1)}, u32[]{:S(2)}, u32[]{:S(2)}) collective-permute-start(bf16[384,256]{1,0:T(8,128)(2,1)S(1)} %copy-done.3), channel_id=1, source_target_pairs={{0,40},{8,48},{16,56},{24,64},{64,104},{72,112},{80,120},{88,128},... | collective-permute-start | bytes 589832 | tf_op jit(solution)/shard_map/ppermute | solution.py:314
  61.0 21.2 %copy-start.5 = (bf16[384,256]{1,0:T(8,128)(2,1)}, bf16[384,256]{1,0:T(8,128)(2,1)S(1)}, u32[]{:S(2)}) copy-start(bf16[384,256]{1,0:T(8,128)(2,1)S(1)} %collective-permute-done.12.f2) | copy-start | bytes 589828
  61.0 17.8 %collective-permute-start.16 = (bf16[384,256]{1,0:T(8,128)(2,1)S(1)}, bf16[384,256]{1,0:T(8,128)(2,1)S(1)}, u32[]{:S(2)}, u32[]{:S(2)}) collective-permute-start(bf16[384,256]{1,0:T(8,128)(2,1)S(1)} %copy-done.3), channel_id=1, source_target_pairs={{0,48},{8,56},{16,64},{64,112},{72,120},{80,128},{128,176},{136,18... | collective-permute-start | bytes 589832 | tf_op jit(solution)/shard_map/ppermute | solution.py:314
  62.3 19.9 %copy-start.6 = (bf16[384,256]{1,0:T(8,128)(2,1)}, bf16[384,256]{1,0:T(8,128)(2,1)S(1)}, u32[]{:S(2)}) copy-start(bf16[384,256]{1,0:T(8,128)(2,1)S(1)} %collective-permute-done.13.f3) | copy-start | bytes 589828
  62.3 19.8 %collective-permute-start.17 = (bf16[384,256]{1,0:T(8,128)(2,1)S(1)}, bf16[384,256]{1,0:T(8,128)(2,1)S(1)}, u32[]{:S(2)}, u32[]{:S(2)}) collective-permute-start(bf16[384,256]{1,0:T(8,128)(2,1)S(1)} %copy-done.3), channel_id=1, source_target_pairs={{0,56},{8,64},{64,120},{72,128},{128,184},{136,192},{192,248},{1,5... | collective-permute-start | bytes 589832 | tf_op jit(solution)/shard_map/ppermute | solution.py:314
  63.6 18.5 %collective-permute-start.18 = (bf16[384,256]{1,0:T(8,128)(2,1)S(1)}, bf16[384,256]{1,0:T(8,128)(2,1)S(1)}, u32[]{:S(2)}, u32[]{:S(2)}) collective-permute-start(bf16[384,256]{1,0:T(8,128)(2,1)S(1)} %copy-done.3), channel_id=1, source_target_pairs={{0,64},{64,128},{128,192},{1,65},{65,129},{129,193},{2,66},{66,130... | collective-permute-start | bytes 589832 | tf_op jit(solution)/shard_map/ppermute | solution.py:314
  64.3 39.4 %copy-start.17 = (f32[8,384]{1,0:T(8,128)}, f32[8,384]{1,0:T(8,128)S(1)}, u32[]{:S(2)}) copy-start(f32[8,384]{1,0:T(8,128)S(1)} %add.7.squares) | copy-start | bytes 36868
  67.2 15.0 %copy-start.7 = (bf16[384,256]{1,0:T(8,128)(2,1)}, bf16[384,256]{1,0:T(8,128)(2,1)S(1)}, u32[]{:S(2)}) copy-start(bf16[384,256]{1,0:T(8,128)(2,1)S(1)} %collective-permute-done.14.f4) | copy-start | bytes 589828
  67.2 36.5 %collective-permute-start.10 = (f32[8,384]{1,0:T(8,128)S(1)}, f32[8,384]{1,0:T(8,128)S(1)}, u32[]{:S(2)}, u32[]{:S(2)}) collective-permute-start(f32[8,384]{1,0:T(8,128)S(1)} %add.7.squares), channel_id=1, source_target_pairs={{0,4},{1,5},{2,6},{3,7},{4,0},{5,1},{6,2},{7,3},{8,12},{9,13},{10,... | collective-permute-start | bytes 36872 | tf_op jit(solution)/shard_map/ppermute | solution.py:349
  73.7 8.5 %copy-start.8 = (bf16[384,256]{1,0:T(8,128)(2,1)}, bf16[384,256]{1,0:T(8,128)(2,1)S(1)}, u32[]{:S(2)}) copy-start(bf16[384,256]{1,0:T(8,128)(2,1)S(1)} %collective-permute-done.15.f5) | copy-start | bytes 589828
  78.8 3.4 %copy-start.9 = (bf16[384,256]{1,0:T(8,128)(2,1)}, bf16[384,256]{1,0:T(8,128)(2,1)S(1)}, u32[]{:S(2)}) copy-start(bf16[384,256]{1,0:T(8,128)(2,1)S(1)} %collective-permute-done.16.f6) | copy-start | bytes 589828
  82.2 0.7 copy-start.10
  82.9 0.7 copy-start.11
  103.7 0.6 copy-start.18
where the time goes:
time: 108 us
  Pallas kernels  41.3 us (38%)
  starting transfers between devices  38.2 us (35%)
  waiting for transfers between devices  22 us (20%)
  local copies, waits for them, and re-layouts  4.41 us (4%)
    pallas_call x7, Pallas kernels, call(): pl.pallas_call(kernel, in_specs=[smem] * tables + [vmem] * (len(operands)...  41.3 us
    ppermute x16, starting transfers between devices, send(): return lax.ppermute(x, 'ctx', pairs)  33.7 us
    ppermute x16, waiting for transfers between devices, send(): return lax.ppermute(x, 'ctx', pairs)  20.7 us
    ppermute x3, starting transfers between devices, per_device(): lax.ppermute(squares, 'head', [(i, i ^ step) for i in range(share)])  4.48 us
    unnamed x38, local copies, waits for them, and re-layouts  4.41 us
  transfers between devices with their start and end apart: 19, of which 8 were waited for; matrix products, arithmetic and copies ran while one was open for 1% of the time, Pallas kernels for 30%

commit v1 on v0

--- a/solution.py
+++ b/solution.py
@@ -12,6 +12,7 @@
 H = 8
 SPAN = 8
 NEG = -1e30
+PART = 4
 GROUP = 2
 EPS = 1e-06
 GONE = -1e5
@@ -189,8 +190,10 @@
         out[:, lanes] = (heads[:, lanes] * scale * gain[:, lanes] * gated).astype(BF16)
 
 
-def soft_kernel(starts, lengths, query, own, f1, f2, f3, f4, f5, f6, f7, f8, out,
-                keys, values, asks, top, acc):
+def soft_kernel(starts, lengths, query, own, f1, f2, f3, f4, f5, f6, f7, f8, *rest, first):
+    *done, out, keys, values, asks, top, acc = rest
+    for ref in done:
+        out[:, 0:first * D] = ref[...]
     room, place, bound, end_prev, end_cur = marks(starts, lengths)
     tail = place == 0
     count = jnp.where(tail, jnp.where(room > 0, SPAN, 0), place)
@@ -205,8 +208,8 @@
             values[m, :, 0:D] = ref[:, D:2 * D]
             values[m, :, D:2 * D] = ones
 
-    for h in range(H):
-        asks[h] = query[:, h * D:(h + 1) * D]
+    for h in range(PART):
+        asks[h] = query[:, (first + h) * D:(first + h + 1) * D]
 
     def attend(m, size, hidden, fresh=False):
         k = keys[m]
@@ -218,11 +221,11 @@
             return lax.dot_general(asks[h:h + span, 0:size, :].reshape(many, D), k, NT,
                                    preferred_element_type=F32)
 
-        heads = range(0, H, span)
+        heads = range(0, PART, span)
         ahead = ask(0)
         for h in heads:
             x = ahead
-            if h + span < H:
+            if h + span < PART:
                 ahead = ask(h + span)
             if hidden is not None:
                 x = (x.reshape(span, size, T) + hidden[None]).reshape(many, T)
@@ -268,9 +271,9 @@
         lax.fori_loop(1, count + 1, one, 0)
 
     valid = valid_rows((T, 1), bound, end_prev, end_cur)
-    for h in range(H):
+    for h in range(PART):
         mixed = acc[h, :, 0:D] / acc[h, :, D:2 * D]
-        out[:, h * D:(h + 1) * D] = jnp.where(valid, mixed, 0.0).astype(BF16)
+        out[:, (first + h) * D:(first + h + 1) * D] = jnp.where(valid, mixed, 0.0).astype(BF16)
 
 
 smem = pl.BlockSpec(memory_space=pltpu.SMEM)
@@ -281,10 +284,12 @@
     return jax.ShapeDtypeStruct(dims, kind)
 
 
-def call(kernel, tables, operands, outs, scratch=()):
+def call(kernel, tables, operands, outs, scratch=(), room=12):
     return pl.pallas_call(
         kernel, in_specs=[smem] * tables + [vmem] * (len(operands) - tables),
         out_specs=[vmem] * len(outs), out_shape=list(outs), scratch_shapes=list(scratch),
+        compiler_params=pltpu.CompilerParams(
+            vmem_limit_bytes=room << 20),
     )(*operands)
 
 
@@ -349,12 +354,16 @@
         others = lax.ppermute(squares, "head", [(i, i ^ step) for i in range(share)])
         step *= 2
 
-    soft_out, = call(
-        soft_kernel, 2, (starts, lengths, soft_query, kv, *far_kv),
-        [shape(T, width, kind=BF16)],
-        [pltpu.VMEM((SPAN + 1, T, D), BF16), pltpu.VMEM((SPAN + 1, T, 2 * D), BF16),
-         pltpu.VMEM((H, T, D), BF16), pltpu.VMEM((H, T, D), F32),
-         pltpu.VMEM((H, T, 2 * D), F32)])
+    done = []
+    for first in range(0, H, PART):
+        done = call(
+            functools.partial(soft_kernel, first=first), 2,
+            (starts, lengths, soft_query, kv, *far_kv, *done),
+            [shape(T, (first + PART) * D, kind=BF16)],
+            [pltpu.VMEM((SPAN + 1, T, D), BF16), pltpu.VMEM((SPAN + 1, T, 2 * D), BF16),
+             pltpu.VMEM((PART, T, D), BF16), pltpu.VMEM((PART, T, D), F32),
+             pltpu.VMEM((PART, T, 2 * D), F32)], room=20)
+    soft_out, = done
 
     lin_out, = call(
         functools.partial(norm_kernel, features=width * share), 0,

time: 108 us -> 101 us (0.935)
  Pallas kernels: 41.3 us -> 33.4 us
  local copies, waits for them, and re-layouts: 4.41 us -> 6.11 us
    pallas_call x7 -> x8, Pallas kernels: 41.3 us -> 33.4 us  [call(): pl.pallas_call(kernel, in_specs=[smem] * tables + [vmem] * (len(operands)...]
    unnamed x38 -> x28, local copies, waits for them, and re-layouts: 4.41 us -> 6.11 us
  transfers between devices with their start and end apart: 19 -> 19, of which waited for: 8 -> 8; matrix products, arithmetic and copies ran while one was open for 1% -> 0% of each run, Pallas kernels for 30% -> 29%
where the time goes in v1:
time: 101 us; the launch traced here: 100 us
  starting transfers between devices  38.1 us (38%)
  Pallas kernels  33.4 us (33%)
  waiting for transfers between devices  21.7 us (21%)
  local copies, waits for them, and re-layouts  6.11 us (6%)
    ppermute x16, starting transfers between devices, send(): return lax.ppermute(x, 'ctx', pairs)  33.6 us
    pallas_call x8, Pallas kernels, call(): pl.pallas_call(kernel, in_specs=[smem] * tables + [vmem] * (len(operands)...  33.4 us
    ppermute x16, waiting for transfers between devices, send(): return lax.ppermute(x, 'ctx', pairs)  20.5 us
    unnamed x28, local copies, waits for them, and re-layouts  6.11 us
    ppermute x3, starting transfers between devices, per_device(): lax.ppermute(squares, 'head', [(i, i ^ step) for i in range(share)])  4.48 us
  transfers between devices with their start and end apart: 19, of which 8 were waited for; matrix products, arithmetic and copies ran while one was open for 0% of the time, Pallas kernels for 29%

profile of v1, /device:TPU:38, one launch (start us, length us, event | category | flops | bytes accessed | tf_op | source)
XLA Modules:
  0.0 100.2 jit_solution(8034038660404643283)
XLA Ops:
  0.7 1.1 %copy-done.1 = bf16[384,1024]{1,0:T(8,128)(2,1)S(1)} copy-done((bf16[384,1024]{1,0:T(8,128)(2,1)S(1)}, bf16[384,1024]{1,0:T(8,128)(2,1)}, u32[]{:S(2)}) %copy-start.1) | copy-done | bytes 786456
  1.8 1.1 %copy-done.3 = bf16[384,1024]{1,0:T(8,128)(2,1)S(1)} copy-done((bf16[384,1024]{1,0:T(8,128)(2,1)S(1)}, bf16[384,1024]{1,0:T(8,128)(2,1)}, u32[]{:S(2)}) %copy-start.3) | copy-done | bytes 786456
  2.9 0.9 copy-done.6
  3.8 0.9 copy-done.7
  4.7 0.7 copy-done.8
  5.4 0.7 copy-done.10
  6.0 0.7 copy-done.12
  6.7 2.3 %shard_map.122 = (bf16[272,128]{1,0:T(8,128)(2,1)S(1)}, bf16[272,128]{1,0:T(8,128)(2,1)S(1)}, bf16[272,128]{1,0:T(8,128)(2,1)S(1)}, bf16[272,128]{1,0:T(8,128)(2...) custom-call(s32[4]{0:T(128)S(1)} %copy-done.8, s32[4]{0:T(128)S(1)} %copy-done.10, ...), custom_call_target="tpu_custom_call" | custom-call | tf_op jit(solution)/shard_map/pallas_call | solution.py:288
  9.1 0.6 collective-permute-start
  9.6 2.4 %collective-permute-start.1 = (bf16[272,128]{1,0:T(8,128)(2,1)S(1)}, bf16[272,128]{1,0:T(8,128)(2,1)S(1)}, u32[]{:S(2)}, u32[]{:S(2)}) collective-permute-start(bf16[272,128]{1,0:T(8,128)(2,1)S(1)} %get-tuple-element.19), channel_id=1, source_target_pairs={{0,16},{8,24},{16,0},{24,8},{32,48},{40,56},{48,32},{56,40},{64,80... | collective-permute-start | bytes 208904 | tf_op jit(solution)/shard_map/ppermute | solution.py:319
  12.0 1.8 %collective-permute-done.r1 = bf16[272,128]{1,0:T(8,128)(2,1)S(1)} collective-permute-done((bf16[272,128]{1,0:T(8,128)(2,1)S(1)}, bf16[272,128]{1,0:T(8,128)(2,1)S(1)}, u32[]{:S(2)}, u32[]{:S(2)}) %collective-permute-start) | collective-permute-done | bytes 69664 | tf_op jit(solution)/shard_map/ppermute | solution.py:319
  13.8 1.9 %collective-permute-done.1.r2 = bf16[272,128]{1,0:T(8,128)(2,1)S(1)} collective-permute-done((bf16[272,128]{1,0:T(8,128)(2,1)S(1)}, bf16[272,128]{1,0:T(8,128)(2,1)S(1)}, u32[]{:S(2)}, u32[]{:S(2)}) %collective-permute-start.1) | collective-permute-done | bytes 69664 | tf_op jit(solution)/shard_map/ppermute | solution.py:319
  15.7 1.8 %collective-permute-done.2.r3 = bf16[272,128]{1,0:T(8,128)(2,1)S(1)} collective-permute-done((bf16[272,128]{1,0:T(8,128)(2,1)S(1)}, bf16[272,128]{1,0:T(8,128)(2,1)S(1)}, u32[]{:S(2)}, u32[]{:S(2)}) %collective-permute-start.2) | collective-permute-done | bytes 69664 | tf_op jit(solution)/shard_map/ppermute | solution.py:319
  17.6 0.1 shard_map.124
  17.7 3.8 %collective-permute-start.3 = (bf16[272,128]{1,0:T(8,128)(2,1)S(1)}, bf16[272,128]{1,0:T(8,128)(2,1)S(1)}, u32[]{:S(2)}, u32[]{:S(2)}) collective-permute-start(bf16[272,128]{1,0:T(8,128)(2,1)S(1)} %shard_map.124), channel_id=1, source_target_pairs={{0,32},{8,40},{16,48},{24,56},{32,64},{40,72},{48,80},{56,88},{64,... | collective-permute-start | bytes 208904 | tf_op jit(solution)/shard_map/ppermute | solution.py:319
  21.5 0.7 collective-permute-start.4
  22.2 8.7 %collective-permute-start.11 = (bf16[384,256]{1,0:T(8,128)(2,1)S(1)}, bf16[384,256]{1,0:T(8,128)(2,1)S(1)}, u32[]{:S(2)}, u32[]{:S(2)}) collective-permute-start(bf16[384,256]{1,0:T(8,128)(2,1)S(1)} %get-tuple-element.27.own), channel_id=1, source_target_pairs={{0,8},{8,16},{16,24},{24,32},{32,40},{40,48},{48,56},{56,64},{64,7... | collective-permute-start | bytes 589832 | tf_op jit(solution)/shard_map/ppermute | solution.py:319
  30.9 1.3 %collective-permute-start.12 = (bf16[384,256]{1,0:T(8,128)(2,1)S(1)}, bf16[384,256]{1,0:T(8,128)(2,1)S(1)}, u32[]{:S(2)}, u32[]{:S(2)}) collective-permute-start(bf16[384,256]{1,0:T(8,128)(2,1)S(1)} %get-tuple-element.27.own), channel_id=1, source_target_pairs={{0,16},{8,24},{16,32},{24,40},{32,48},{40,56},{48,64},{64,80},{72,... | collective-permute-start | bytes 589832 | tf_op jit(solution)/shard_map/ppermute | solution.py:319
  32.2 1.3 %collective-permute-start.13 = (bf16[384,256]{1,0:T(8,128)(2,1)S(1)}, bf16[384,256]{1,0:T(8,128)(2,1)S(1)}, u32[]{:S(2)}, u32[]{:S(2)}) collective-permute-start(bf16[384,256]{1,0:T(8,128)(2,1)S(1)} %get-tuple-element.27.own), channel_id=1, source_target_pairs={{0,24},{8,32},{16,40},{24,48},{32,56},{40,64},{64,88},{72,96},{80,... | collective-permute-start | bytes 589832 | tf_op jit(solution)/shard_map/ppermute | solution.py:319
  33.5 0.0 collective-permute-done.4.z2
  33.5 0.2 shard_map.125
  33.7 3.9 %collective-permute-start.5 = (bf16[256,128]{1,0:T(8,128)(2,1)S(1)}, bf16[256,128]{1,0:T(8,128)(2,1)S(1)}, u32[]{:S(2)}, u32[]{:S(2)}) collective-permute-start(bf16[256,128]{1,0:T(8,128)(2,1)S(1)} %get-tuple-element.22), channel_id=1, source_target_pairs={{0,8},{8,16},{16,24},{24,0},{32,40},{40,48},{48,56},{56,32},{64,72... | collective-permute-start | bytes 196616 | tf_op jit(solution)/shard_map/ppermute | solution.py:319
  37.6 3.0 %collective-permute-start.6 = (bf16[256,128]{1,0:T(8,128)(2,1)S(1)}, bf16[256,128]{1,0:T(8,128)(2,1)S(1)}, u32[]{:S(2)}, u32[]{:S(2)}) collective-permute-start(bf16[256,128]{1,0:T(8,128)(2,1)S(1)} %get-tuple-element.23), channel_id=1, source_target_pairs={{0,16},{8,24},{16,0},{24,8},{32,48},{40,56},{48,32},{56,40},{64,80... | collective-permute-start | bytes 196616 | tf_op jit(solution)/shard_map/ppermute | solution.py:319
  40.6 0.0 collective-permute-done.5.p1
  40.6 2.1 %collective-permute-start.7 = (bf16[256,128]{1,0:T(8,128)(2,1)S(1)}, bf16[256,128]{1,0:T(8,128)(2,1)S(1)}, u32[]{:S(2)}, u32[]{:S(2)}) collective-permute-start(bf16[256,128]{1,0:T(8,128)(2,1)S(1)} %get-tuple-element.24), channel_id=1, source_target_pairs={{0,24},{8,0},{16,8},{24,16},{32,56},{40,32},{48,40},{56,48},{64,88... | collective-permute-start | bytes 196616 | tf_op jit(solution)/shard_map/ppermute | solution.py:319
  42.7 4.4 %shard_map.123.intra = f32[384,1024]{1,0:T(8,128)S(1)} custom-call(s32[4]{0:T(128)S(1)} %copy-done.9, s32[4]{0:T(128)S(1)} %copy-done.11, bf16[384,1024]{1,0:T(8,128)(2,1)S(1)} %copy-done.4, bf16[384,1024]{1,0:T(8,128)(2,1)S(1)} %copy-done.2, bf16[384,1024]{1,0:T(8,128)(2,1)S(1)} %copy-done.3, f32[384,8]{1,0:T(8,128)S(1)} %get-tuple-element.15.cum, ...), custom_call_target="tpu_custom_call" | custom-call | tf_op jit(solution)/shard_map/pallas_call | solution.py:288
  47.2 0.0 copy-start
  47.2 0.0 collective-permute-done.7.p3
  47.2 1.6 %shard_map.126 = (f32[384,1024]{1,0:T(8,128)S(1)}, f32[8,384]{1,0:T(8,128)S(1)}) custom-call(s32[4]{0:T(128)S(1)} %copy-done.9, s32[4]{0:T(128)S(1)} %copy-done.11, bf16[384,1024]{1,0:T(8,128)(2,1)S(1)} %copy-done.4, f32[384,1024]{1,0:T(8,128)S(1)} %shard_map.123.intra, bf16[256,128]{1,0:T(8,128)(2,1)S(1)} %get-tuple-element.21.p0, ...), custom_call_target="tpu_custom_call" | custom-call | tf_op jit(solution)/shard_map/pallas_call | solution.py:288
  48.8 1.2 %collective-permute-done.8 = f32[8,384]{1,0:T(8,128)S(1)} collective-permute-done((f32[8,384]{1,0:T(8,128)S(1)}, f32[8,384]{1,0:T(8,128)S(1)}, u32[]{:S(2)}, u32[]{:S(2)}) %collective-permute-start.8) | collective-permute-done | bytes 12320 | tf_op jit(solution)/shard_map/ppermute | solution.py:354
  50.0 1.6 %collective-permute-start.9 = (f32[8,384]{1,0:T(8,128)S(1)}, f32[8,384]{1,0:T(8,128)S(1)}, u32[]{:S(2)}, u32[]{:S(2)}) collective-permute-start(f32[8,384]{1,0:T(8,128)S(1)} %add.6), channel_id=1, source_target_pairs={{0,2},{1,3},{2,0},{3,1},{4,6},{5,7},{6,4},{7,5},{8,10},{9,11},{10,... | collective-permute-start | bytes 36872 | tf_op jit(solution)/shard_map/ppermute | solution.py:354
  51.6 1.3 %collective-permute-start.14 = (bf16[384,256]{1,0:T(8,128)(2,1)S(1)}, bf16[384,256]{1,0:T(8,128)(2,1)S(1)}, u32[]{:S(2)}, u32[]{:S(2)}) collective-permute-start(bf16[384,256]{1,0:T(8,128)(2,1)S(1)} %get-tuple-element.27.own), channel_id=1, source_target_pairs={{0,32},{8,40},{16,48},{24,56},{32,64},{64,96},{72,104},{80,112},{8... | collective-permute-start | bytes 589832 | tf_op jit(solution)/shard_map/ppermute | solution.py:319
  52.9 0.0 collective-permute-done.11.f1
  52.9 1.3 %collective-permute-start.15 = (bf16[384,256]{1,0:T(8,128)(2,1)S(1)}, bf16[384,256]{1,0:T(8,128)(2,1)S(1)}, u32[]{:S(2)}, u32[]{:S(2)}) collective-permute-start(bf16[384,256]{1,0:T(8,128)(2,1)S(1)} %get-tuple-element.27.own), channel_id=1, source_target_pairs={{0,40},{8,48},{16,56},{24,64},{64,104},{72,112},{80,120},{88,128},... | collective-permute-start | bytes 589832 | tf_op jit(solution)/shard_map/ppermute | solution.py:319
  54.2 1.3 %collective-permute-start.16 = (bf16[384,256]{1,0:T(8,128)(2,1)S(1)}, bf16[384,256]{1,0:T(8,128)(2,1)S(1)}, u32[]{:S(2)}, u32[]{:S(2)}) collective-permute-start(bf16[384,256]{1,0:T(8,128)(2,1)S(1)} %get-tuple-element.27.own), channel_id=1, source_target_pairs={{0,48},{8,56},{16,64},{64,112},{72,120},{80,128},{128,176},{136,18... | collective-permute-start | bytes 589832 | tf_op jit(solution)/shard_map/ppermute | solution.py:319
  55.5 1.3 %collective-permute-start.17 = (bf16[384,256]{1,0:T(8,128)(2,1)S(1)}, bf16[384,256]{1,0:T(8,128)(2,1)S(1)}, u32[]{:S(2)}, u32[]{:S(2)}) collective-permute-start(bf16[384,256]{1,0:T(8,128)(2,1)S(1)} %get-tuple-element.27.own), channel_id=1, source_target_pairs={{0,56},{8,64},{64,120},{72,128},{128,184},{136,192},{192,248},{1,5... | collective-permute-start | bytes 589832 | tf_op jit(solution)/shard_map/ppermute | solution.py:319
  56.8 0.0 collective-permute-done.9
  56.8 0.7 collective-permute-start.18
  57.5 2.9 %collective-permute-done.14.f4 = bf16[384,256]{1,0:T(8,128)(2,1)S(1)} collective-permute-done((bf16[384,256]{1,0:T(8,128)(2,1)S(1)}, bf16[384,256]{1,0:T(8,128)(2,1)S(1)}, u32[]{:S(2)}, u32[]{:S(2)}) %collective-permute-start.14) | collective-permute-done | bytes 196640 | tf_op jit(solution)/shard_map/ppermute | solution.py:319
  60.4 2.9 %collective-permute-start.10 = (f32[8,384]{1,0:T(8,128)S(1)}, f32[8,384]{1,0:T(8,128)S(1)}, u32[]{:S(2)}, u32[]{:S(2)}) collective-permute-start(f32[8,384]{1,0:T(8,128)S(1)} %add.7.squares), channel_id=1, source_target_pairs={{0,4},{1,5},{2,6},{3,7},{4,0},{5,1},{6,2},{7,3},{8,12},{9,13},{10,... | collective-permute-start | bytes 36872 | tf_op jit(solution)/shard_map/ppermute | solution.py:354
  63.4 3.6 %collective-permute-done.15.f5 = bf16[384,256]{1,0:T(8,128)(2,1)S(1)} collective-permute-done((bf16[384,256]{1,0:T(8,128)(2,1)S(1)}, bf16[384,256]{1,0:T(8,128)(2,1)S(1)}, u32[]{:S(2)}, u32[]{:S(2)}) %collective-permute-start.15) | collective-permute-done | bytes 196640 | tf_op jit(solution)/shard_map/ppermute | solution.py:319
  66.9 5.0 %collective-permute-done.16.f6 = bf16[384,256]{1,0:T(8,128)(2,1)S(1)} collective-permute-done((bf16[384,256]{1,0:T(8,128)(2,1)S(1)}, bf16[384,256]{1,0:T(8,128)(2,1)S(1)}, u32[]{:S(2)}, u32[]{:S(2)}) %collective-permute-start.16) | collective-permute-done | bytes 196640 | tf_op jit(solution)/shard_map/ppermute | solution.py:319
  71.9 3.4 %collective-permute-done.17.f7 = bf16[384,256]{1,0:T(8,128)(2,1)S(1)} collective-permute-done((bf16[384,256]{1,0:T(8,128)(2,1)S(1)}, bf16[384,256]{1,0:T(8,128)(2,1)S(1)}, u32[]{:S(2)}, u32[]{:S(2)}) %collective-permute-start.17) | collective-permute-done | bytes 196640 | tf_op jit(solution)/shard_map/ppermute | solution.py:319
  75.3 11.2 %shard_map.128.rest_0_ = bf16[384,512]{1,0:T(8,128)(2,1)S(1)} custom-call(s32[4]{0:T(128)S(1)} %copy-done.9, s32[4]{0:T(128)S(1)} %copy-done.11, bf16[384,1024]{1,0:T(8,128)(2,1)S(1)} %copy-done, bf16[384,256]{1,0:T(8,128)(2,1)S(1)} %get-tuple-element.27.own, bf16[384,256]{1,0:T(8,128)(2,1)S(1)} %collective-permute-done.11.f1, ...), custom_call_target="tpu_custom_call" | custom-call | tf_op jit(solution)/shard_map/pallas_call | solution.py:288
  86.6 0.0 copy-start.5
  86.6 0.0 copy-start.13
  86.6 11.9 %shard_map.129 = bf16[384,1024]{1,0:T(8,128)(2,1)} custom-call(s32[4]{0:T(128)S(1)} %copy-done.9, s32[4]{0:T(128)S(1)} %copy-done.11, bf16[384,1024]{1,0:T(8,128)(2,1)S(1)} %copy-done, bf16[384,256]{1,0:T(8,128)(2,1)S(1)} %get-tuple-element.27.own, bf16[384,256]{1,0:T(8,128)(2,1)S(1)} %collective-permute-done.11.f1, ...), custom_call_target="tpu_custom_call" | custom-call | tf_op jit(solution)/shard_map/pallas_call | solution.py:288
  98.6 1.6 %shard_map.127 = bf16[384,1024]{1,0:T(8,128)(2,1)} custom-call(f32[384,1024]{1,0:T(8,128)S(1)} %get-tuple-element.25.heads, bf16[384,1024]{1,0:T(8,128)(2,1)S(1)} %copy-done.5, f32[1,1024]{1,0:T(1,128)S(1)} %bitcast.3, f32[8,384]{1,0:T(8,128)S(1)} %add.7.squares, f32[8,384]{1,0:T(8,128)S(1)} %collective-permute-done.10.others), custom_call_target="tpu_custom_call" | custom-call | tf_op jit(solution)/shard_map/pallas_call | solution.py:288
  (28 shorter events, 0.1 us)
Async XLA Ops:
  0.6 42.1 %copy-start.9 = (s32[4]{0:T(128)S(1)}, s32[4]{0:T(128)}, u32[]{:S(2)}) copy-start(s32[4]{0:T(128)} %starts.9) | copy-start | bytes 52
  0.6 42.1 %copy-start.11 = (s32[4]{0:T(128)S(1)}, s32[4]{0:T(128)}, u32[]{:S(2)}) copy-start(s32[4]{0:T(128)} %lengths.9) | copy-start | bytes 52
  0.7 1.1 %copy-start.1 = (bf16[384,1024]{1,0:T(8,128)(2,1)S(1)}, bf16[384,1024]{1,0:T(8,128)(2,1)}, u32[]{:S(2)}) copy-start(bf16[384,1024]{1,0:T(8,128)(2,1)} %key.3) | copy-start | bytes 2359300
  1.8 1.1 %copy-start.3 = (bf16[384,1024]{1,0:T(8,128)(2,1)S(1)}, bf16[384,1024]{1,0:T(8,128)(2,1)}, u32[]{:S(2)}) copy-start(bf16[384,1024]{1,0:T(8,128)(2,1)} %value.3) | copy-start | bytes 2359300
  2.9 0.9 copy-start.6
  3.8 0.9 copy-start.7
  4.7 0.7 copy-start.8
  5.4 0.7 copy-start.10
  6.0 0.7 copy-start.12
  6.7 36.0 %copy-start.2 = (bf16[384,1024]{1,0:T(8,128)(2,1)S(1)}, bf16[384,1024]{1,0:T(8,128)(2,1)}, u32[]{:S(2)}) copy-start(bf16[384,1024]{1,0:T(8,128)(2,1)} %key.3) | copy-start | bytes 2359300
  6.7 36.0 %copy-start.4 = (bf16[384,1024]{1,0:T(8,128)(2,1)S(1)}, bf16[384,1024]{1,0:T(8,128)(2,1)}, u32[]{:S(2)}) copy-start(bf16[384,1024]{1,0:T(8,128)(2,1)} %query.5) | copy-start | bytes 2359300
  9.1 4.7 %collective-permute-start = (bf16[272,128]{1,0:T(8,128)(2,1)S(1)}, bf16[272,128]{1,0:T(8,128)(2,1)S(1)}, u32[]{:S(2)}, u32[]{:S(2)}) collective-permute-start(bf16[272,128]{1,0:T(8,128)(2,1)S(1)} %get-tuple-element.18), channel_id=1, source_target_pairs={{0,8},{8,16},{16,24},{24,0},{32,40},{40,48},{48,56},{56,32},{64,72... | collective-permute-start | bytes 208904 | tf_op jit(solution)/shard_map/ppermute | solution.py:319
  9.6 6.1 %collective-permute-start.1 = (bf16[272,128]{1,0:T(8,128)(2,1)S(1)}, bf16[272,128]{1,0:T(8,128)(2,1)S(1)}, u32[]{:S(2)}, u32[]{:S(2)}) collective-permute-start(bf16[272,128]{1,0:T(8,128)(2,1)S(1)} %get-tuple-element.19), channel_id=1, source_target_pairs={{0,16},{8,24},{16,0},{24,8},{32,48},{40,56},{48,32},{56,40},{64,80... | collective-permute-start | bytes 208904 | tf_op jit(solution)/shard_map/ppermute | solution.py:319
  12.0 5.5 %collective-permute-start.2 = (bf16[272,128]{1,0:T(8,128)(2,1)S(1)}, bf16[272,128]{1,0:T(8,128)(2,1)S(1)}, u32[]{:S(2)}, u32[]{:S(2)}) collective-permute-start(bf16[272,128]{1,0:T(8,128)(2,1)S(1)} %get-tuple-element.20), channel_id=1, source_target_pairs={{0,24},{8,0},{16,8},{24,16},{32,56},{40,32},{48,40},{56,48},{64,88... | collective-permute-start | bytes 208904 | tf_op jit(solution)/shard_map/ppermute | solution.py:319
  17.7 15.8 %collective-permute-start.3 = (bf16[272,128]{1,0:T(8,128)(2,1)S(1)}, bf16[272,128]{1,0:T(8,128)(2,1)S(1)}, u32[]{:S(2)}, u32[]{:S(2)}) collective-permute-start(bf16[272,128]{1,0:T(8,128)(2,1)S(1)} %shard_map.124), channel_id=1, source_target_pairs={{0,32},{8,40},{16,48},{24,56},{32,64},{40,72},{48,80},{56,88},{64,... | collective-permute-start | bytes 208904 | tf_op jit(solution)/shard_map/ppermute | solution.py:319
  21.5 12.0 %collective-permute-start.4 = (bf16[272,128]{1,0:T(8,128)(2,1)S(1)}, bf16[272,128]{1,0:T(8,128)(2,1)S(1)}, u32[]{:S(2)}, u32[]{:S(2)}) collective-permute-start(bf16[272,128]{1,0:T(8,128)(2,1)S(1)} %shard_map.124), channel_id=1, source_target_pairs={{0,64},{8,72},{16,80},{24,88},{64,128},{72,136},{80,144},{88,152},... | collective-permute-start | bytes 208904 | tf_op jit(solution)/shard_map/ppermute | solution.py:319
  22.2 30.7 %collective-permute-start.11 = (bf16[384,256]{1,0:T(8,128)(2,1)S(1)}, bf16[384,256]{1,0:T(8,128)(2,1)S(1)}, u32[]{:S(2)}, u32[]{:S(2)}) collective-permute-start(bf16[384,256]{1,0:T(8,128)(2,1)S(1)} %get-tuple-element.27.own), channel_id=1, source_target_pairs={{0,8},{8,16},{16,24},{24,32},{32,40},{40,48},{48,56},{56,64},{64,7... | collective-permute-start | bytes 589832 | tf_op jit(solution)/shard_map/ppermute | solution.py:319
  30.9 23.3 %collective-permute-start.12 = (bf16[384,256]{1,0:T(8,128)(2,1)S(1)}, bf16[384,256]{1,0:T(8,128)(2,1)S(1)}, u32[]{:S(2)}, u32[]{:S(2)}) collective-permute-start(bf16[384,256]{1,0:T(8,128)(2,1)S(1)} %get-tuple-element.27.own), channel_id=1, source_target_pairs={{0,16},{8,24},{16,32},{24,40},{32,48},{40,56},{48,64},{64,80},{72,... | collective-permute-start | bytes 589832 | tf_op jit(solution)/shard_map/ppermute | solution.py:319
  32.2 23.3 %collective-permute-start.13 = (bf16[384,256]{1,0:T(8,128)(2,1)S(1)}, bf16[384,256]{1,0:T(8,128)(2,1)S(1)}, u32[]{:S(2)}, u32[]{:S(2)}) collective-permute-start(bf16[384,256]{1,0:T(8,128)(2,1)S(1)} %get-tuple-element.27.own), channel_id=1, source_target_pairs={{0,24},{8,32},{16,40},{24,48},{32,56},{40,64},{64,88},{72,96},{80,... | collective-permute-start | bytes 589832 | tf_op jit(solution)/shard_map/ppermute | solution.py:319
  33.7 7.0 %collective-permute-start.5 = (bf16[256,128]{1,0:T(8,128)(2,1)S(1)}, bf16[256,128]{1,0:T(8,128)(2,1)S(1)}, u32[]{:S(2)}, u32[]{:S(2)}) collective-permute-start(bf16[256,128]{1,0:T(8,128)(2,1)S(1)} %get-tuple-element.22), channel_id=1, source_target_pairs={{0,8},{8,16},{16,24},{24,0},{32,40},{40,48},{48,56},{56,32},{64,72... | collective-permute-start | bytes 196616 | tf_op jit(solution)/shard_map/ppermute | solution.py:319
  37.6 9.6 %collective-permute-start.6 = (bf16[256,128]{1,0:T(8,128)(2,1)S(1)}, bf16[256,128]{1,0:T(8,128)(2,1)S(1)}, u32[]{:S(2)}, u32[]{:S(2)}) collective-permute-start(bf16[256,128]{1,0:T(8,128)(2,1)S(1)} %get-tuple-element.23), channel_id=1, source_target_pairs={{0,16},{8,24},{16,0},{24,8},{32,48},{40,56},{48,32},{56,40},{64,80... | collective-permute-start | bytes 196616 | tf_op jit(solution)/shard_map/ppermute | solution.py:319
  40.6 6.6 %collective-permute-start.7 = (bf16[256,128]{1,0:T(8,128)(2,1)S(1)}, bf16[256,128]{1,0:T(8,128)(2,1)S(1)}, u32[]{:S(2)}, u32[]{:S(2)}) collective-permute-start(bf16[256,128]{1,0:T(8,128)(2,1)S(1)} %get-tuple-element.24), channel_id=1, source_target_pairs={{0,24},{8,0},{16,8},{24,16},{32,56},{40,32},{48,40},{56,48},{64,88... | collective-permute-start | bytes 196616 | tf_op jit(solution)/shard_map/ppermute | solution.py:319
  47.2 28.2 %copy-start = (bf16[384,1024]{1,0:T(8,128)(2,1)S(1)}, bf16[384,1024]{1,0:T(8,128)(2,1)}, u32[]{:S(2)}) copy-start(bf16[384,1024]{1,0:T(8,128)(2,1)} %query.7) | copy-start | bytes 2359300
  48.8 1.2 %collective-permute-start.8 = (f32[8,384]{1,0:T(8,128)S(1)}, f32[8,384]{1,0:T(8,128)S(1)}, u32[]{:S(2)}, u32[]{:S(2)}) collective-permute-start(f32[8,384]{1,0:T(8,128)S(1)} %get-tuple-element.26), channel_id=1, source_target_pairs={{0,1},{1,0},{2,3},{3,2},{4,5},{5,4},{6,7},{7,6},{8,9},{9,8},{10,11... | collective-permute-start | bytes 36872 | tf_op jit(solution)/shard_map/ppermute | solution.py:354
  50.0 6.8 %collective-permute-start.9 = (f32[8,384]{1,0:T(8,128)S(1)}, f32[8,384]{1,0:T(8,128)S(1)}, u32[]{:S(2)}, u32[]{:S(2)}) collective-permute-start(f32[8,384]{1,0:T(8,128)S(1)} %add.6), channel_id=1, source_target_pairs={{0,2},{1,3},{2,0},{3,1},{4,6},{5,7},{6,4},{7,5},{8,10},{9,11},{10,... | collective-permute-start | bytes 36872 | tf_op jit(solution)/shard_map/ppermute | solution.py:354
  51.6 8.9 %collective-permute-start.14 = (bf16[384,256]{1,0:T(8,128)(2,1)S(1)}, bf16[384,256]{1,0:T(8,128)(2,1)S(1)}, u32[]{:S(2)}, u32[]{:S(2)}) collective-permute-start(bf16[384,256]{1,0:T(8,128)(2,1)S(1)} %get-tuple-element.27.own), channel_id=1, source_target_pairs={{0,32},{8,40},{16,48},{24,56},{32,64},{64,96},{72,104},{80,112},{8... | collective-permute-start | bytes 589832 | tf_op jit(solution)/shard_map/ppermute | solution.py:319
  52.9 14.0 %collective-permute-start.15 = (bf16[384,256]{1,0:T(8,128)(2,1)S(1)}, bf16[384,256]{1,0:T(8,128)(2,1)S(1)}, u32[]{:S(2)}, u32[]{:S(2)}) collective-permute-start(bf16[384,256]{1,0:T(8,128)(2,1)S(1)} %get-tuple-element.27.own), channel_id=1, source_target_pairs={{0,40},{8,48},{16,56},{24,64},{64,104},{72,112},{80,120},{88,128},... | collective-permute-start | bytes 589832 | tf_op jit(solution)/shard_map/ppermute | solution.py:319
  54.2 17.7 %collective-permute-start.16 = (bf16[384,256]{1,0:T(8,128)(2,1)S(1)}, bf16[384,256]{1,0:T(8,128)(2,1)S(1)}, u32[]{:S(2)}, u32[]{:S(2)}) collective-permute-start(bf16[384,256]{1,0:T(8,128)(2,1)S(1)} %get-tuple-element.27.own), channel_id=1, source_target_pairs={{0,48},{8,56},{16,64},{64,112},{72,120},{80,128},{128,176},{136,18... | collective-permute-start | bytes 589832 | tf_op jit(solution)/shard_map/ppermute | solution.py:319
  55.5 19.8 %collective-permute-start.17 = (bf16[384,256]{1,0:T(8,128)(2,1)S(1)}, bf16[384,256]{1,0:T(8,128)(2,1)S(1)}, u32[]{:S(2)}, u32[]{:S(2)}) collective-permute-start(bf16[384,256]{1,0:T(8,128)(2,1)S(1)} %get-tuple-element.27.own), channel_id=1, source_target_pairs={{0,56},{8,64},{64,120},{72,128},{128,184},{136,192},{192,248},{1,5... | collective-permute-start | bytes 589832 | tf_op jit(solution)/shard_map/ppermute | solution.py:319
  56.8 18.5 %collective-permute-start.18 = (bf16[384,256]{1,0:T(8,128)(2,1)S(1)}, bf16[384,256]{1,0:T(8,128)(2,1)S(1)}, u32[]{:S(2)}, u32[]{:S(2)}) collective-permute-start(bf16[384,256]{1,0:T(8,128)(2,1)S(1)} %get-tuple-element.27.own), channel_id=1, source_target_pairs={{0,64},{64,128},{128,192},{1,65},{65,129},{129,193},{2,66},{66,130... | collective-permute-start | bytes 589832 | tf_op jit(solution)/shard_map/ppermute | solution.py:319
  60.4 38.1 %collective-permute-start.10 = (f32[8,384]{1,0:T(8,128)S(1)}, f32[8,384]{1,0:T(8,128)S(1)}, u32[]{:S(2)}, u32[]{:S(2)}) collective-permute-start(f32[8,384]{1,0:T(8,128)S(1)} %add.7.squares), channel_id=1, source_target_pairs={{0,4},{1,5},{2,6},{3,7},{4,0},{5,1},{6,2},{7,3},{8,12},{9,13},{10,... | collective-permute-start | bytes 36872 | tf_op jit(solution)/shard_map/ppermute | solution.py:354
  86.6 12.0 %copy-start.5 = (bf16[384,1024]{1,0:T(8,128)(2,1)S(1)}, bf16[384,1024]{1,0:T(8,128)(2,1)}, u32[]{:S(2)}) copy-start(bf16[384,1024]{1,0:T(8,128)(2,1)} %gate.1) | copy-start | bytes 2359300
  86.6 12.0 %copy-start.13 = (f32[1024]{0:T(1024)S(1)}, f32[1024]{0:T(1024)}, u32[]{:S(2)}) copy-start(f32[1024]{0:T(1024)} %param.16) | copy-start | bytes 12292

commit v2 on v0

--- a/solution.py
+++ b/solution.py
@@ -12,6 +12,7 @@
 H = 8
 SPAN = 8
 NEG = -1e30
+FAR = 4
 GROUP = 2
 EPS = 1e-06
 GONE = -1e5
@@ -47,10 +48,16 @@
     return rows < jnp.where(rows < bound, end_prev, end_cur)
 
 
-def state_kernel(starts, lengths, key, value, dec_t, soft_key, soft_value, s0, s1, s2, s3, cum,
-                 cum_t, both, pack, rest):
-    both[:, 0:D] = soft_key[...]
-    both[:, D:2 * D] = soft_value[...]
+def state_kernel(starts_in, lengths_in, dec_in, key_in, value_in, soft_key, soft_value,
+                 s0, s1, s2, s3, cum, cum_t, both,
+                 starts, lengths, dec_t, key, value, pack, rest, sems):
+    moves = ((dec_in, dec_t), (starts_in, starts), (lengths_in, lengths), (key_in, key),
+             (value_in, value), (soft_key, both.at[:, 0:D]), (soft_value, both.at[:, D:2 * D]))
+    copies = [pltpu.make_async_copy(a, b, sems.at[n]) for n, (a, b) in enumerate(moves)]
+    for copy in copies:
+        copy.start()
+    for copy in copies[:3]:
+        copy.wait()
     _, place, bound, _, end_cur = marks(starts, lengths)
     lower = (iota((T, T), 1) <= iota((T, T), 0)).astype(F32)
     dec = dec_t[...]
@@ -62,6 +69,8 @@
     last = col[T - 1:T, :]
     to_end = jnp.where(keep, jnp.exp(last - col), 0.0)
     total = jnp.where(place == 0, GONE, last)
+    for copy in copies[3:]:
+        copy.wait()
     for h in range(H):
         part = slice(h * D, (h + 1) * D)
         scaled = (key[:, part].astype(F32) * to_end[:, h:h + 1]).astype(BF16)
@@ -189,8 +198,14 @@
         out[:, lanes] = (heads[:, lanes] * scale * gain[:, lanes] * gated).astype(BF16)
 
 
-def soft_kernel(starts, lengths, query, own, f1, f2, f3, f4, f5, f6, f7, f8, out,
-                keys, values, asks, top, acc):
+def soft_kernel(starts, lengths, query, own, *rest, low, last):
+    far = rest[:FAR]
+    if last:
+        top_in, acc_in, out, keys, values, asks, top, acc = rest[FAR:]
+        top[...] = top_in[...]
+        acc[...] = acc_in[...]
+    else:
+        top, acc, keys, values, asks = rest[FAR:]
     room, place, bound, end_prev, end_cur = marks(starts, lengths)
     tail = place == 0
     count = jnp.where(tail, jnp.where(room > 0, SPAN, 0), place)
@@ -198,19 +213,19 @@
     begin = starts[begin_room] - begin_room * SPAN * T
     factor = (D ** -0.5) * 1.4426950408889634
     ones = jnp.ones((T, D), BF16)
-    for m, ref in enumerate((own, f1, f2, f3, f4, f5, f6, f7, f8)):
-        @pl.when(m <= count)
+    for slot, ref in enumerate((own,) + far):
+        @pl.when((slot + low - 1 <= count) if slot else (low == 1))
         def _():
-            keys[m] = ref[:, 0:D]
-            values[m, :, 0:D] = ref[:, D:2 * D]
-            values[m, :, D:2 * D] = ones
+            keys[slot] = ref[:, 0:D]
+            values[slot, :, 0:D] = ref[:, D:2 * D]
+            values[slot, :, D:2 * D] = ones
 
     for h in range(H):
         asks[h] = query[:, h * D:(h + 1) * D]
 
-    def attend(m, size, hidden, fresh=False):
-        k = keys[m]
-        v = values[m]
+    def attend(slot, size, hidden, fresh=False):
+        k = keys[slot]
+        v = values[slot]
         span = GROUP if size == T else 1
         many = span * size
 
@@ -218,14 +233,12 @@
             return lax.dot_general(asks[h:h + span, 0:size, :].reshape(many, D), k, NT,
                                    preferred_element_type=F32)
 
-        heads = range(0, H, span)
         ahead = ask(0)
-        for h in heads:
+        for h in range(0, H, span):
             x = ahead
             if h + span < H:
                 ahead = ask(h + span)
-            if hidden is not None:
-                x = (x.reshape(span, size, T) + hidden[None]).reshape(many, T)
+            x = (x.reshape(span, size, T) + hidden[None]).reshape(many, T)
             parts = [x[:, j * D:(j + 1) * D] for j in range(T // D)]
             best = functools.reduce(jnp.maximum, parts)
             peak = jnp.broadcast_to(jnp.max(best, axis=1, keepdims=True), (many, D)) * factor
@@ -241,50 +254,57 @@
                 mixed = mixed + kept * jnp.concatenate([shrink, shrink], axis=1)
             acc[h:h + span, 0:size, :] = mixed.reshape(span, size, 2 * D)
 
-    t = iota((T, T), 0)
-    i = iota((T, T), 1)
-    seen = (i <= t) & ((i >= bound) | (t < bound))
-    attend(0, T, jnp.where(seen, 0.0, NEG), fresh=True)
+    if low == 1:
+        t = iota((T, T), 0)
+        i = iota((T, T), 1)
+        seen = (i <= t) & ((i >= bound) | (t < bound))
+        attend(0, T, jnp.where(seen, 0.0, NEG), fresh=True)
+    slots = jnp.minimum(count, low + FAR - 1) - low + 2
+
+    def first_key(slot):
+        return jnp.where(slot + low - 1 == count, begin, 0)
 
     @pl.when(place > 0)
     def _():
-        def middle(m, _):
-            attend(m, T, None)
+        def one(slot, _):
+            attend(slot, T, jnp.where(iota((1, T), 1) < first_key(slot), NEG, 0.0))
             return 0
 
-        lax.fori_loop(1, count, middle, 0)
-        attend(count, T, jnp.where(iota((1, T), 1) < begin, NEG, 0.0))
+        lax.fori_loop(1, slots, one, 0)
 
     half = T // 2
 
     @pl.when(tail & (count > 0))
     def _():
-        def one(m, _):
-            row_ok = iota((half, T), 0) < bound
-            first_key = jnp.where(m == count, begin, 0)
-            attend(m, half, jnp.where(row_ok & (iota((half, T), 1) >= first_key), 0.0, NEG))
+        def one(slot, _):
+            seen = (iota((half, T), 0) < bound) & (iota((half, T), 1) >= first_key(slot))
+            attend(slot, half, jnp.where(seen, 0.0, NEG))
             return 0
 
-        lax.fori_loop(1, count + 1, one, 0)
-
-    valid = valid_rows((T, 1), bound, end_prev, end_cur)
-    for h in range(H):
-        mixed = acc[h, :, 0:D] / acc[h, :, D:2 * D]
-        out[:, h * D:(h + 1) * D] = jnp.where(valid, mixed, 0.0).astype(BF16)
+        lax.fori_loop(1, slots, one, 0)
+
+    if last:
+        valid = valid_rows((T, 1), bound, end_prev, end_cur)
+        for h in range(H):
+            mixed = acc[h, :, 0:D] / acc[h, :, D:2 * D]
+            out[:, h * D:(h + 1) * D] = jnp.where(valid, mixed, 0.0).astype(BF16)
 
 
 smem = pl.BlockSpec(memory_space=pltpu.SMEM)
 vmem = pl.BlockSpec(memory_space=pltpu.VMEM)
+hbm = pl.BlockSpec(memory_space=pltpu.HBM)
 
 
 def shape(*dims, kind=F32):
     return jax.ShapeDtypeStruct(dims, kind)
 
 
-def call(kernel, tables, operands, outs, scratch=()):
+def call(kernel, tables, operands, outs, scratch=(), room=12, given=vmem):
     return pl.pallas_call(
-        kernel, in_specs=[smem] * tables + [vmem] * (len(operands) - tables),
+        kernel, in_specs=[smem] * tables + [given] * (len(operands) - tables),
         out_specs=[vmem] * len(outs), out_shape=list(outs), scratch_shapes=list(scratch),
+        compiler_params=pltpu.CompilerParams(
+            vmem_limit_bytes=room << 20),
     )(*operands)
 
 
@@ -317,10 +337,14 @@
 
     pair = shape(T, 2 * D, kind=BF16)
     *slices, cum, cum_t, kv = call(
-        state_kernel, 2,
-        (starts, lengths, lin_key, lin_value, lin_decay.T, soft_key, soft_value),
+        state_kernel, 0,
+        [pltpu.with_memory_space_constraint(x, pltpu.HBM) for x in
+         (starts, lengths, lin_decay.T, lin_key, lin_value, soft_key, soft_value)],
         [packed] * ROW + [shape(T, H), shape(H, T), pair],
-        [pltpu.VMEM((ROW, piece, D), BF16), pltpu.VMEM((ROW, EXTRA, D), BF16)])
+        [pltpu.SMEM(starts.shape, jnp.int32), pltpu.SMEM(lengths.shape, jnp.int32),
+         pltpu.VMEM((H, T), F32), pltpu.VMEM((T, width), BF16), pltpu.VMEM((T, width), BF16),
+         pltpu.VMEM((ROW, piece, D), BF16), pltpu.VMEM((ROW, EXTRA, D), BF16),
+         pltpu.SemaphoreType.DMA((7,))], given=hbm)
     row = [slices[0]] + [send(slices[j], around[j]) for j in range(1, ROW)]
 
     intra, = call(intra_kernel, 2,
@@ -336,7 +360,9 @@
         table + [pltpu.VMEM((ROW, piece, D), BF16)])
     before = [ready[0]] + [send(ready[j], around[j]) for j in range(1, ROW)]
 
-    far_kv = [send(kv, window(m, rooms)) for m in range(1, SPAN + 1)]
+    far_kv = [send(kv, window(m, rooms)) for m in range(1, ROW + 1)]
+    far_kv += [send(far_kv[ROW - 1], [(i + ROW, j) for i, j in window(m, rooms)])
+               for m in range(ROW + 1, SPAN + 1)]
 
     heads, squares = call(
         carry_kernel, 2, (starts, lengths, lin_query, intra, *before, cum),
@@ -349,12 +375,15 @@
         others = lax.ppermute(squares, "head", [(i, i ^ step) for i in range(share)])
         step *= 2
 
-    soft_out, = call(
-        soft_kernel, 2, (starts, lengths, soft_query, kv, *far_kv),
-        [shape(T, width, kind=BF16)],
-        [pltpu.VMEM((SPAN + 1, T, D), BF16), pltpu.VMEM((SPAN + 1, T, 2 * D), BF16),
-         pltpu.VMEM((H, T, D), BF16), pltpu.VMEM((H, T, D), F32),
-         pltpu.VMEM((H, T, 2 * D), F32)])
+    held = [shape(H, T, D), shape(H, T, 2 * D)]
+    room = [pltpu.VMEM((FAR + 1, T, D), BF16), pltpu.VMEM((FAR + 1, T, 2 * D), BF16),
+            pltpu.VMEM((H, T, D), BF16)]
+    asked = (starts, lengths, soft_query, kv)
+    running = call(functools.partial(soft_kernel, low=1, last=False), 2,
+                   (*asked, *far_kv[:FAR]), held, room, room=20)
+    soft_out, = call(functools.partial(soft_kernel, low=FAR + 1, last=True), 2,
+                     (*asked, *far_kv[FAR:], *running), [shape(T, width, kind=BF16)],
+                     room + [pltpu.VMEM(x.shape, F32) for x in held], room=24)
 
     lin_out, = call(
         functools.partial(norm_kernel, features=width * share), 0,

time: 108 us -> 85.1 us (0.79)
  waiting for transfers between devices: 22 us -> 11.8 us
  Pallas kernels: 41.3 us -> 32.6 us
  local copies, waits for them, and re-layouts: 4.41 us -> 0.03 us
  starting transfers between devices: 38.2 us -> 39.4 us
    ppermute x16, waiting for transfers between devices: 20.7 us -> 11.8 us  [send(): return lax.ppermute(x, 'ctx', pairs)]
    pallas_call x7 -> x8, Pallas kernels: 41.3 us -> 32.6 us  [call(): pl.pallas_call(kernel, in_specs=[smem] * tables + [given] * (len(operands...]
    unnamed x38 -> x16, local copies, waits for them, and re-layouts: 4.41 us -> 0.03 us
    ppermute x3, waiting for transfers between devices: 1.39 us -> 0.01 us  [per_device(): lax.ppermute(squares, 'head', [(i, i ^ step) for i in range(share)])]
  transfers between devices with their start and end apart: 19 -> 19, of which waited for: 8 -> 5; matrix products, arithmetic and copies ran while one was open for 1% -> 0% of each run, Pallas kernels for 30% -> 24%
where the time goes in v2:
time: 85.1 us; the launch traced here: 84.8 us
  starting transfers between devices  39.4 us (46%)
  Pallas kernels  32.6 us (38%)
  waiting for transfers between devices  11.8 us (14%)
  between operations  0.94 us (1%)
    ppermute x16, starting transfers between devices, send(): return lax.ppermute(x, 'ctx', pairs)  34.5 us
    pallas_call x8, Pallas kernels, call(): pl.pallas_call(kernel, in_specs=[smem] * tables + [given] * (len(operands...  32.6 us
    ppermute x16, waiting for transfers between devices, send(): return lax.ppermute(x, 'ctx', pairs)  11.8 us
    ppermute x3, starting transfers between devices, per_device(): lax.ppermute(squares, 'head', [(i, i ^ step) for i in range(share)])  4.86 us
  transfers between devices with their start and end apart: 19, of which 5 were waited for; matrix products, arithmetic and copies ran while one was open for 0% of the time, Pallas kernels for 24%

profile of v2, /device:TPU:38, one launch (start us, length us, event | category | flops | bytes accessed | tf_op | source)
XLA Modules:
  0.0 84.8 jit_solution(12231235387983315414)
XLA Ops:
  0.7 3.3 %shard_map.122 = (bf16[272,128]{1,0:T(8,128)(2,1)S(1)}, bf16[272,128]{1,0:T(8,128)(2,1)S(1)}, bf16[272,128]{1,0:T(8,128)(2,1)S(1)}, bf16[272,128]{1,0:T(8,128)(2...) custom-call(s32[4]{0:T(128)} %starts.7, s32[4]{0:T(128)} %lengths.7, ...), custom_call_target="tpu_custom_call" | custom-call | tf_op jit(solution)/shard_map/pallas_call | solution.py:303
  4.0 0.6 collective-permute-start
  4.6 2.4 %collective-permute-start.1 = (bf16[272,128]{1,0:T(8,128)(2,1)S(1)}, bf16[272,128]{1,0:T(8,128)(2,1)S(1)}, u32[]{:S(2)}, u32[]{:S(2)}) collective-permute-start(bf16[272,128]{1,0:T(8,128)(2,1)S(1)} %get-tuple-element.21), channel_id=1, source_target_pairs={{0,16},{8,24},{16,0},{24,8},{32,48},{40,56},{48,32},{56,40},{64,80... | collective-permute-start | bytes 208904 | tf_op jit(solution)/shard_map/ppermute | solution.py:334
  7.0 0.0 collective-permute-start.2
  7.0 1.8 %collective-permute-done.r1 = bf16[272,128]{1,0:T(8,128)(2,1)S(1)} collective-permute-done((bf16[272,128]{1,0:T(8,128)(2,1)S(1)}, bf16[272,128]{1,0:T(8,128)(2,1)S(1)}, u32[]{:S(2)}, u32[]{:S(2)}) %collective-permute-start) | collective-permute-done | bytes 69664 | tf_op jit(solution)/shard_map/ppermute | solution.py:334
  8.7 1.9 %collective-permute-done.1.r2 = bf16[272,128]{1,0:T(8,128)(2,1)S(1)} collective-permute-done((bf16[272,128]{1,0:T(8,128)(2,1)S(1)}, bf16[272,128]{1,0:T(8,128)(2,1)S(1)}, u32[]{:S(2)}, u32[]{:S(2)}) %collective-permute-start.1) | collective-permute-done | bytes 69664 | tf_op jit(solution)/shard_map/ppermute | solution.py:334
  10.6 1.8 %collective-permute-done.2.r3 = bf16[272,128]{1,0:T(8,128)(2,1)S(1)} collective-permute-done((bf16[272,128]{1,0:T(8,128)(2,1)S(1)}, bf16[272,128]{1,0:T(8,128)(2,1)S(1)}, u32[]{:S(2)}, u32[]{:S(2)}) %collective-permute-start.2) | collective-permute-done | bytes 69664 | tf_op jit(solution)/shard_map/ppermute | solution.py:334
  12.5 0.1 shard_map.124
  12.6 3.8 %collective-permute-start.3 = (bf16[272,128]{1,0:T(8,128)(2,1)S(1)}, bf16[272,128]{1,0:T(8,128)(2,1)S(1)}, u32[]{:S(2)}, u32[]{:S(2)}) collective-permute-start(bf16[272,128]{1,0:T(8,128)(2,1)S(1)} %shard_map.124), channel_id=1, source_target_pairs={{0,32},{8,40},{16,48},{24,56},{32,64},{40,72},{48,80},{56,88},{64,... | collective-permute-start | bytes 208904 | tf_op jit(solution)/shard_map/ppermute | solution.py:334
  16.4 0.7 collective-permute-start.4
  17.1 1.3 %collective-permute-start.11 = (bf16[384,256]{1,0:T(8,128)(2,1)S(1)}, bf16[384,256]{1,0:T(8,128)(2,1)S(1)}, u32[]{:S(2)}, u32[]{:S(2)}) collective-permute-start(bf16[384,256]{1,0:T(8,128)(2,1)S(1)} %get-tuple-element.29.own), channel_id=1, source_target_pairs={{0,32},{8,40},{16,48},{24,56},{32,64},{64,96},{72,104},{80,112},{8... | collective-permute-start | bytes 589832 | tf_op jit(solution)/shard_map/ppermute | solution.py:334
  18.4 9.3 %collective-permute-start.16 = (bf16[384,256]{1,0:T(8,128)(2,1)S(1)}, bf16[384,256]{1,0:T(8,128)(2,1)S(1)}, u32[]{:S(2)}, u32[]{:S(2)}) collective-permute-start(bf16[384,256]{1,0:T(8,128)(2,1)S(1)} %get-tuple-element.29.own), channel_id=1, source_target_pairs={{0,8},{8,16},{16,24},{24,32},{32,40},{40,48},{48,56},{56,64},{64,7... | collective-permute-start | bytes 589832 | tf_op jit(solution)/shard_map/ppermute | solution.py:334
  27.7 1.3 %collective-permute-start.17 = (bf16[384,256]{1,0:T(8,128)(2,1)S(1)}, bf16[384,256]{1,0:T(8,128)(2,1)S(1)}, u32[]{:S(2)}, u32[]{:S(2)}) collective-permute-start(bf16[384,256]{1,0:T(8,128)(2,1)S(1)} %get-tuple-element.29.own), channel_id=1, source_target_pairs={{0,16},{8,24},{16,32},{24,40},{32,48},{40,56},{48,64},{64,80},{72,... | collective-permute-start | bytes 589832 | tf_op jit(solution)/shard_map/ppermute | solution.py:334
  29.0 0.0 collective-permute-done.3.z1
  29.0 0.0 collective-permute-done.4.z2
  29.0 0.2 shard_map.125
  29.2 1.3 %collective-permute-start.5 = (bf16[256,128]{1,0:T(8,128)(2,1)S(1)}, bf16[256,128]{1,0:T(8,128)(2,1)S(1)}, u32[]{:S(2)}, u32[]{:S(2)}) collective-permute-start(bf16[256,128]{1,0:T(8,128)(2,1)S(1)} %get-tuple-element.24), channel_id=1, source_target_pairs={{0,8},{8,16},{16,24},{24,0},{32,40},{40,48},{48,56},{56,32},{64,72... | collective-permute-start | bytes 196616 | tf_op jit(solution)/shard_map/ppermute | solution.py:334
  30.5 3.1 %collective-permute-start.6 = (bf16[256,128]{1,0:T(8,128)(2,1)S(1)}, bf16[256,128]{1,0:T(8,128)(2,1)S(1)}, u32[]{:S(2)}, u32[]{:S(2)}) collective-permute-start(bf16[256,128]{1,0:T(8,128)(2,1)S(1)} %get-tuple-element.25), channel_id=1, source_target_pairs={{0,16},{8,24},{16,0},{24,8},{32,48},{40,56},{48,32},{56,40},{64,80... | collective-permute-start | bytes 196616 | tf_op jit(solution)/shard_map/ppermute | solution.py:334
  33.5 4.9 %collective-permute-done.5.p1 = bf16[256,128]{1,0:T(8,128)(2,1)S(1)} collective-permute-done((bf16[256,128]{1,0:T(8,128)(2,1)S(1)}, bf16[256,128]{1,0:T(8,128)(2,1)S(1)}, u32[]{:S(2)}, u32[]{:S(2)}) %collective-permute-start.5) | collective-permute-done | bytes 65568 | tf_op jit(solution)/shard_map/ppermute | solution.py:334
  38.4 0.0 collective-permute-start.7
  38.4 0.0 copy-done.1
  38.4 4.4 %shard_map.123.intra = f32[384,1024]{1,0:T(8,128)S(1)} custom-call(s32[4]{0:T(128)S(1)} %copy-done.5, s32[4]{0:T(128)S(1)} %copy-done.6, bf16[384,1024]{1,0:T(8,128)(2,1)S(1)} %copy-done.3, bf16[384,1024]{1,0:T(8,128)(2,1)S(1)} %copy-done, bf16[384,1024]{1,0:T(8,128)(2,1)S(1)} %copy-done.1, f32[384,8]{1,0:T(8,128)S(1)} %get-tuple-element.17.cum, ...), custom_call_target="tpu_custom_call" | custom-call | tf_op jit(solution)/shard_map/pallas_call | solution.py:303
  42.9 0.0 copy-start.2
  42.9 0.0 collective-permute-done.6.p2
  42.9 1.4 %collective-permute-done.7.p3 = bf16[256,128]{1,0:T(8,128)(2,1)S(1)} collective-permute-done((bf16[256,128]{1,0:T(8,128)(2,1)S(1)}, bf16[256,128]{1,0:T(8,128)(2,1)S(1)}, u32[]{:S(2)}, u32[]{:S(2)}) %collective-permute-start.7) | collective-permute-done | bytes 65568 | tf_op jit(solution)/shard_map/ppermute | solution.py:334
  44.3 1.6 %shard_map.126 = (f32[384,1024]{1,0:T(8,128)S(1)}, f32[8,384]{1,0:T(8,128)S(1)}) custom-call(s32[4]{0:T(128)S(1)} %copy-done.5, s32[4]{0:T(128)S(1)} %copy-done.6, bf16[384,1024]{1,0:T(8,128)(2,1)S(1)} %copy-done.3, f32[384,1024]{1,0:T(8,128)S(1)} %shard_map.123.intra, bf16[256,128]{1,0:T(8,128)(2,1)S(1)} %get-tuple-element.23.p0, ...), custom_call_target="tpu_custom_call" | custom-call | tf_op jit(solution)/shard_map/pallas_call | solution.py:303
  45.9 0.0 collective-permute-start.8
  45.9 1.4 %collective-permute-start.18 = (bf16[384,256]{1,0:T(8,128)(2,1)S(1)}, bf16[384,256]{1,0:T(8,128)(2,1)S(1)}, u32[]{:S(2)}, u32[]{:S(2)}) collective-permute-start(bf16[384,256]{1,0:T(8,128)(2,1)S(1)} %get-tuple-element.29.own), channel_id=1, source_target_pairs={{0,24},{8,32},{16,40},{24,48},{32,56},{40,64},{64,88},{72,96},{80,... | collective-permute-start | bytes 589832 | tf_op jit(solution)/shard_map/ppermute | solution.py:334
  47.4 0.0 collective-permute-done.8
  47.4 1.7 %collective-permute-start.9 = (f32[8,384]{1,0:T(8,128)S(1)}, f32[8,384]{1,0:T(8,128)S(1)}, u32[]{:S(2)}, u32[]{:S(2)}) collective-permute-start(f32[8,384]{1,0:T(8,128)S(1)} %add.6), channel_id=1, source_target_pairs={{0,2},{1,3},{2,0},{3,1},{4,6},{5,7},{6,4},{7,5},{8,10},{9,11},{10,... | collective-permute-start | bytes 36872 | tf_op jit(solution)/shard_map/ppermute | solution.py:375
  49.1 0.0 collective-permute-done.11.rest_3_
  49.1 6.2 %collective-permute-start.12 = (bf16[384,256]{1,0:T(8,128)(2,1)S(1)}, bf16[384,256]{1,0:T(8,128)(2,1)S(1)}, u32[]{:S(2)}, u32[]{:S(2)}) collective-permute-start(bf16[384,256]{1,0:T(8,128)(2,1)S(1)} %collective-permute-done.11.rest_3_), channel_id=1, source_target_pairs={{32,40},{40,48},{48,56},{56,64},{96,104},{104,112},{112,120},{120,... | collective-permute-start | bytes 589832 | tf_op jit(solution)/shard_map/ppermute | solution.py:334
  55.2 0.0 collective-permute-done.16.rest_0_
  55.2 1.3 %collective-permute-start.13 = (bf16[384,256]{1,0:T(8,128)(2,1)S(1)}, bf16[384,256]{1,0:T(8,128)(2,1)S(1)}, u32[]{:S(2)}, u32[]{:S(2)}) collective-permute-start(bf16[384,256]{1,0:T(8,128)(2,1)S(1)} %collective-permute-done.11.rest_3_), channel_id=1, source_target_pairs={{32,48},{40,56},{48,64},{96,112},{104,120},{112,128},{160,176},{16... | collective-permute-start | bytes 589832 | tf_op jit(solution)/shard_map/ppermute | solution.py:334
  56.5 0.0 collective-permute-done.17.rest_1_
  56.5 1.3 %collective-permute-start.14 = (bf16[384,256]{1,0:T(8,128)(2,1)S(1)}, bf16[384,256]{1,0:T(8,128)(2,1)S(1)}, u32[]{:S(2)}, u32[]{:S(2)}) collective-permute-start(bf16[384,256]{1,0:T(8,128)(2,1)S(1)} %collective-permute-done.11.rest_3_), channel_id=1, source_target_pairs={{32,56},{40,64},{96,120},{104,128},{160,184},{168,192},{224,248},{... | collective-permute-start | bytes 589832 | tf_op jit(solution)/shard_map/ppermute | solution.py:334
  57.8 0.0 collective-permute-done.9
  57.9 0.7 collective-permute-start.15
  58.5 0.0 collective-permute-done.18.rest_2_
  58.6 3.2 %collective-permute-start.10 = (f32[8,384]{1,0:T(8,128)S(1)}, f32[8,384]{1,0:T(8,128)S(1)}, u32[]{:S(2)}, u32[]{:S(2)}) collective-permute-start(f32[8,384]{1,0:T(8,128)S(1)} %add.7.squares), channel_id=1, source_target_pairs={{0,4},{1,5},{2,6},{3,7},{4,0},{5,1},{6,2},{7,3},{8,12},{9,13},{10,... | collective-permute-start | bytes 36872 | tf_op jit(solution)/shard_map/ppermute | solution.py:375
  61.7 12.6 %shard_map.128 = (f32[8,384,128]{2,1,0:T(8,128)S(1)}, f32[8,384,256]{2,1,0:T(8,128)S(1)}) custom-call(s32[4]{0:T(128)S(1)} %copy-done.5, s32[4]{0:T(128)S(1)} %copy-done.6, bf16[384,1024]{1,0:T(8,128)(2,1)S(1)} %copy-done.2, bf16[384,256]{1,0:T(8,128)(2,1)S(1)} %get-tuple-element.29.own, bf16[384,256]{1,0:T(8,128)(2,1)S(1)} %collective-permute-done.16.rest_0_, ...), custom_call_target="tpu_custom_call" | custom-call | tf_op jit(solution)/shard_map/pallas_call | solution.py:303
  74.3 0.0 collective-permute-done.10.others
  74.4 1.6 %shard_map.127 = bf16[384,1024]{1,0:T(8,128)(2,1)} custom-call(f32[384,1024]{1,0:T(8,128)S(1)} %get-tuple-element.27.heads, bf16[384,1024]{1,0:T(8,128)(2,1)S(1)} %copy-done.4, f32[1,1024]{1,0:T(1,128)S(1)} %bitcast.2, f32[8,384]{1,0:T(8,128)S(1)} %add.7.squares, f32[8,384]{1,0:T(8,128)S(1)} %collective-permute-done.10.others), custom_call_target="tpu_custom_call" | custom-call | tf_op jit(solution)/shard_map/pallas_call | solution.py:303
  76.0 0.0 collective-permute-done.12.rest_0_
  76.0 0.0 collective-permute-done.13.rest_1_
  76.0 0.0 collective-permute-done.14.rest_2_
  76.0 0.0 collective-permute-done.15.rest_3_
  76.0 8.8 %shard_map.129 = bf16[384,1024]{1,0:T(8,128)(2,1)} custom-call(s32[4]{0:T(128)S(1)} %copy-done.5, s32[4]{0:T(128)S(1)} %copy-done.6, bf16[384,1024]{1,0:T(8,128)(2,1)S(1)} %copy-done.2, bf16[384,256]{1,0:T(8,128)(2,1)S(1)} %get-tuple-element.29.own, bf16[384,256]{1,0:T(8,128)(2,1)S(1)} %collective-permute-done.12.rest_0_, ...), custom_call_target="tpu_custom_call" | custom-call | tf_op jit(solution)/shard_map/pallas_call | solution.py:303
  (16 shorter events, 0.0 us)
Async XLA Ops:
  0.6 37.8 %copy-start = (bf16[384,1024]{1,0:T(8,128)(2,1)S(1)}, bf16[384,1024]{1,0:T(8,128)(2,1)}, u32[]{:S(2)}) copy-start(bf16[384,1024]{1,0:T(8,128)(2,1)} %key.1) | copy-start | bytes 2359300
  0.6 37.8 %copy-start.1 = (bf16[384,1024]{1,0:T(8,128)(2,1)S(1)}, bf16[384,1024]{1,0:T(8,128)(2,1)}, u32[]{:S(2)}) copy-start(bf16[384,1024]{1,0:T(8,128)(2,1)} %value.1) | copy-start | bytes 2359300
  0.7 37.8 %copy-start.5 = (s32[4]{0:T(128)S(1)}, s32[4]{0:T(128)}, u32[]{:S(2)}) copy-start(s32[4]{0:T(128)} %starts.7) | copy-start | bytes 52
  0.7 37.8 %copy-start.6 = (s32[4]{0:T(128)S(1)}, s32[4]{0:T(128)}, u32[]{:S(2)}) copy-start(s32[4]{0:T(128)} %lengths.7) | copy-start | bytes 52
  0.7 37.8 %copy-start.3 = (bf16[384,1024]{1,0:T(8,128)(2,1)S(1)}, bf16[384,1024]{1,0:T(8,128)(2,1)}, u32[]{:S(2)}) copy-start(bf16[384,1024]{1,0:T(8,128)(2,1)} %query.5) | copy-start | bytes 2359300
  4.0 4.7 %collective-permute-start = (bf16[272,128]{1,0:T(8,128)(2,1)S(1)}, bf16[272,128]{1,0:T(8,128)(2,1)S(1)}, u32[]{:S(2)}, u32[]{:S(2)}) collective-permute-start(bf16[272,128]{1,0:T(8,128)(2,1)S(1)} %get-tuple-element.20), channel_id=1, source_target_pairs={{0,8},{8,16},{16,24},{24,0},{32,40},{40,48},{48,56},{56,32},{64,72... | collective-permute-start | bytes 208904 | tf_op jit(solution)/shard_map/ppermute | solution.py:334
  4.6 6.1 %collective-permute-start.1 = (bf16[272,128]{1,0:T(8,128)(2,1)S(1)}, bf16[272,128]{1,0:T(8,128)(2,1)S(1)}, u32[]{:S(2)}, u32[]{:S(2)}) collective-permute-start(bf16[272,128]{1,0:T(8,128)(2,1)S(1)} %get-tuple-element.21), channel_id=1, source_target_pairs={{0,16},{8,24},{16,0},{24,8},{32,48},{40,56},{48,32},{56,40},{64,80... | collective-permute-start | bytes 208904 | tf_op jit(solution)/shard_map/ppermute | solution.py:334
  7.0 5.5 %collective-permute-start.2 = (bf16[272,128]{1,0:T(8,128)(2,1)S(1)}, bf16[272,128]{1,0:T(8,128)(2,1)S(1)}, u32[]{:S(2)}, u32[]{:S(2)}) collective-permute-start(bf16[272,128]{1,0:T(8,128)(2,1)S(1)} %get-tuple-element.22), channel_id=1, source_target_pairs={{0,24},{8,0},{16,8},{24,16},{32,56},{40,32},{48,40},{56,48},{64,88... | collective-permute-start | bytes 208904 | tf_op jit(solution)/shard_map/ppermute | solution.py:334
  12.6 16.4 %collective-permute-start.3 = (bf16[272,128]{1,0:T(8,128)(2,1)S(1)}, bf16[272,128]{1,0:T(8,128)(2,1)S(1)}, u32[]{:S(2)}, u32[]{:S(2)}) collective-permute-start(bf16[272,128]{1,0:T(8,128)(2,1)S(1)} %shard_map.124), channel_id=1, source_target_pairs={{0,32},{8,40},{16,48},{24,56},{32,64},{40,72},{48,80},{56,88},{64,... | collective-permute-start | bytes 208904 | tf_op jit(solution)/shard_map/ppermute | solution.py:334
  16.4 12.6 %collective-permute-start.4 = (bf16[272,128]{1,0:T(8,128)(2,1)S(1)}, bf16[272,128]{1,0:T(8,128)(2,1)S(1)}, u32[]{:S(2)}, u32[]{:S(2)}) collective-permute-start(bf16[272,128]{1,0:T(8,128)(2,1)S(1)} %shard_map.124), channel_id=1, source_target_pairs={{0,64},{8,72},{16,80},{24,88},{64,128},{72,136},{80,144},{88,152},... | collective-permute-start | bytes 208904 | tf_op jit(solution)/shard_map/ppermute | solution.py:334
  17.1 31.9 %collective-permute-start.11 = (bf16[384,256]{1,0:T(8,128)(2,1)S(1)}, bf16[384,256]{1,0:T(8,128)(2,1)S(1)}, u32[]{:S(2)}, u32[]{:S(2)}) collective-permute-start(bf16[384,256]{1,0:T(8,128)(2,1)S(1)} %get-tuple-element.29.own), channel_id=1, source_target_pairs={{0,32},{8,40},{16,48},{24,56},{32,64},{64,96},{72,104},{80,112},{8... | collective-permute-start | bytes 589832 | tf_op jit(solution)/shard_map/ppermute | solution.py:334
  18.4 36.8 %collective-permute-start.16 = (bf16[384,256]{1,0:T(8,128)(2,1)S(1)}, bf16[384,256]{1,0:T(8,128)(2,1)S(1)}, u32[]{:S(2)}, u32[]{:S(2)}) collective-permute-start(bf16[384,256]{1,0:T(8,128)(2,1)S(1)} %get-tuple-element.29.own), channel_id=1, source_target_pairs={{0,8},{8,16},{16,24},{24,32},{32,40},{40,48},{48,56},{56,64},{64,7... | collective-permute-start | bytes 589832 | tf_op jit(solution)/shard_map/ppermute | solution.py:334
  27.7 28.8 %collective-permute-start.17 = (bf16[384,256]{1,0:T(8,128)(2,1)S(1)}, bf16[384,256]{1,0:T(8,128)(2,1)S(1)}, u32[]{:S(2)}, u32[]{:S(2)}) collective-permute-start(bf16[384,256]{1,0:T(8,128)(2,1)S(1)} %get-tuple-element.29.own), channel_id=1, source_target_pairs={{0,16},{8,24},{16,32},{24,40},{32,48},{40,56},{48,64},{64,80},{72,... | collective-permute-start | bytes 589832 | tf_op jit(solution)/shard_map/ppermute | solution.py:334
  29.2 9.2 %collective-permute-start.5 = (bf16[256,128]{1,0:T(8,128)(2,1)S(1)}, bf16[256,128]{1,0:T(8,128)(2,1)S(1)}, u32[]{:S(2)}, u32[]{:S(2)}) collective-permute-start(bf16[256,128]{1,0:T(8,128)(2,1)S(1)} %get-tuple-element.24), channel_id=1, source_target_pairs={{0,8},{8,16},{16,24},{24,0},{32,40},{40,48},{48,56},{56,32},{64,72... | collective-permute-start | bytes 196616 | tf_op jit(solution)/shard_map/ppermute | solution.py:334
  30.5 12.4 %collective-permute-start.6 = (bf16[256,128]{1,0:T(8,128)(2,1)S(1)}, bf16[256,128]{1,0:T(8,128)(2,1)S(1)}, u32[]{:S(2)}, u32[]{:S(2)}) collective-permute-start(bf16[256,128]{1,0:T(8,128)(2,1)S(1)} %get-tuple-element.25), channel_id=1, source_target_pairs={{0,16},{8,24},{16,0},{24,8},{32,48},{40,56},{48,32},{56,40},{64,80... | collective-permute-start | bytes 196616 | tf_op jit(solution)/shard_map/ppermute | solution.py:334
  38.4 5.9 %collective-permute-start.7 = (bf16[256,128]{1,0:T(8,128)(2,1)S(1)}, bf16[256,128]{1,0:T(8,128)(2,1)S(1)}, u32[]{:S(2)}, u32[]{:S(2)}) collective-permute-start(bf16[256,128]{1,0:T(8,128)(2,1)S(1)} %get-tuple-element.26), channel_id=1, source_target_pairs={{0,24},{8,0},{16,8},{24,16},{32,56},{40,32},{48,40},{56,48},{64,88... | collective-permute-start | bytes 196616 | tf_op jit(solution)/shard_map/ppermute | solution.py:334
  42.9 18.8 %copy-start.2 = (bf16[384,1024]{1,0:T(8,128)(2,1)S(1)}, bf16[384,1024]{1,0:T(8,128)(2,1)}, u32[]{:S(2)}) copy-start(bf16[384,1024]{1,0:T(8,128)(2,1)} %query.7) | copy-start | bytes 2359300
  45.9 28.5 %copy-start.4 = (bf16[384,1024]{1,0:T(8,128)(2,1)S(1)}, bf16[384,1024]{1,0:T(8,128)(2,1)}, u32[]{:S(2)}) copy-start(bf16[384,1024]{1,0:T(8,128)(2,1)} %gate.1) | copy-start | bytes 2359300
  45.9 28.5 %copy-start.7 = (f32[1024]{0:T(1024)S(1)}, f32[1024]{0:T(1024)}, u32[]{:S(2)}) copy-start(f32[1024]{0:T(1024)} %param.16) | copy-start | bytes 12292
  45.9 1.5 %collective-permute-start.8 = (f32[8,384]{1,0:T(8,128)S(1)}, f32[8,384]{1,0:T(8,128)S(1)}, u32[]{:S(2)}, u32[]{:S(2)}) collective-permute-start(f32[8,384]{1,0:T(8,128)S(1)} %get-tuple-element.28), channel_id=1, source_target_pairs={{0,1},{1,0},{2,3},{3,2},{4,5},{5,4},{6,7},{7,6},{8,9},{9,8},{10,11... | collective-permute-start | bytes 36872 | tf_op jit(solution)/shard_map/ppermute | solution.py:375
  45.9 12.6 %collective-permute-start.18 = (bf16[384,256]{1,0:T(8,128)(2,1)S(1)}, bf16[384,256]{1,0:T(8,128)(2,1)S(1)}, u32[]{:S(2)}, u32[]{:S(2)}) collective-permute-start(bf16[384,256]{1,0:T(8,128)(2,1)S(1)} %get-tuple-element.29.own), channel_id=1, source_target_pairs={{0,24},{8,32},{16,40},{24,48},{32,56},{40,64},{64,88},{72,96},{80,... | collective-permute-start | bytes 589832 | tf_op jit(solution)/shard_map/ppermute | solution.py:334
  47.4 10.4 %collective-permute-start.9 = (f32[8,384]{1,0:T(8,128)S(1)}, f32[8,384]{1,0:T(8,128)S(1)}, u32[]{:S(2)}, u32[]{:S(2)}) collective-permute-start(f32[8,384]{1,0:T(8,128)S(1)} %add.6), channel_id=1, source_target_pairs={{0,2},{1,3},{2,0},{3,1},{4,6},{5,7},{6,4},{7,5},{8,10},{9,11},{10,... | collective-permute-start | bytes 36872 | tf_op jit(solution)/shard_map/ppermute | solution.py:375
  49.1 26.9 %collective-permute-start.12 = (bf16[384,256]{1,0:T(8,128)(2,1)S(1)}, bf16[384,256]{1,0:T(8,128)(2,1)S(1)}, u32[]{:S(2)}, u32[]{:S(2)}) collective-permute-start(bf16[384,256]{1,0:T(8,128)(2,1)S(1)} %collective-permute-done.11.rest_3_), channel_id=1, source_target_pairs={{32,40},{40,48},{48,56},{56,64},{96,104},{104,112},{112,120},{120,... | collective-permute-start | bytes 589832 | tf_op jit(solution)/shard_map/ppermute | solution.py:334
  55.2 20.8 %collective-permute-start.13 = (bf16[384,256]{1,0:T(8,128)(2,1)S(1)}, bf16[384,256]{1,0:T(8,128)(2,1)S(1)}, u32[]{:S(2)}, u32[]{:S(2)}) collective-permute-start(bf16[384,256]{1,0:T(8,128)(2,1)S(1)} %collective-permute-done.11.rest_3_), channel_id=1, source_target_pairs={{32,48},{40,56},{48,64},{96,112},{104,120},{112,128},{160,176},{16... | collective-permute-start | bytes 589832 | tf_op jit(solution)/shard_map/ppermute | solution.py:334
  56.5 19.4 %collective-permute-start.14 = (bf16[384,256]{1,0:T(8,128)(2,1)S(1)}, bf16[384,256]{1,0:T(8,128)(2,1)S(1)}, u32[]{:S(2)}, u32[]{:S(2)}) collective-permute-start(bf16[384,256]{1,0:T(8,128)(2,1)S(1)} %collective-permute-done.11.rest_3_), channel_id=1, source_target_pairs={{32,56},{40,64},{96,120},{104,128},{160,184},{168,192},{224,248},{... | collective-permute-start | bytes 589832 | tf_op jit(solution)/shard_map/ppermute | solution.py:334
  57.9 18.1 %collective-permute-start.15 = (bf16[384,256]{1,0:T(8,128)(2,1)S(1)}, bf16[384,256]{1,0:T(8,128)(2,1)S(1)}, u32[]{:S(2)}, u32[]{:S(2)}) collective-permute-start(bf16[384,256]{1,0:T(8,128)(2,1)S(1)} %collective-permute-done.11.rest_3_), channel_id=1, source_target_pairs={{32,64},{96,128},{160,192},{33,65},{97,129},{161,193},{34,66},{98,... | collective-permute-start | bytes 589832 | tf_op jit(solution)/shard_map/ppermute | solution.py:334
  58.6 15.8 %collective-permute-start.10 = (f32[8,384]{1,0:T(8,128)S(1)}, f32[8,384]{1,0:T(8,128)S(1)}, u32[]{:S(2)}, u32[]{:S(2)}) collective-permute-start(f32[8,384]{1,0:T(8,128)S(1)} %add.7.squares), channel_id=1, source_target_pairs={{0,4},{1,5},{2,6},{3,7},{4,0},{5,1},{6,2},{7,3},{8,12},{9,13},{10,... | collective-permute-start | bytes 36872 | tf_op jit(solution)/shard_map/ppermute | solution.py:375

commit v3 on v2

--- a/solution.py
+++ b/solution.py
@@ -111,8 +111,6 @@
 
 def row_kernel(own, r1, r2, r3, out, states, logs):
     gather_row(own, r1, r2, r3, states, logs)
-    at = iota((EXTRA, D), 0)
-    table = jnp.zeros((EXTRA, D), F32)
     for j in range(PAIR):
         part = slice(j * D, (j + 1) * D)
         c = [logs[w, 8 * j:8 * j + 1, :] for w in range(ROW)]
@@ -120,21 +118,14 @@
                  + jnp.exp(c[3] + c[2]) * states[1, part, :]
                  + jnp.exp(c[3] + c[2] + c[1]) * states[0, part, :])
         out[part, :] = total.astype(BF16)
-        one = jnp.broadcast_to(c[0] + c[1] + c[2] + c[3], (EXTRA, D))
-        a = one.astype(BF16).astype(F32)
-        b = (one - a).astype(BF16).astype(F32)
-        for i, x in enumerate((a, b, one - a - b)):
-            table = jnp.where(at == 3 * j + i, x, table)
-    out[PAIR * D:PAIR * D + EXTRA, :] = table.astype(BF16)
-
-
-def prefix_kernel(own, r1, r2, r3, z1, z2, p0, p1, p2, p3, states, logs, ready):
+
+
+def prefix_kernel(own, r1, r2, r3, above, p0, p1, p2, p3, states, logs, ready):
     gather_row(own, r1, r2, r3, states, logs)
-    decay = log_decays(z1)
     for j in range(PAIR):
         part = slice(j * D, (j + 1) * D)
         c = [logs[w, 8 * j:8 * j + 1, :] for w in range(ROW)]
-        state = (z1[part, :].astype(F32) + jnp.exp(decay[j]) * z2[part, :].astype(F32))
+        state = above[part, :].astype(F32)
         ready[0, part, :] = state.astype(BF16)
         state1 = states[0, part, :]
         ready[1, part, :] = (state1 + jnp.exp(c[0]) * state).astype(BF16)
@@ -145,6 +136,19 @@
     x = (lax.axis_index("ctx") % SPAN) % ROW
     for step, out in enumerate((p0, p1, p2, p3)):
         out[...] = ready[(x + step) % ROW]
+
+
+def pass_kernel(s0, s1, s2, s3, p0, p1, p2, p3, out):
+    x = (lax.axis_index("ctx") % SPAN) % ROW
+    entering = (p0, p3, p2, p1)
+    for step, ref in enumerate((s0, s1, s2, s3)):
+        w = (x + step) % ROW
+        logs = log_decays(ref)
+        for j in range(PAIR):
+            part = slice(j * D, (j + 1) * D)
+            state = (ref[part, :].astype(F32)
+                     + jnp.exp(logs[j]) * entering[step][part, :].astype(F32))
+            out[w, part, :] = state.astype(BF16)
 
 
 def intra_kernel(starts, lengths, query, key, value, cum, cum_t, out, bias):
@@ -165,11 +169,17 @@
             out[part, lanes] = jnp.dot(weights, value[0:wide, lanes], preferred_element_type=F32)
 
 
-def carry_kernel(starts, lengths, query, intra, p0, p1, p2, p3, cum, out, squares, states):
+def carry_kernel(starts, lengths, query, intra, p0, p1, p2, p3, passed, cum, out, squares,
+                 states):
     _, place, bound, end_prev, end_cur = marks(starts, lengths)
     x = place % ROW
     for step, ref in enumerate((p0, p1, p2, p3)):
         states[(x - step + ROW) % ROW] = ref[...]
+
+    @pl.when(place == 0)
+    def _():
+        states[...] = passed[...]
+
     rows = iota((T, 1), 0)
     valid = rows < jnp.where(rows < bound, end_prev, end_cur)
     enters = (rows < jnp.where(place > 0, T, bound)) & valid
@@ -327,8 +337,8 @@
     width = H * D
     piece = PAIR * D
     around = [[(i, i - i % ROW + (i + step) % ROW) for i in range(places)] for step in range(ROW)]
-    onward = [(i, i + ROW) for i in range(places - ROW)]
-    beyond = [(i, i + 2 * ROW) for i in range(places - 2 * ROW) if i // ROW % 2 == 0]
+    onward = [(i, i + ROW) for i in range(places) if i % SPAN < ROW]
+    next_room = [(i, i + 1) for i in range(SPAN - 1, places - 1, SPAN)]
 
     def send(x, pairs):
         return lax.ppermute(x, "ctx", pairs)
@@ -352,20 +362,22 @@
                   [shape(T, width)], [pltpu.VMEM((T, T), F32)])
 
     table = [pltpu.VMEM((ROW, piece, D), F32), pltpu.VMEM((ROW, 8 * PAIR, D), F32)]
-    row_total, = call(row_kernel, 0, row, [packed], table)
+    row_total, = call(row_kernel, 0, row, [shape(piece, D, kind=BF16)], table)
     above = send(row_total, onward)
-    above2 = send(row_total, beyond)
     ready = call(
-        prefix_kernel, 0, (*row, above, above2), [shape(piece, D, kind=BF16)] * ROW,
+        prefix_kernel, 0, (*row, above), [shape(piece, D, kind=BF16)] * ROW,
         table + [pltpu.VMEM((ROW, piece, D), BF16)])
     before = [ready[0]] + [send(ready[j], around[j]) for j in range(1, ROW)]
+
+    left, = call(pass_kernel, 0, (*slices, *before), [shape(ROW, piece, D, kind=BF16)])
+    passed = send(left, next_room)
 
     far_kv = [send(kv, window(m, rooms)) for m in range(1, ROW + 1)]
     far_kv += [send(far_kv[ROW - 1], [(i + ROW, j) for i, j in window(m, rooms)])
                for m in range(ROW + 1, SPAN + 1)]
 
     heads, squares = call(
-        carry_kernel, 2, (starts, lengths, lin_query, intra, *before, cum),
+        carry_kernel, 2, (starts, lengths, lin_query, intra, *before, passed, cum),
         [shape(T, width), shape(8, T)], [pltpu.VMEM((ROW, piece, D), BF16)])
     step = 1
     others = jnp.zeros_like(squares)

time: 85.1 us -> 87.6 us (1.029)
  waiting for transfers between devices: 11.8 us -> 16.7 us
  starting transfers between devices: 39.4 us -> 36.9 us
    ppermute x16, waiting for transfers between devices: 11.8 us -> 15.5 us  [send(): return lax.ppermute(x, 'ctx', pairs)]
    ppermute x16, starting transfers between devices: 34.5 us -> 32.2 us  [send(): return lax.ppermute(x, 'ctx', pairs)]
    ppermute x3, waiting for transfers between devices: 0.01 us -> 1.2 us  [per_device(): lax.ppermute(squares, 'head', [(i, i ^ step) for i in range(share)])]
    pallas_call x8 -> x9, Pallas kernels: 32.6 us -> 32.7 us  [call(): pl.pallas_call(kernel, in_specs=[smem] * tables + [given] * (len(operands...]
  transfers between devices with their start and end apart: 19 -> 19, of which waited for: 5 -> 8; matrix products, arithmetic and copies ran while one was open for 0% -> 0% of each run, Pallas kernels for 24% -> 31%
where the time goes in v3:
time: 87.6 us; the launch traced here: 87.3 us
  starting transfers between devices  36.9 us (42%)
  Pallas kernels  32.7 us (37%)
  waiting for transfers between devices  16.7 us (19%)
  between operations  0.96 us (1%)
    pallas_call x9, Pallas kernels, call(): pl.pallas_call(kernel, in_specs=[smem] * tables + [given] * (len(operands...  32.7 us
    ppermute x16, starting transfers between devices, send(): return lax.ppermute(x, 'ctx', pairs)  32.2 us
    ppermute x16, waiting for transfers between devices, send(): return lax.ppermute(x, 'ctx', pairs)  15.5 us
    ppermute x3, starting transfers between devices, per_device(): lax.ppermute(squares, 'head', [(i, i ^ step) for i in range(share)])  4.75 us
  transfers between devices with their start and end apart: 19, of which 8 were waited for; matrix products, arithmetic and copies ran while one was open for 0% of the time, Pallas kernels for 31%

profile of v3, /device:TPU:38, one launch (start us, length us, event | category | flops | bytes accessed | tf_op | source)
XLA Modules:
  0.0 87.3 jit_solution(13718723599057299613)
XLA Ops:
  0.7 3.3 %shard_map.122 = (bf16[272,128]{1,0:T(8,128)(2,1)S(1)}, bf16[272,128]{1,0:T(8,128)(2,1)S(1)}, bf16[272,128]{1,0:T(8,128)(2,1)S(1)}, bf16[272,128]{1,0:T(8,128)(2...) custom-call(s32[4]{0:T(128)} %starts.7, s32[4]{0:T(128)} %lengths.7, ...), custom_call_target="tpu_custom_call" | custom-call | tf_op jit(solution)/shard_map/pallas_call | solution.py:313
  4.0 0.6 collective-permute-start
  4.6 2.4 %collective-permute-start.1 = (bf16[272,128]{1,0:T(8,128)(2,1)S(1)}, bf16[272,128]{1,0:T(8,128)(2,1)S(1)}, u32[]{:S(2)}, u32[]{:S(2)}) collective-permute-start(bf16[272,128]{1,0:T(8,128)(2,1)S(1)} %get-tuple-element.21.s2), channel_id=1, source_target_pairs={{0,16},{8,24},{16,0},{24,8},{32,48},{40,56},{48,32},{56,40},{64,80... | collective-permute-start | bytes 208904 | tf_op jit(solution)/shard_map/ppermute | solution.py:344
  7.0 0.0 collective-permute-start.2
  7.0 1.8 %collective-permute-done.r1 = bf16[272,128]{1,0:T(8,128)(2,1)S(1)} collective-permute-done((bf16[272,128]{1,0:T(8,128)(2,1)S(1)}, bf16[272,128]{1,0:T(8,128)(2,1)S(1)}, u32[]{:S(2)}, u32[]{:S(2)}) %collective-permute-start) | collective-permute-done | bytes 69664 | tf_op jit(solution)/shard_map/ppermute | solution.py:344
  8.7 1.9 %collective-permute-done.1.r2 = bf16[272,128]{1,0:T(8,128)(2,1)S(1)} collective-permute-done((bf16[272,128]{1,0:T(8,128)(2,1)S(1)}, bf16[272,128]{1,0:T(8,128)(2,1)S(1)}, u32[]{:S(2)}, u32[]{:S(2)}) %collective-permute-start.1) | collective-permute-done | bytes 69664 | tf_op jit(solution)/shard_map/ppermute | solution.py:344
  10.6 1.8 %collective-permute-done.2.r3 = bf16[272,128]{1,0:T(8,128)(2,1)S(1)} collective-permute-done((bf16[272,128]{1,0:T(8,128)(2,1)S(1)}, bf16[272,128]{1,0:T(8,128)(2,1)S(1)}, u32[]{:S(2)}, u32[]{:S(2)}) %collective-permute-start.2) | collective-permute-done | bytes 69664 | tf_op jit(solution)/shard_map/ppermute | solution.py:344
  12.5 0.1 shard_map.124
  12.6 1.3 %collective-permute-start.3 = (bf16[256,128]{1,0:T(8,128)(2,1)S(1)}, bf16[256,128]{1,0:T(8,128)(2,1)S(1)}, u32[]{:S(2)}, u32[]{:S(2)}) collective-permute-start(bf16[256,128]{1,0:T(8,128)(2,1)S(1)} %shard_map.124), channel_id=1, source_target_pairs={{0,32},{8,40},{16,48},{24,56},{64,96},{72,104},{80,112},{88,120},{... | collective-permute-start | bytes 196616 | tf_op jit(solution)/shard_map/ppermute | solution.py:344
  13.9 4.9 %collective-permute-done.3.above = bf16[256,128]{1,0:T(8,128)(2,1)S(1)} collective-permute-done((bf16[256,128]{1,0:T(8,128)(2,1)S(1)}, bf16[256,128]{1,0:T(8,128)(2,1)S(1)}, u32[]{:S(2)}, u32[]{:S(2)}) %collective-permute-start.3) | collective-permute-done | bytes 65568 | tf_op jit(solution)/shard_map/ppermute | solution.py:344
  18.8 0.1 shard_map.125
  18.9 0.7 collective-permute-start.4
  19.6 1.1 %collective-permute-start.5 = (bf16[256,128]{1,0:T(8,128)(2,1)S(1)}, bf16[256,128]{1,0:T(8,128)(2,1)S(1)}, u32[]{:S(2)}, u32[]{:S(2)}) collective-permute-start(bf16[256,128]{1,0:T(8,128)(2,1)S(1)} %get-tuple-element.25), channel_id=1, source_target_pairs={{0,16},{8,24},{16,0},{24,8},{32,48},{40,56},{48,32},{56,40},{64,80... | collective-permute-start | bytes 196616 | tf_op jit(solution)/shard_map/ppermute | solution.py:344
  20.7 0.4 collective-permute-start.6
  21.1 2.2 %collective-permute-done.4.p1 = bf16[256,128]{1,0:T(8,128)(2,1)S(1)} collective-permute-done((bf16[256,128]{1,0:T(8,128)(2,1)S(1)}, bf16[256,128]{1,0:T(8,128)(2,1)S(1)}, u32[]{:S(2)}, u32[]{:S(2)}) %collective-permute-start.4) | collective-permute-done | bytes 65568 | tf_op jit(solution)/shard_map/ppermute | solution.py:344
  23.3 2.1 %collective-permute-done.5.p2 = bf16[256,128]{1,0:T(8,128)(2,1)S(1)} collective-permute-done((bf16[256,128]{1,0:T(8,128)(2,1)S(1)}, bf16[256,128]{1,0:T(8,128)(2,1)S(1)}, u32[]{:S(2)}, u32[]{:S(2)}) %collective-permute-start.5) | collective-permute-done | bytes 65568 | tf_op jit(solution)/shard_map/ppermute | solution.py:344
  25.4 0.8 collective-permute-done.6.p3
  26.1 0.1 shard_map.126
  26.3 4.6 %collective-permute-start.7 = (bf16[4,256,128]{2,1,0:T(8,128)(2,1)S(1)}, bf16[4,256,128]{2,1,0:T(8,128)(2,1)S(1)}, u32[]{:S(2)}, u32[]{:S(2)}) collective-permute-start(bf16[4,256,128]{2,1,0:T(8,128)(2,1)S(1)} %shard_map.126), channel_id=1, source_target_pairs={{56,64},{120,128},{184,192},{57,65},{121,129},{185,193},{58,66},{1... | collective-permute-start | bytes 786440 | tf_op jit(solution)/shard_map/ppermute | solution.py:344
  30.9 1.3 %collective-permute-start.11 = (bf16[384,256]{1,0:T(8,128)(2,1)S(1)}, bf16[384,256]{1,0:T(8,128)(2,1)S(1)}, u32[]{:S(2)}, u32[]{:S(2)}) collective-permute-start(bf16[384,256]{1,0:T(8,128)(2,1)S(1)} %get-tuple-element.29.own), channel_id=1, source_target_pairs={{0,32},{8,40},{16,48},{24,56},{32,64},{64,96},{72,104},{80,112},{8... | collective-permute-start | bytes 589832 | tf_op jit(solution)/shard_map/ppermute | solution.py:344
  32.2 3.6 %collective-permute-start.16 = (bf16[384,256]{1,0:T(8,128)(2,1)S(1)}, bf16[384,256]{1,0:T(8,128)(2,1)S(1)}, u32[]{:S(2)}, u32[]{:S(2)}) collective-permute-start(bf16[384,256]{1,0:T(8,128)(2,1)S(1)} %get-tuple-element.29.own), channel_id=1, source_target_pairs={{0,8},{8,16},{16,24},{24,32},{32,40},{40,48},{48,56},{56,64},{64,7... | collective-permute-start | bytes 589832 | tf_op jit(solution)/shard_map/ppermute | solution.py:344
  35.9 1.3 %collective-permute-start.17 = (bf16[384,256]{1,0:T(8,128)(2,1)S(1)}, bf16[384,256]{1,0:T(8,128)(2,1)S(1)}, u32[]{:S(2)}, u32[]{:S(2)}) collective-permute-start(bf16[384,256]{1,0:T(8,128)(2,1)S(1)} %get-tuple-element.29.own), channel_id=1, source_target_pairs={{0,16},{8,24},{16,32},{24,40},{32,48},{40,56},{48,64},{64,80},{72,... | collective-permute-start | bytes 589832 | tf_op jit(solution)/shard_map/ppermute | solution.py:344
  37.2 4.4 %shard_map.123.intra = f32[384,1024]{1,0:T(8,128)S(1)} custom-call(s32[4]{0:T(128)S(1)} %copy-done.5, s32[4]{0:T(128)S(1)} %copy-done.6, bf16[384,1024]{1,0:T(8,128)(2,1)S(1)} %copy-done.3, bf16[384,1024]{1,0:T(8,128)(2,1)S(1)} %copy-done, bf16[384,1024]{1,0:T(8,128)(2,1)S(1)} %copy-done.1, f32[384,8]{1,0:T(8,128)S(1)} %get-tuple-element.17.cum, ...), custom_call_target="tpu_custom_call" | custom-call | tf_op jit(solution)/shard_map/pallas_call | solution.py:313
  41.7 0.0 copy-start.2
  41.7 0.0 collective-permute-done.7.passed
  41.7 1.6 %shard_map.127 = (f32[384,1024]{1,0:T(8,128)S(1)}, f32[8,384]{1,0:T(8,128)S(1)}) custom-call(s32[4]{0:T(128)S(1)} %copy-done.5, s32[4]{0:T(128)S(1)} %copy-done.6, bf16[384,1024]{1,0:T(8,128)(2,1)S(1)} %copy-done.3, f32[384,1024]{1,0:T(8,128)S(1)} %shard_map.123.intra, bf16[256,128]{1,0:T(8,128)(2,1)S(1)} %get-tuple-element.23.p0, ...), custom_call_target="tpu_custom_call" | custom-call | tf_op jit(solution)/shard_map/pallas_call | solution.py:313
  43.3 0.0 collective-permute-start.8
  43.3 1.2 %collective-permute-done.8 = f32[8,384]{1,0:T(8,128)S(1)} collective-permute-done((f32[8,384]{1,0:T(8,128)S(1)}, f32[8,384]{1,0:T(8,128)S(1)}, u32[]{:S(2)}, u32[]{:S(2)}) %collective-permute-start.8) | collective-permute-done | bytes 12320 | tf_op jit(solution)/shard_map/ppermute | solution.py:387
  44.5 1.6 %collective-permute-start.9 = (f32[8,384]{1,0:T(8,128)S(1)}, f32[8,384]{1,0:T(8,128)S(1)}, u32[]{:S(2)}, u32[]{:S(2)}) collective-permute-start(f32[8,384]{1,0:T(8,128)S(1)} %add.6), channel_id=1, source_target_pairs={{0,2},{1,3},{2,0},{3,1},{4,6},{5,7},{6,4},{7,5},{8,10},{9,11},{10,... | collective-permute-start | bytes 36872 | tf_op jit(solution)/shard_map/ppermute | solution.py:387
  46.0 1.3 %collective-permute-start.18 = (bf16[384,256]{1,0:T(8,128)(2,1)S(1)}, bf16[384,256]{1,0:T(8,128)(2,1)S(1)}, u32[]{:S(2)}, u32[]{:S(2)}) collective-permute-start(bf16[384,256]{1,0:T(8,128)(2,1)S(1)} %get-tuple-element.29.own), channel_id=1, source_target_pairs={{0,24},{8,32},{16,40},{24,48},{32,56},{40,64},{64,88},{72,96},{80,... | collective-permute-start | bytes 589832 | tf_op jit(solution)/shard_map/ppermute | solution.py:344
  47.3 0.0 collective-permute-done.11.rest_3_
  47.3 10.3 %collective-permute-start.12 = (bf16[384,256]{1,0:T(8,128)(2,1)S(1)}, bf16[384,256]{1,0:T(8,128)(2,1)S(1)}, u32[]{:S(2)}, u32[]{:S(2)}) collective-permute-start(bf16[384,256]{1,0:T(8,128)(2,1)S(1)} %collective-permute-done.11.rest_3_), channel_id=1, source_target_pairs={{32,40},{40,48},{48,56},{56,64},{96,104},{104,112},{112,120},{120,... | collective-permute-start | bytes 589832 | tf_op jit(solution)/shard_map/ppermute | solution.py:344
  57.7 0.0 collective-permute-done.16.rest_0_
  57.7 1.3 %collective-permute-start.13 = (bf16[384,256]{1,0:T(8,128)(2,1)S(1)}, bf16[384,256]{1,0:T(8,128)(2,1)S(1)}, u32[]{:S(2)}, u32[]{:S(2)}) collective-permute-start(bf16[384,256]{1,0:T(8,128)(2,1)S(1)} %collective-permute-done.11.rest_3_), channel_id=1, source_target_pairs={{32,48},{40,56},{48,64},{96,112},{104,120},{112,128},{160,176},{16... | collective-permute-start | bytes 589832 | tf_op jit(solution)/shard_map/ppermute | solution.py:344
  59.0 0.0 collective-permute-done.17.rest_1_
  59.0 1.3 %collective-permute-start.14 = (bf16[384,256]{1,0:T(8,128)(2,1)S(1)}, bf16[384,256]{1,0:T(8,128)(2,1)S(1)}, u32[]{:S(2)}, u32[]{:S(2)}) collective-permute-start(bf16[384,256]{1,0:T(8,128)(2,1)S(1)} %collective-permute-done.11.rest_3_), channel_id=1, source_target_pairs={{32,56},{40,64},{96,120},{104,128},{160,184},{168,192},{224,248},{... | collective-permute-start | bytes 589832 | tf_op jit(solution)/shard_map/ppermute | solution.py:344
  60.3 0.0 collective-permute-done.9
  60.3 0.7 collective-permute-start.15
  61.0 0.0 collective-permute-done.18.rest_2_
  61.0 3.2 %collective-permute-start.10 = (f32[8,384]{1,0:T(8,128)S(1)}, f32[8,384]{1,0:T(8,128)S(1)}, u32[]{:S(2)}, u32[]{:S(2)}) collective-permute-start(f32[8,384]{1,0:T(8,128)S(1)} %add.7.squares), channel_id=1, source_target_pairs={{0,4},{1,5},{2,6},{3,7},{4,0},{5,1},{6,2},{7,3},{8,12},{9,13},{10,... | collective-permute-start | bytes 36872 | tf_op jit(solution)/shard_map/ppermute | solution.py:387
  64.2 12.6 %shard_map.129 = (f32[8,384,128]{2,1,0:T(8,128)S(1)}, f32[8,384,256]{2,1,0:T(8,128)S(1)}) custom-call(s32[4]{0:T(128)S(1)} %copy-done.5, s32[4]{0:T(128)S(1)} %copy-done.6, bf16[384,1024]{1,0:T(8,128)(2,1)S(1)} %copy-done.2, bf16[384,256]{1,0:T(8,128)(2,1)S(1)} %get-tuple-element.29.own, bf16[384,256]{1,0:T(8,128)(2,1)S(1)} %collective-permute-done.16.rest_0_, ...), custom_call_target="tpu_custom_call" | custom-call | tf_op jit(solution)/shard_map/pallas_call | solution.py:313
  76.8 0.0 collective-permute-done.12.rest_0_
  76.8 0.0 collective-permute-done.13.rest_1_
  76.8 0.0 collective-permute-done.14.rest_2_
  76.9 0.0 copy-start.4
  76.9 0.0 copy-start.7
  76.9 8.8 %shard_map.130 = bf16[384,1024]{1,0:T(8,128)(2,1)} custom-call(s32[4]{0:T(128)S(1)} %copy-done.5, s32[4]{0:T(128)S(1)} %copy-done.6, bf16[384,1024]{1,0:T(8,128)(2,1)S(1)} %copy-done.2, bf16[384,256]{1,0:T(8,128)(2,1)S(1)} %get-tuple-element.29.own, bf16[384,256]{1,0:T(8,128)(2,1)S(1)} %collective-permute-done.12.rest_0_, ...), custom_call_target="tpu_custom_call" | custom-call | tf_op jit(solution)/shard_map/pallas_call | solution.py:313
  85.7 1.6 %shard_map.128 = bf16[384,1024]{1,0:T(8,128)(2,1)} custom-call(f32[384,1024]{1,0:T(8,128)S(1)} %get-tuple-element.27.heads, bf16[384,1024]{1,0:T(8,128)(2,1)S(1)} %copy-done.4, f32[1,1024]{1,0:T(1,128)S(1)} %bitcast.2, f32[8,384]{1,0:T(8,128)S(1)} %add.7.squares, f32[8,384]{1,0:T(8,128)S(1)} %collective-permute-done.10.others), custom_call_target="tpu_custom_call" | custom-call | tf_op jit(solution)/shard_map/pallas_call | solution.py:313
  (17 shorter events, 0.0 us)
Async XLA Ops:
  0.6 36.5 %copy-start = (bf16[384,1024]{1,0:T(8,128)(2,1)S(1)}, bf16[384,1024]{1,0:T(8,128)(2,1)}, u32[]{:S(2)}) copy-start(bf16[384,1024]{1,0:T(8,128)(2,1)} %key.1) | copy-start | bytes 2359300
  0.6 36.5 %copy-start.1 = (bf16[384,1024]{1,0:T(8,128)(2,1)S(1)}, bf16[384,1024]{1,0:T(8,128)(2,1)}, u32[]{:S(2)}) copy-start(bf16[384,1024]{1,0:T(8,128)(2,1)} %value.1) | copy-start | bytes 2359300
  0.7 36.5 %copy-start.3 = (bf16[384,1024]{1,0:T(8,128)(2,1)S(1)}, bf16[384,1024]{1,0:T(8,128)(2,1)}, u32[]{:S(2)}) copy-start(bf16[384,1024]{1,0:T(8,128)(2,1)} %query.5) | copy-start | bytes 2359300
  0.7 36.5 %copy-start.5 = (s32[4]{0:T(128)S(1)}, s32[4]{0:T(128)}, u32[]{:S(2)}) copy-start(s32[4]{0:T(128)} %starts.7) | copy-start | bytes 52
  0.7 36.5 %copy-start.6 = (s32[4]{0:T(128)S(1)}, s32[4]{0:T(128)}, u32[]{:S(2)}) copy-start(s32[4]{0:T(128)} %lengths.7) | copy-start | bytes 52
  4.0 4.7 %collective-permute-start = (bf16[272,128]{1,0:T(8,128)(2,1)S(1)}, bf16[272,128]{1,0:T(8,128)(2,1)S(1)}, u32[]{:S(2)}, u32[]{:S(2)}) collective-permute-start(bf16[272,128]{1,0:T(8,128)(2,1)S(1)} %get-tuple-element.20.s1), channel_id=1, source_target_pairs={{0,8},{8,16},{16,24},{24,0},{32,40},{40,48},{48,56},{56,32},{64,72... | collective-permute-start | bytes 208904 | tf_op jit(solution)/shard_map/ppermute | solution.py:344
  4.6 6.1 %collective-permute-start.1 = (bf16[272,128]{1,0:T(8,128)(2,1)S(1)}, bf16[272,128]{1,0:T(8,128)(2,1)S(1)}, u32[]{:S(2)}, u32[]{:S(2)}) collective-permute-start(bf16[272,128]{1,0:T(8,128)(2,1)S(1)} %get-tuple-element.21.s2), channel_id=1, source_target_pairs={{0,16},{8,24},{16,0},{24,8},{32,48},{40,56},{48,32},{56,40},{64,80... | collective-permute-start | bytes 208904 | tf_op jit(solution)/shard_map/ppermute | solution.py:344
  7.0 5.5 %collective-permute-start.2 = (bf16[272,128]{1,0:T(8,128)(2,1)S(1)}, bf16[272,128]{1,0:T(8,128)(2,1)S(1)}, u32[]{:S(2)}, u32[]{:S(2)}) collective-permute-start(bf16[272,128]{1,0:T(8,128)(2,1)S(1)} %get-tuple-element.22.s3), channel_id=1, source_target_pairs={{0,24},{8,0},{16,8},{24,16},{32,56},{40,32},{48,40},{56,48},{64,88... | collective-permute-start | bytes 208904 | tf_op jit(solution)/shard_map/ppermute | solution.py:344
  12.6 6.2 %collective-permute-start.3 = (bf16[256,128]{1,0:T(8,128)(2,1)S(1)}, bf16[256,128]{1,0:T(8,128)(2,1)S(1)}, u32[]{:S(2)}, u32[]{:S(2)}) collective-permute-start(bf16[256,128]{1,0:T(8,128)(2,1)S(1)} %shard_map.124), channel_id=1, source_target_pairs={{0,32},{8,40},{16,48},{24,56},{64,96},{72,104},{80,112},{88,120},{... | collective-permute-start | bytes 196616 | tf_op jit(solution)/shard_map/ppermute | solution.py:344
  18.9 4.3 %collective-permute-start.4 = (bf16[256,128]{1,0:T(8,128)(2,1)S(1)}, bf16[256,128]{1,0:T(8,128)(2,1)S(1)}, u32[]{:S(2)}, u32[]{:S(2)}) collective-permute-start(bf16[256,128]{1,0:T(8,128)(2,1)S(1)} %get-tuple-element.24), channel_id=1, source_target_pairs={{0,8},{8,16},{16,24},{24,0},{32,40},{40,48},{48,56},{56,32},{64,72... | collective-permute-start | bytes 196616 | tf_op jit(solution)/shard_map/ppermute | solution.py:344
  19.6 5.8 %collective-permute-start.5 = (bf16[256,128]{1,0:T(8,128)(2,1)S(1)}, bf16[256,128]{1,0:T(8,128)(2,1)S(1)}, u32[]{:S(2)}, u32[]{:S(2)}) collective-permute-start(bf16[256,128]{1,0:T(8,128)(2,1)S(1)} %get-tuple-element.25), channel_id=1, source_target_pairs={{0,16},{8,24},{16,0},{24,8},{32,48},{40,56},{48,32},{56,40},{64,80... | collective-permute-start | bytes 196616 | tf_op jit(solution)/shard_map/ppermute | solution.py:344
  20.7 5.5 %collective-permute-start.6 = (bf16[256,128]{1,0:T(8,128)(2,1)S(1)}, bf16[256,128]{1,0:T(8,128)(2,1)S(1)}, u32[]{:S(2)}, u32[]{:S(2)}) collective-permute-start(bf16[256,128]{1,0:T(8,128)(2,1)S(1)} %get-tuple-element.26), channel_id=1, source_target_pairs={{0,24},{8,0},{16,8},{24,16},{32,56},{40,32},{48,40},{56,48},{64,88... | collective-permute-start | bytes 196616 | tf_op jit(solution)/shard_map/ppermute | solution.py:344
  26.3 15.4 %collective-permute-start.7 = (bf16[4,256,128]{2,1,0:T(8,128)(2,1)S(1)}, bf16[4,256,128]{2,1,0:T(8,128)(2,1)S(1)}, u32[]{:S(2)}, u32[]{:S(2)}) collective-permute-start(bf16[4,256,128]{2,1,0:T(8,128)(2,1)S(1)} %shard_map.126), channel_id=1, source_target_pairs={{56,64},{120,128},{184,192},{57,65},{121,129},{185,193},{58,66},{1... | collective-permute-start | bytes 786440 | tf_op jit(solution)/shard_map/ppermute | solution.py:344
  30.9 16.4 %collective-permute-start.11 = (bf16[384,256]{1,0:T(8,128)(2,1)S(1)}, bf16[384,256]{1,0:T(8,128)(2,1)S(1)}, u32[]{:S(2)}, u32[]{:S(2)}) collective-permute-start(bf16[384,256]{1,0:T(8,128)(2,1)S(1)} %get-tuple-element.29.own), channel_id=1, source_target_pairs={{0,32},{8,40},{16,48},{24,56},{32,64},{64,96},{72,104},{80,112},{8... | collective-permute-start | bytes 589832 | tf_op jit(solution)/shard_map/ppermute | solution.py:344
  32.2 25.5 %collective-permute-start.16 = (bf16[384,256]{1,0:T(8,128)(2,1)S(1)}, bf16[384,256]{1,0:T(8,128)(2,1)S(1)}, u32[]{:S(2)}, u32[]{:S(2)}) collective-permute-start(bf16[384,256]{1,0:T(8,128)(2,1)S(1)} %get-tuple-element.29.own), channel_id=1, source_target_pairs={{0,8},{8,16},{16,24},{24,32},{32,40},{40,48},{48,56},{56,64},{64,7... | collective-permute-start | bytes 589832 | tf_op jit(solution)/shard_map/ppermute | solution.py:344
  35.9 23.1 %collective-permute-start.17 = (bf16[384,256]{1,0:T(8,128)(2,1)S(1)}, bf16[384,256]{1,0:T(8,128)(2,1)S(1)}, u32[]{:S(2)}, u32[]{:S(2)}) collective-permute-start(bf16[384,256]{1,0:T(8,128)(2,1)S(1)} %get-tuple-element.29.own), channel_id=1, source_target_pairs={{0,16},{8,24},{16,32},{24,40},{32,48},{40,56},{48,64},{64,80},{72,... | collective-permute-start | bytes 589832 | tf_op jit(solution)/shard_map/ppermute | solution.py:344
  41.7 22.5 %copy-start.2 = (bf16[384,1024]{1,0:T(8,128)(2,1)S(1)}, bf16[384,1024]{1,0:T(8,128)(2,1)}, u32[]{:S(2)}) copy-start(bf16[384,1024]{1,0:T(8,128)(2,1)} %query.7) | copy-start | bytes 2359300
  43.3 1.2 %collective-permute-start.8 = (f32[8,384]{1,0:T(8,128)S(1)}, f32[8,384]{1,0:T(8,128)S(1)}, u32[]{:S(2)}, u32[]{:S(2)}) collective-permute-start(f32[8,384]{1,0:T(8,128)S(1)} %get-tuple-element.28), channel_id=1, source_target_pairs={{0,1},{1,0},{2,3},{3,2},{4,5},{5,4},{6,7},{7,6},{8,9},{9,8},{10,11... | collective-permute-start | bytes 36872 | tf_op jit(solution)/shard_map/ppermute | solution.py:387
  44.5 15.9 %collective-permute-start.9 = (f32[8,384]{1,0:T(8,128)S(1)}, f32[8,384]{1,0:T(8,128)S(1)}, u32[]{:S(2)}, u32[]{:S(2)}) collective-permute-start(f32[8,384]{1,0:T(8,128)S(1)} %add.6), channel_id=1, source_target_pairs={{0,2},{1,3},{2,0},{3,1},{4,6},{5,7},{6,4},{7,5},{8,10},{9,11},{10,... | collective-permute-start | bytes 36872 | tf_op jit(solution)/shard_map/ppermute | solution.py:387
  46.0 15.0 %collective-permute-start.18 = (bf16[384,256]{1,0:T(8,128)(2,1)S(1)}, bf16[384,256]{1,0:T(8,128)(2,1)S(1)}, u32[]{:S(2)}, u32[]{:S(2)}) collective-permute-start(bf16[384,256]{1,0:T(8,128)(2,1)S(1)} %get-tuple-element.29.own), channel_id=1, source_target_pairs={{0,24},{8,32},{16,40},{24,48},{32,56},{40,64},{64,88},{72,96},{80,... | collective-permute-start | bytes 589832 | tf_op jit(solution)/shard_map/ppermute | solution.py:344
  47.3 29.5 %collective-permute-start.12 = (bf16[384,256]{1,0:T(8,128)(2,1)S(1)}, bf16[384,256]{1,0:T(8,128)(2,1)S(1)}, u32[]{:S(2)}, u32[]{:S(2)}) collective-permute-start(bf16[384,256]{1,0:T(8,128)(2,1)S(1)} %collective-permute-done.11.rest_3_), channel_id=1, source_target_pairs={{32,40},{40,48},{48,56},{56,64},{96,104},{104,112},{112,120},{120,... | collective-permute-start | bytes 589832 | tf_op jit(solution)/shard_map/ppermute | solution.py:344
  57.7 19.1 %collective-permute-start.13 = (bf16[384,256]{1,0:T(8,128)(2,1)S(1)}, bf16[384,256]{1,0:T(8,128)(2,1)S(1)}, u32[]{:S(2)}, u32[]{:S(2)}) collective-permute-start(bf16[384,256]{1,0:T(8,128)(2,1)S(1)} %collective-permute-done.11.rest_3_), channel_id=1, source_target_pairs={{32,48},{40,56},{48,64},{96,112},{104,120},{112,128},{160,176},{16... | collective-permute-start | bytes 589832 | tf_op jit(solution)/shard_map/ppermute | solution.py:344
  59.0 17.8 %collective-permute-start.14 = (bf16[384,256]{1,0:T(8,128)(2,1)S(1)}, bf16[384,256]{1,0:T(8,128)(2,1)S(1)}, u32[]{:S(2)}, u32[]{:S(2)}) collective-permute-start(bf16[384,256]{1,0:T(8,128)(2,1)S(1)} %collective-permute-done.11.rest_3_), channel_id=1, source_target_pairs={{32,56},{40,64},{96,120},{104,128},{160,184},{168,192},{224,248},{... | collective-permute-start | bytes 589832 | tf_op jit(solution)/shard_map/ppermute | solution.py:344
  60.3 16.5 %collective-permute-start.15 = (bf16[384,256]{1,0:T(8,128)(2,1)S(1)}, bf16[384,256]{1,0:T(8,128)(2,1)S(1)}, u32[]{:S(2)}, u32[]{:S(2)}) collective-permute-start(bf16[384,256]{1,0:T(8,128)(2,1)S(1)} %collective-permute-done.11.rest_3_), channel_id=1, source_target_pairs={{32,64},{96,128},{160,192},{33,65},{97,129},{161,193},{34,66},{98,... | collective-permute-start | bytes 589832 | tf_op jit(solution)/shard_map/ppermute | solution.py:344
  61.0 24.6 %collective-permute-start.10 = (f32[8,384]{1,0:T(8,128)S(1)}, f32[8,384]{1,0:T(8,128)S(1)}, u32[]{:S(2)}, u32[]{:S(2)}) collective-permute-start(f32[8,384]{1,0:T(8,128)S(1)} %add.7.squares), channel_id=1, source_target_pairs={{0,4},{1,5},{2,6},{3,7},{4,0},{5,1},{6,2},{7,3},{8,12},{9,13},{10,... | collective-permute-start | bytes 36872 | tf_op jit(solution)/shard_map/ppermute | solution.py:387
  76.9 8.8 %copy-start.4 = (bf16[384,1024]{1,0:T(8,128)(2,1)S(1)}, bf16[384,1024]{1,0:T(8,128)(2,1)}, u32[]{:S(2)}) copy-start(bf16[384,1024]{1,0:T(8,128)(2,1)} %gate.1) | copy-start | bytes 2359300
  76.9 8.8 %copy-start.7 = (f32[1024]{0:T(1024)S(1)}, f32[1024]{0:T(1024)}, u32[]{:S(2)}) copy-start(f32[1024]{0:T(1024)} %param.16) | copy-start | bytes 12292

commit v4 on v3

--- a/solution.py
+++ b/solution.py
@@ -109,7 +109,9 @@
             logs[w, 8 * j:8 * j + 8, :] = jnp.broadcast_to(one, (8, D))
 
 
-def row_kernel(own, r1, r2, r3, out, states, logs):
+def row_kernel(own, r1, r2, r3, kv, above_kv, out, both, states, logs):
+    both[0:T, :] = kv[...]
+    both[T:2 * T, :] = above_kv[...]
     gather_row(own, r1, r2, r3, states, logs)
     for j in range(PAIR):
         part = slice(j * D, (j + 1) * D)
@@ -215,7 +217,7 @@
         top[...] = top_in[...]
         acc[...] = acc_in[...]
     else:
-        top, acc, keys, values, asks = rest[FAR:]
+        above_kv, top, acc, keys, values, asks = rest[FAR:]
     room, place, bound, end_prev, end_cur = marks(starts, lengths)
     tail = place == 0
     count = jnp.where(tail, jnp.where(room > 0, SPAN, 0), place)
@@ -223,12 +225,23 @@
     begin = starts[begin_room] - begin_room * SPAN * T
     factor = (D ** -0.5) * 1.4426950408889634
     ones = jnp.ones((T, D), BF16)
-    for slot, ref in enumerate((own,) + far):
-        @pl.when((slot + low - 1 <= count) if slot else (low == 1))
+    first = low - 1
+
+    def take(slot, ref, needed):
+        @pl.when(needed)
         def _():
             keys[slot] = ref[:, 0:D]
             values[slot, :, 0:D] = ref[:, D:2 * D]
             values[slot, :, D:2 * D] = ones
+
+    if not last:
+        take(0, own, place >= 0)
+        take(FAR, above_kv, (place >= FAR))
+    for slot in range(1, FAR + 1):
+        used = slot + low - 1 <= count
+        if slot == FAR:
+            used = used & tail
+        take(slot, far[slot - 1].at[pl.ds(first // FAR * T, T), :], used)
 
     for h in range(H):
         asks[h] = query[:, h * D:(h + 1) * D]
@@ -362,7 +375,9 @@
                   [shape(T, width)], [pltpu.VMEM((T, T), F32)])
 
     table = [pltpu.VMEM((ROW, piece, D), F32), pltpu.VMEM((ROW, 8 * PAIR, D), F32)]
-    row_total, = call(row_kernel, 0, row, [shape(piece, D, kind=BF16)], table)
+    above_kv = send(kv, onward)
+    row_total, pair_kv = call(row_kernel, 0, (*row, kv, above_kv),
+                              [shape(piece, D, kind=BF16), shape(2 * T, 2 * D, kind=BF16)], table)
     above = send(row_total, onward)
     ready = call(
         prefix_kernel, 0, (*row, above), [shape(piece, D, kind=BF16)] * ROW,
@@ -372,9 +387,8 @@
     left, = call(pass_kernel, 0, (*slices, *before), [shape(ROW, piece, D, kind=BF16)])
     passed = send(left, next_room)
 
-    far_kv = [send(kv, window(m, rooms)) for m in range(1, ROW + 1)]
-    far_kv += [send(far_kv[ROW - 1], [(i + ROW, j) for i, j in window(m, rooms)])
-               for m in range(ROW + 1, SPAN + 1)]
+    far_kv = [send(pair_kv, window(m, rooms)) for m in range(1, ROW)]
+    far_kv += [send(pair_kv, [(i, i + ROW) for i in range(ROW, places - ROW, SPAN)])]
 
     heads, squares = call(
         carry_kernel, 2, (starts, lengths, lin_query, intra, *before, passed, cum),
@@ -392,9 +406,9 @@
             pltpu.VMEM((H, T, D), BF16)]
     asked = (starts, lengths, soft_query, kv)
     running = call(functools.partial(soft_kernel, low=1, last=False), 2,
-                   (*asked, *far_kv[:FAR]), held, room, room=20)
+                   (*asked, *far_kv, above_kv), held, room, room=20)
     soft_out, = call(functools.partial(soft_kernel, low=FAR + 1, last=True), 2,
-                     (*asked, *far_kv[FAR:], *running), [shape(T, width, kind=BF16)],
+                     (*asked, *far_kv, *running), [shape(T, width, kind=BF16)],
                      room + [pltpu.VMEM(x.shape, F32) for x in held], room=24)
 
     lin_out, = call(

time: 87.6 us -> 91.2 us (1.041)
  waiting for transfers between devices: 16.7 us -> 30.2 us
  starting transfers between devices: 36.9 us -> 26.8 us
    ppermute x16 -> x13, waiting for transfers between devices: 15.5 us -> 26.9 us  [send(): return lax.ppermute(x, 'ctx', pairs)]
    ppermute x16 -> x13, starting transfers between devices: 32.2 us -> 22 us  [send(): return lax.ppermute(x, 'ctx', pairs)]
    ppermute x3, waiting for transfers between devices: 1.2 us -> 3.31 us  [per_device(): lax.ppermute(squares, 'head', [(i, i ^ step) for i in range(share)])]
  transfers between devices with their start and end apart: 19 -> 16, of which waited for: 8 -> 7; matrix products, arithmetic and copies ran while one was open for 0% -> 0% of each run, Pallas kernels for 31% -> 30%
where the time goes in v4:
time: 91.2 us; the launch traced here: 90.6 us
  Pallas kernels  32.7 us (36%)
  waiting for transfers between devices  30.2 us (33%)
  starting transfers between devices  26.8 us (29%)
    pallas_call x9, Pallas kernels, call(): pl.pallas_call(kernel, in_specs=[smem] * tables + [given] * (len(operands...  32.7 us
    ppermute x13, waiting for transfers between devices, send(): return lax.ppermute(x, 'ctx', pairs)  26.9 us
    ppermute x13, starting transfers between devices, send(): return lax.ppermute(x, 'ctx', pairs)  22 us
    ppermute x3, starting transfers between devices, per_device(): lax.ppermute(squares, 'head', [(i, i ^ step) for i in range(share)])  4.76 us
    ppermute x3, waiting for transfers between devices, per_device(): lax.ppermute(squares, 'head', [(i, i ^ step) for i in range(share)])  3.31 us
  transfers between devices with their start and end apart: 16, of which 7 were waited for; matrix products, arithmetic and copies ran while one was open for 0% of the time, Pallas kernels for 30%

profile of v4, /device:TPU:38, one launch (start us, length us, event | category | flops | bytes accessed | tf_op | source)
XLA Modules:
  0.0 90.6 jit_solution(8179153675688815315)
XLA Ops:
  0.6 0.0 copy-start.1
  0.6 0.0 copy-start.2
  0.7 3.3 %shard_map.122 = (bf16[272,128]{1,0:T(8,128)(2,1)S(1)}, bf16[272,128]{1,0:T(8,128)(2,1)S(1)}, bf16[272,128]{1,0:T(8,128)(2,1)S(1)}, bf16[272,128]{1,0:T(8,128)(2...) custom-call(s32[4]{0:T(128)} %starts.7, s32[4]{0:T(128)} %lengths.7, ...), custom_call_target="tpu_custom_call" | custom-call | tf_op jit(solution)/shard_map/pallas_call | solution.py:326
  4.0 1.3 %collective-permute-start.3 = (bf16[384,256]{1,0:T(8,128)(2,1)S(1)}, bf16[384,256]{1,0:T(8,128)(2,1)S(1)}, u32[]{:S(2)}, u32[]{:S(2)}) collective-permute-start(bf16[384,256]{1,0:T(8,128)(2,1)S(1)} %get-tuple-element.25.kv.own), channel_id=1, source_target_pairs={{0,32},{8,40},{16,48},{24,56},{64,96},{72,104},{80,112},{88,120},{... | collective-permute-start | bytes 589832 | tf_op jit(solution)/shard_map/ppermute | solution.py:357
  5.3 0.6 collective-permute-start
  5.9 2.4 %collective-permute-start.1 = (bf16[272,128]{1,0:T(8,128)(2,1)S(1)}, bf16[272,128]{1,0:T(8,128)(2,1)S(1)}, u32[]{:S(2)}, u32[]{:S(2)}) collective-permute-start(bf16[272,128]{1,0:T(8,128)(2,1)S(1)} %get-tuple-element.23.s2), channel_id=1, source_target_pairs={{0,16},{8,24},{16,0},{24,8},{32,48},{40,56},{48,32},{56,40},{64,80... | collective-permute-start | bytes 208904 | tf_op jit(solution)/shard_map/ppermute | solution.py:357
  8.3 0.0 collective-permute-start.2
  8.3 1.8 %collective-permute-done.r1 = bf16[272,128]{1,0:T(8,128)(2,1)S(1)} collective-permute-done((bf16[272,128]{1,0:T(8,128)(2,1)S(1)}, bf16[272,128]{1,0:T(8,128)(2,1)S(1)}, u32[]{:S(2)}, u32[]{:S(2)}) %collective-permute-start) | collective-permute-done | bytes 69664 | tf_op jit(solution)/shard_map/ppermute | solution.py:357
  10.0 1.9 %collective-permute-done.1.r2 = bf16[272,128]{1,0:T(8,128)(2,1)S(1)} collective-permute-done((bf16[272,128]{1,0:T(8,128)(2,1)S(1)}, bf16[272,128]{1,0:T(8,128)(2,1)S(1)}, u32[]{:S(2)}, u32[]{:S(2)}) %collective-permute-start.1) | collective-permute-done | bytes 69664 | tf_op jit(solution)/shard_map/ppermute | solution.py:357
  11.9 1.8 %collective-permute-done.2.r3 = bf16[272,128]{1,0:T(8,128)(2,1)S(1)} collective-permute-done((bf16[272,128]{1,0:T(8,128)(2,1)S(1)}, bf16[272,128]{1,0:T(8,128)(2,1)S(1)}, u32[]{:S(2)}, u32[]{:S(2)}) %collective-permute-start.2) | collective-permute-done | bytes 69664 | tf_op jit(solution)/shard_map/ppermute | solution.py:357
  13.8 0.0 collective-permute-done.3.above_kv.rest_4_
  13.8 0.1 shard_map.124
  13.9 1.3 %collective-permute-start.4 = (bf16[256,128]{1,0:T(8,128)(2,1)S(1)}, bf16[256,128]{1,0:T(8,128)(2,1)S(1)}, u32[]{:S(2)}, u32[]{:S(2)}) collective-permute-start(bf16[256,128]{1,0:T(8,128)(2,1)S(1)} %get-tuple-element.26), channel_id=1, source_target_pairs={{0,32},{8,40},{16,48},{24,56},{64,96},{72,104},{80,112},{88,120},{... | collective-permute-start | bytes 196616 | tf_op jit(solution)/shard_map/ppermute | solution.py:357
  15.2 4.9 %collective-permute-done.4.above = bf16[256,128]{1,0:T(8,128)(2,1)S(1)} collective-permute-done((bf16[256,128]{1,0:T(8,128)(2,1)S(1)}, bf16[256,128]{1,0:T(8,128)(2,1)S(1)}, u32[]{:S(2)}, u32[]{:S(2)}) %collective-permute-start.4) | collective-permute-done | bytes 65568 | tf_op jit(solution)/shard_map/ppermute | solution.py:357
  20.1 0.2 shard_map.125
  20.2 0.7 collective-permute-start.5
  20.9 1.1 %collective-permute-start.6 = (bf16[256,128]{1,0:T(8,128)(2,1)S(1)}, bf16[256,128]{1,0:T(8,128)(2,1)S(1)}, u32[]{:S(2)}, u32[]{:S(2)}) collective-permute-start(bf16[256,128]{1,0:T(8,128)(2,1)S(1)} %get-tuple-element.29), channel_id=1, source_target_pairs={{0,16},{8,24},{16,0},{24,8},{32,48},{40,56},{48,32},{56,40},{64,80... | collective-permute-start | bytes 196616 | tf_op jit(solution)/shard_map/ppermute | solution.py:357
  22.0 5.8 %collective-permute-start.12 = (bf16[768,256]{1,0:T(8,128)(2,1)S(1)}, bf16[768,256]{1,0:T(8,128)(2,1)S(1)}, u32[]{:S(2)}, u32[]{:S(2)}) collective-permute-start(bf16[768,256]{1,0:T(8,128)(2,1)S(1)} %get-tuple-element.33), channel_id=1, source_target_pairs={{0,8},{8,16},{16,24},{24,32},{32,40},{40,48},{48,56},{56,64},{64,7... | collective-permute-start | bytes 1179656 | tf_op jit(solution)/shard_map/ppermute | solution.py:357
  27.8 1.3 %collective-permute-start.13 = (bf16[768,256]{1,0:T(8,128)(2,1)S(1)}, bf16[768,256]{1,0:T(8,128)(2,1)S(1)}, u32[]{:S(2)}, u32[]{:S(2)}) collective-permute-start(bf16[768,256]{1,0:T(8,128)(2,1)S(1)} %get-tuple-element.33), channel_id=1, source_target_pairs={{0,16},{8,24},{16,32},{24,40},{32,48},{40,56},{48,64},{64,80},{72,... | collective-permute-start | bytes 1179656 | tf_op jit(solution)/shard_map/ppermute | solution.py:357
  29.1 1.3 %collective-permute-start.14 = (bf16[768,256]{1,0:T(8,128)(2,1)S(1)}, bf16[768,256]{1,0:T(8,128)(2,1)S(1)}, u32[]{:S(2)}, u32[]{:S(2)}) collective-permute-start(bf16[768,256]{1,0:T(8,128)(2,1)S(1)} %get-tuple-element.33), channel_id=1, source_target_pairs={{0,24},{8,32},{16,40},{24,48},{32,56},{40,64},{64,88},{72,96},{80,... | collective-permute-start | bytes 1179656 | tf_op jit(solution)/shard_map/ppermute | solution.py:357
  30.4 0.0 collective-permute-done.5.p1
  30.4 0.7 collective-permute-start.15
  31.1 0.0 collective-permute-done.6.p2
  31.1 1.6 %collective-permute-start.7 = (bf16[256,128]{1,0:T(8,128)(2,1)S(1)}, bf16[256,128]{1,0:T(8,128)(2,1)S(1)}, u32[]{:S(2)}, u32[]{:S(2)}) collective-permute-start(bf16[256,128]{1,0:T(8,128)(2,1)S(1)} %get-tuple-element.30), channel_id=1, source_target_pairs={{0,24},{8,0},{16,8},{24,16},{32,56},{40,32},{48,40},{56,48},{64,88... | collective-permute-start | bytes 196616 | tf_op jit(solution)/shard_map/ppermute | solution.py:357
  32.7 16.5 %collective-permute-done.7.p3 = bf16[256,128]{1,0:T(8,128)(2,1)S(1)} collective-permute-done((bf16[256,128]{1,0:T(8,128)(2,1)S(1)}, bf16[256,128]{1,0:T(8,128)(2,1)S(1)}, u32[]{:S(2)}, u32[]{:S(2)}) %collective-permute-start.7) | collective-permute-done | bytes 65568 | tf_op jit(solution)/shard_map/ppermute | solution.py:357
  49.2 0.1 shard_map.126
  49.3 4.0 %collective-permute-start.8 = (bf16[4,256,128]{2,1,0:T(8,128)(2,1)S(1)}, bf16[4,256,128]{2,1,0:T(8,128)(2,1)S(1)}, u32[]{:S(2)}, u32[]{:S(2)}) collective-permute-start(bf16[4,256,128]{2,1,0:T(8,128)(2,1)S(1)} %shard_map.126), channel_id=1, source_target_pairs={{56,64},{120,128},{184,192},{57,65},{121,129},{185,193},{58,66},{1... | collective-permute-start | bytes 786440 | tf_op jit(solution)/shard_map/ppermute | solution.py:357
  53.4 4.4 %shard_map.123.intra = f32[384,1024]{1,0:T(8,128)S(1)} custom-call(s32[4]{0:T(128)S(1)} %copy-done.5, s32[4]{0:T(128)S(1)} %copy-done.6, bf16[384,1024]{1,0:T(8,128)(2,1)S(1)} %copy-done.3, bf16[384,1024]{1,0:T(8,128)(2,1)S(1)} %copy-done.1, bf16[384,1024]{1,0:T(8,128)(2,1)S(1)} %copy-done.2, f32[384,8]{1,0:T(8,128)S(1)} %get-tuple-element.19.cum, ...), custom_call_target="tpu_custom_call" | custom-call | tf_op jit(solution)/shard_map/pallas_call | solution.py:326
  57.9 0.0 copy-start
  57.9 0.0 collective-permute-done.8.passed
  57.9 1.6 %shard_map.127 = (f32[384,1024]{1,0:T(8,128)S(1)}, f32[8,384]{1,0:T(8,128)S(1)}) custom-call(s32[4]{0:T(128)S(1)} %copy-done.5, s32[4]{0:T(128)S(1)} %copy-done.6, bf16[384,1024]{1,0:T(8,128)(2,1)S(1)} %copy-done.3, f32[384,1024]{1,0:T(8,128)S(1)} %shard_map.123.intra, bf16[256,128]{1,0:T(8,128)(2,1)S(1)} %get-tuple-element.27.p0, ...), custom_call_target="tpu_custom_call" | custom-call | tf_op jit(solution)/shard_map/pallas_call | solution.py:326
  59.5 0.0 collective-permute-start.9
  59.5 1.2 %collective-permute-done.9 = f32[8,384]{1,0:T(8,128)S(1)} collective-permute-done((f32[8,384]{1,0:T(8,128)S(1)}, f32[8,384]{1,0:T(8,128)S(1)}, u32[]{:S(2)}, u32[]{:S(2)}) %collective-permute-start.9) | collective-permute-done | bytes 12320 | tf_op jit(solution)/shard_map/ppermute | solution.py:401
  60.7 1.6 %collective-permute-start.10 = (f32[8,384]{1,0:T(8,128)S(1)}, f32[8,384]{1,0:T(8,128)S(1)}, u32[]{:S(2)}, u32[]{:S(2)}) collective-permute-start(f32[8,384]{1,0:T(8,128)S(1)} %add.6), channel_id=1, source_target_pairs={{0,2},{1,3},{2,0},{3,1},{4,6},{5,7},{6,4},{7,5},{8,10},{9,11},{10,... | collective-permute-start | bytes 36872 | tf_op jit(solution)/shard_map/ppermute | solution.py:401
  62.2 2.1 %collective-permute-done.10 = f32[8,384]{1,0:T(8,128)S(1)} collective-permute-done((f32[8,384]{1,0:T(8,128)S(1)}, f32[8,384]{1,0:T(8,128)S(1)}, u32[]{:S(2)}, u32[]{:S(2)}) %collective-permute-start.10) | collective-permute-done | bytes 12320 | tf_op jit(solution)/shard_map/ppermute | solution.py:401
  64.4 3.2 %collective-permute-start.11 = (f32[8,384]{1,0:T(8,128)S(1)}, f32[8,384]{1,0:T(8,128)S(1)}, u32[]{:S(2)}, u32[]{:S(2)}) collective-permute-start(f32[8,384]{1,0:T(8,128)S(1)} %add.7.squares), channel_id=1, source_target_pairs={{0,4},{1,5},{2,6},{3,7},{4,0},{5,1},{6,2},{7,3},{8,12},{9,13},{10,... | collective-permute-start | bytes 36872 | tf_op jit(solution)/shard_map/ppermute | solution.py:401
  67.6 0.0 collective-permute-done.12.rest_0_
  67.6 0.0 collective-permute-done.13.rest_1_
  67.6 0.0 collective-permute-done.14.rest_2_
  67.6 0.0 collective-permute-done.15.rest_3_
  67.6 0.0 copy-done
  67.6 12.6 %shard_map.129 = (f32[8,384,128]{2,1,0:T(8,128)S(1)}, f32[8,384,256]{2,1,0:T(8,128)S(1)}) custom-call(s32[4]{0:T(128)S(1)} %copy-done.5, s32[4]{0:T(128)S(1)} %copy-done.6, bf16[384,1024]{1,0:T(8,128)(2,1)S(1)} %copy-done, bf16[384,256]{1,0:T(8,128)(2,1)S(1)} %get-tuple-element.25.kv.own, bf16[768,256]{1,0:T(8,128)(2,1)S(1)} %collective-permute-done.12.rest_0_, ...), custom_call_target="tpu_custom_call" | custom-call | tf_op jit(solution)/shard_map/pallas_call | solution.py:326
  80.2 0.0 copy-start.4
  80.2 0.0 copy-start.7
  80.3 8.8 %shard_map.130 = bf16[384,1024]{1,0:T(8,128)(2,1)} custom-call(s32[4]{0:T(128)S(1)} %copy-done.5, s32[4]{0:T(128)S(1)} %copy-done.6, bf16[384,1024]{1,0:T(8,128)(2,1)S(1)} %copy-done, bf16[384,256]{1,0:T(8,128)(2,1)S(1)} %get-tuple-element.25.kv.own, bf16[768,256]{1,0:T(8,128)(2,1)S(1)} %collective-permute-done.12.rest_0_, ...), custom_call_target="tpu_custom_call" | custom-call | tf_op jit(solution)/shard_map/pallas_call | solution.py:326
  89.0 0.0 collective-permute-done.11.others
  89.0 0.0 copy-done.7
  89.0 1.6 %shard_map.128 = bf16[384,1024]{1,0:T(8,128)(2,1)} custom-call(f32[384,1024]{1,0:T(8,128)S(1)} %get-tuple-element.31.heads, bf16[384,1024]{1,0:T(8,128)(2,1)S(1)} %copy-done.4, f32[1,1024]{1,0:T(1,128)S(1)} %bitcast.2, f32[8,384]{1,0:T(8,128)S(1)} %add.7.squares, f32[8,384]{1,0:T(8,128)S(1)} %collective-permute-done.11.others), custom_call_target="tpu_custom_call" | custom-call | tf_op jit(solution)/shard_map/pallas_call | solution.py:326
  (11 shorter events, 0.0 us)
Async XLA Ops:
  0.6 52.8 %copy-start.1 = (bf16[384,1024]{1,0:T(8,128)(2,1)S(1)}, bf16[384,1024]{1,0:T(8,128)(2,1)}, u32[]{:S(2)}) copy-start(bf16[384,1024]{1,0:T(8,128)(2,1)} %key.1) | copy-start | bytes 2359300
  0.6 52.8 %copy-start.2 = (bf16[384,1024]{1,0:T(8,128)(2,1)S(1)}, bf16[384,1024]{1,0:T(8,128)(2,1)}, u32[]{:S(2)}) copy-start(bf16[384,1024]{1,0:T(8,128)(2,1)} %value.1) | copy-start | bytes 2359300
  0.7 52.8 %copy-start.3 = (bf16[384,1024]{1,0:T(8,128)(2,1)S(1)}, bf16[384,1024]{1,0:T(8,128)(2,1)}, u32[]{:S(2)}) copy-start(bf16[384,1024]{1,0:T(8,128)(2,1)} %query.5) | copy-start | bytes 2359300
  0.7 52.8 %copy-start.5 = (s32[4]{0:T(128)S(1)}, s32[4]{0:T(128)}, u32[]{:S(2)}) copy-start(s32[4]{0:T(128)} %starts.7) | copy-start | bytes 52
  0.7 52.8 %copy-start.6 = (s32[4]{0:T(128)S(1)}, s32[4]{0:T(128)}, u32[]{:S(2)}) copy-start(s32[4]{0:T(128)} %lengths.7) | copy-start | bytes 52
  4.0 9.8 %collective-permute-start.3 = (bf16[384,256]{1,0:T(8,128)(2,1)S(1)}, bf16[384,256]{1,0:T(8,128)(2,1)S(1)}, u32[]{:S(2)}, u32[]{:S(2)}) collective-permute-start(bf16[384,256]{1,0:T(8,128)(2,1)S(1)} %get-tuple-element.25.kv.own), channel_id=1, source_target_pairs={{0,32},{8,40},{16,48},{24,56},{64,96},{72,104},{80,112},{88,120},{... | collective-permute-start | bytes 589832 | tf_op jit(solution)/shard_map/ppermute | solution.py:357
  5.3 4.7 %collective-permute-start = (bf16[272,128]{1,0:T(8,128)(2,1)S(1)}, bf16[272,128]{1,0:T(8,128)(2,1)S(1)}, u32[]{:S(2)}, u32[]{:S(2)}) collective-permute-start(bf16[272,128]{1,0:T(8,128)(2,1)S(1)} %get-tuple-element.22.s1), channel_id=1, source_target_pairs={{0,8},{8,16},{16,24},{24,0},{32,40},{40,48},{48,56},{56,32},{64,72... | collective-permute-start | bytes 208904 | tf_op jit(solution)/shard_map/ppermute | solution.py:357
  5.9 6.1 %collective-permute-start.1 = (bf16[272,128]{1,0:T(8,128)(2,1)S(1)}, bf16[272,128]{1,0:T(8,128)(2,1)S(1)}, u32[]{:S(2)}, u32[]{:S(2)}) collective-permute-start(bf16[272,128]{1,0:T(8,128)(2,1)S(1)} %get-tuple-element.23.s2), channel_id=1, source_target_pairs={{0,16},{8,24},{16,0},{24,8},{32,48},{40,56},{48,32},{56,40},{64,80... | collective-permute-start | bytes 208904 | tf_op jit(solution)/shard_map/ppermute | solution.py:357
  8.3 5.5 %collective-permute-start.2 = (bf16[272,128]{1,0:T(8,128)(2,1)S(1)}, bf16[272,128]{1,0:T(8,128)(2,1)S(1)}, u32[]{:S(2)}, u32[]{:S(2)}) collective-permute-start(bf16[272,128]{1,0:T(8,128)(2,1)S(1)} %get-tuple-element.24.s3), channel_id=1, source_target_pairs={{0,24},{8,0},{16,8},{24,16},{32,56},{40,32},{48,40},{56,48},{64,88... | collective-permute-start | bytes 208904 | tf_op jit(solution)/shard_map/ppermute | solution.py:357
  13.9 6.2 %collective-permute-start.4 = (bf16[256,128]{1,0:T(8,128)(2,1)S(1)}, bf16[256,128]{1,0:T(8,128)(2,1)S(1)}, u32[]{:S(2)}, u32[]{:S(2)}) collective-permute-start(bf16[256,128]{1,0:T(8,128)(2,1)S(1)} %get-tuple-element.26), channel_id=1, source_target_pairs={{0,32},{8,40},{16,48},{24,56},{64,96},{72,104},{80,112},{88,120},{... | collective-permute-start | bytes 196616 | tf_op jit(solution)/shard_map/ppermute | solution.py:357
  20.2 10.2 %collective-permute-start.5 = (bf16[256,128]{1,0:T(8,128)(2,1)S(1)}, bf16[256,128]{1,0:T(8,128)(2,1)S(1)}, u32[]{:S(2)}, u32[]{:S(2)}) collective-permute-start(bf16[256,128]{1,0:T(8,128)(2,1)S(1)} %get-tuple-element.28), channel_id=1, source_target_pairs={{0,8},{8,16},{16,24},{24,0},{32,40},{40,48},{48,56},{56,32},{64,72... | collective-permute-start | bytes 196616 | tf_op jit(solution)/shard_map/ppermute | solution.py:357
  20.9 10.2 %collective-permute-start.6 = (bf16[256,128]{1,0:T(8,128)(2,1)S(1)}, bf16[256,128]{1,0:T(8,128)(2,1)S(1)}, u32[]{:S(2)}, u32[]{:S(2)}) collective-permute-start(bf16[256,128]{1,0:T(8,128)(2,1)S(1)} %get-tuple-element.29), channel_id=1, source_target_pairs={{0,16},{8,24},{16,0},{24,8},{32,48},{40,56},{48,32},{56,40},{64,80... | collective-permute-start | bytes 196616 | tf_op jit(solution)/shard_map/ppermute | solution.py:357
  22.0 45.6 %collective-permute-start.12 = (bf16[768,256]{1,0:T(8,128)(2,1)S(1)}, bf16[768,256]{1,0:T(8,128)(2,1)S(1)}, u32[]{:S(2)}, u32[]{:S(2)}) collective-permute-start(bf16[768,256]{1,0:T(8,128)(2,1)S(1)} %get-tuple-element.33), channel_id=1, source_target_pairs={{0,8},{8,16},{16,24},{24,32},{32,40},{40,48},{48,56},{56,64},{64,7... | collective-permute-start | bytes 1179656 | tf_op jit(solution)/shard_map/ppermute | solution.py:357
  27.8 39.7 %collective-permute-start.13 = (bf16[768,256]{1,0:T(8,128)(2,1)S(1)}, bf16[768,256]{1,0:T(8,128)(2,1)S(1)}, u32[]{:S(2)}, u32[]{:S(2)}) collective-permute-start(bf16[768,256]{1,0:T(8,128)(2,1)S(1)} %get-tuple-element.33), channel_id=1, source_target_pairs={{0,16},{8,24},{16,32},{24,40},{32,48},{40,56},{48,64},{64,80},{72,... | collective-permute-start | bytes 1179656 | tf_op jit(solution)/shard_map/ppermute | solution.py:357
  29.1 38.4 %collective-permute-start.14 = (bf16[768,256]{1,0:T(8,128)(2,1)S(1)}, bf16[768,256]{1,0:T(8,128)(2,1)S(1)}, u32[]{:S(2)}, u32[]{:S(2)}) collective-permute-start(bf16[768,256]{1,0:T(8,128)(2,1)S(1)} %get-tuple-element.33), channel_id=1, source_target_pairs={{0,24},{8,32},{16,40},{24,48},{32,56},{40,64},{64,88},{72,96},{80,... | collective-permute-start | bytes 1179656 | tf_op jit(solution)/shard_map/ppermute | solution.py:357
  30.4 37.1 %collective-permute-start.15 = (bf16[768,256]{1,0:T(8,128)(2,1)S(1)}, bf16[768,256]{1,0:T(8,128)(2,1)S(1)}, u32[]{:S(2)}, u32[]{:S(2)}) collective-permute-start(bf16[768,256]{1,0:T(8,128)(2,1)S(1)} %get-tuple-element.33), channel_id=1, source_target_pairs={{32,64},{96,128},{160,192},{33,65},{97,129},{161,193},{34,66},{98,... | collective-permute-start | bytes 1179656 | tf_op jit(solution)/shard_map/ppermute | solution.py:357
  31.1 18.1 %collective-permute-start.7 = (bf16[256,128]{1,0:T(8,128)(2,1)S(1)}, bf16[256,128]{1,0:T(8,128)(2,1)S(1)}, u32[]{:S(2)}, u32[]{:S(2)}) collective-permute-start(bf16[256,128]{1,0:T(8,128)(2,1)S(1)} %get-tuple-element.30), channel_id=1, source_target_pairs={{0,24},{8,0},{16,8},{24,16},{32,56},{40,32},{48,40},{56,48},{64,88... | collective-permute-start | bytes 196616 | tf_op jit(solution)/shard_map/ppermute | solution.py:357
  49.3 8.6 %collective-permute-start.8 = (bf16[4,256,128]{2,1,0:T(8,128)(2,1)S(1)}, bf16[4,256,128]{2,1,0:T(8,128)(2,1)S(1)}, u32[]{:S(2)}, u32[]{:S(2)}) collective-permute-start(bf16[4,256,128]{2,1,0:T(8,128)(2,1)S(1)} %shard_map.126), channel_id=1, source_target_pairs={{56,64},{120,128},{184,192},{57,65},{121,129},{185,193},{58,66},{1... | collective-permute-start | bytes 786440 | tf_op jit(solution)/shard_map/ppermute | solution.py:357
  57.9 9.7 %copy-start = (bf16[384,1024]{1,0:T(8,128)(2,1)S(1)}, bf16[384,1024]{1,0:T(8,128)(2,1)}, u32[]{:S(2)}) copy-start(bf16[384,1024]{1,0:T(8,128)(2,1)} %query.7) | copy-start | bytes 2359300
  59.5 1.2 %collective-permute-start.9 = (f32[8,384]{1,0:T(8,128)S(1)}, f32[8,384]{1,0:T(8,128)S(1)}, u32[]{:S(2)}, u32[]{:S(2)}) collective-permute-start(f32[8,384]{1,0:T(8,128)S(1)} %get-tuple-element.32), channel_id=1, source_target_pairs={{0,1},{1,0},{2,3},{3,2},{4,5},{5,4},{6,7},{7,6},{8,9},{9,8},{10,11... | collective-permute-start | bytes 36872 | tf_op jit(solution)/shard_map/ppermute | solution.py:401
  60.7 3.7 %collective-permute-start.10 = (f32[8,384]{1,0:T(8,128)S(1)}, f32[8,384]{1,0:T(8,128)S(1)}, u32[]{:S(2)}, u32[]{:S(2)}) collective-permute-start(f32[8,384]{1,0:T(8,128)S(1)} %add.6), channel_id=1, source_target_pairs={{0,2},{1,3},{2,0},{3,1},{4,6},{5,7},{6,4},{7,5},{8,10},{9,11},{10,... | collective-permute-start | bytes 36872 | tf_op jit(solution)/shard_map/ppermute | solution.py:401
  64.4 24.7 %collective-permute-start.11 = (f32[8,384]{1,0:T(8,128)S(1)}, f32[8,384]{1,0:T(8,128)S(1)}, u32[]{:S(2)}, u32[]{:S(2)}) collective-permute-start(f32[8,384]{1,0:T(8,128)S(1)} %add.7.squares), channel_id=1, source_target_pairs={{0,4},{1,5},{2,6},{3,7},{4,0},{5,1},{6,2},{7,3},{8,12},{9,13},{10,... | collective-permute-start | bytes 36872 | tf_op jit(solution)/shard_map/ppermute | solution.py:401
  80.2 8.8 %copy-start.4 = (bf16[384,1024]{1,0:T(8,128)(2,1)S(1)}, bf16[384,1024]{1,0:T(8,128)(2,1)}, u32[]{:S(2)}) copy-start(bf16[384,1024]{1,0:T(8,128)(2,1)} %gate.1) | copy-start | bytes 2359300
  80.2 8.8 %copy-start.7 = (f32[1024]{0:T(1024)S(1)}, f32[1024]{0:T(1024)}, u32[]{:S(2)}) copy-start(f32[1024]{0:T(1024)} %param.16) | copy-start | bytes 12292

commit v5 on v2

--- a/solution.py
+++ b/solution.py
@@ -13,7 +13,7 @@
 SPAN = 8
 NEG = -1e30
 FAR = 4
-GROUP = 2
+GROUP = 4
 EPS = 1e-06
 GONE = -1e5
 ROW = 4
@@ -238,7 +238,8 @@
             x = ahead
             if h + span < H:
                 ahead = ask(h + span)
-            x = (x.reshape(span, size, T) + hidden[None]).reshape(many, T)
+            if hidden is not None:
+                x = (x.reshape(span, size, T) + hidden[None]).reshape(many, T)
             parts = [x[:, j * D:(j + 1) * D] for j in range(T // D)]
             best = functools.reduce(jnp.maximum, parts)
             peak = jnp.broadcast_to(jnp.max(best, axis=1, keepdims=True), (many, D)) * factor
@@ -267,10 +268,15 @@
     @pl.when(place > 0)
     def _():
         def one(slot, _):
-            attend(slot, T, jnp.where(iota((1, T), 1) < first_key(slot), NEG, 0.0))
+            attend(slot, T, None)
             return 0
 
-        lax.fori_loop(1, slots, one, 0)
+        farthest = count - low + 1
+        lax.fori_loop(1, jnp.minimum(slots, farthest), one, 0)
+
+        @pl.when((farthest >= 1) & (farthest < slots))
+        def _():
+            attend(farthest, T, jnp.where(iota((1, T), 1) < begin, NEG, 0.0))
 
     half = T // 2
 

time: 85.1 us -> 86.3 us (1.014)
  Pallas kernels: 32.6 us -> 33.8 us
    pallas_call x8, Pallas kernels: 32.6 us -> 33.8 us  [call(): pl.pallas_call(kernel, in_specs=[smem] * tables + [given] * (len(operands...]
where the time goes in v5:
time: 86.3 us; the launch traced here: 86 us
  starting transfers between devices  39.4 us (46%)
  Pallas kernels  33.8 us (39%)
  waiting for transfers between devices  11.8 us (14%)
  between operations  0.94 us (1%)
    ppermute x16, starting transfers between devices, send(): return lax.ppermute(x, 'ctx', pairs)  34.5 us
    pallas_call x8, Pallas kernels, call(): pl.pallas_call(kernel, in_specs=[smem] * tables + [given] * (len(operands...  33.8 us
    ppermute x16, waiting for transfers between devices, send(): return lax.ppermute(x, 'ctx', pairs)  11.8 us
    ppermute x3, starting transfers between devices, per_device(): lax.ppermute(squares, 'head', [(i, i ^ step) for i in range(share)])  4.86 us
  transfers between devices with their start and end apart: 19, of which 5 were waited for; matrix products, arithmetic and copies ran while one was open for 0% of the time, Pallas kernels for 24%

profile of v5, /device:TPU:38, one launch (start us, length us, event | category | flops | bytes accessed | tf_op | source)
XLA Modules:
  0.0 86.0 jit_solution(3519251860485528259)
XLA Ops:
  0.7 3.3 %shard_map.122 = (bf16[272,128]{1,0:T(8,128)(2,1)S(1)}, bf16[272,128]{1,0:T(8,128)(2,1)S(1)}, bf16[272,128]{1,0:T(8,128)(2,1)S(1)}, bf16[272,128]{1,0:T(8,128)(2...) custom-call(s32[4]{0:T(128)} %starts.7, s32[4]{0:T(128)} %lengths.7, ...), custom_call_target="tpu_custom_call" | custom-call | tf_op jit(solution)/shard_map/pallas_call | solution.py:309
  4.0 0.6 collective-permute-start
  4.6 2.4 %collective-permute-start.1 = (bf16[272,128]{1,0:T(8,128)(2,1)S(1)}, bf16[272,128]{1,0:T(8,128)(2,1)S(1)}, u32[]{:S(2)}, u32[]{:S(2)}) collective-permute-start(bf16[272,128]{1,0:T(8,128)(2,1)S(1)} %get-tuple-element.21), channel_id=1, source_target_pairs={{0,16},{8,24},{16,0},{24,8},{32,48},{40,56},{48,32},{56,40},{64,80... | collective-permute-start | bytes 208904 | tf_op jit(solution)/shard_map/ppermute | solution.py:340
  7.0 0.0 collective-permute-start.2
  7.0 1.8 %collective-permute-done.r1 = bf16[272,128]{1,0:T(8,128)(2,1)S(1)} collective-permute-done((bf16[272,128]{1,0:T(8,128)(2,1)S(1)}, bf16[272,128]{1,0:T(8,128)(2,1)S(1)}, u32[]{:S(2)}, u32[]{:S(2)}) %collective-permute-start) | collective-permute-done | bytes 69664 | tf_op jit(solution)/shard_map/ppermute | solution.py:340
  8.7 1.9 %collective-permute-done.1.r2 = bf16[272,128]{1,0:T(8,128)(2,1)S(1)} collective-permute-done((bf16[272,128]{1,0:T(8,128)(2,1)S(1)}, bf16[272,128]{1,0:T(8,128)(2,1)S(1)}, u32[]{:S(2)}, u32[]{:S(2)}) %collective-permute-start.1) | collective-permute-done | bytes 69664 | tf_op jit(solution)/shard_map/ppermute | solution.py:340
  10.6 1.8 %collective-permute-done.2.r3 = bf16[272,128]{1,0:T(8,128)(2,1)S(1)} collective-permute-done((bf16[272,128]{1,0:T(8,128)(2,1)S(1)}, bf16[272,128]{1,0:T(8,128)(2,1)S(1)}, u32[]{:S(2)}, u32[]{:S(2)}) %collective-permute-start.2) | collective-permute-done | bytes 69664 | tf_op jit(solution)/shard_map/ppermute | solution.py:340
  12.5 0.1 shard_map.124
  12.6 3.8 %collective-permute-start.3 = (bf16[272,128]{1,0:T(8,128)(2,1)S(1)}, bf16[272,128]{1,0:T(8,128)(2,1)S(1)}, u32[]{:S(2)}, u32[]{:S(2)}) collective-permute-start(bf16[272,128]{1,0:T(8,128)(2,1)S(1)} %shard_map.124), channel_id=1, source_target_pairs={{0,32},{8,40},{16,48},{24,56},{32,64},{40,72},{48,80},{56,88},{64,... | collective-permute-start | bytes 208904 | tf_op jit(solution)/shard_map/ppermute | solution.py:340
  16.4 0.7 collective-permute-start.4
  17.1 1.3 %collective-permute-start.11 = (bf16[384,256]{1,0:T(8,128)(2,1)S(1)}, bf16[384,256]{1,0:T(8,128)(2,1)S(1)}, u32[]{:S(2)}, u32[]{:S(2)}) collective-permute-start(bf16[384,256]{1,0:T(8,128)(2,1)S(1)} %get-tuple-element.29.own), channel_id=1, source_target_pairs={{0,32},{8,40},{16,48},{24,56},{32,64},{64,96},{72,104},{80,112},{8... | collective-permute-start | bytes 589832 | tf_op jit(solution)/shard_map/ppermute | solution.py:340
  18.4 9.3 %collective-permute-start.16 = (bf16[384,256]{1,0:T(8,128)(2,1)S(1)}, bf16[384,256]{1,0:T(8,128)(2,1)S(1)}, u32[]{:S(2)}, u32[]{:S(2)}) collective-permute-start(bf16[384,256]{1,0:T(8,128)(2,1)S(1)} %get-tuple-element.29.own), channel_id=1, source_target_pairs={{0,8},{8,16},{16,24},{24,32},{32,40},{40,48},{48,56},{56,64},{64,7... | collective-permute-start | bytes 589832 | tf_op jit(solution)/shard_map/ppermute | solution.py:340
  27.7 1.3 %collective-permute-start.17 = (bf16[384,256]{1,0:T(8,128)(2,1)S(1)}, bf16[384,256]{1,0:T(8,128)(2,1)S(1)}, u32[]{:S(2)}, u32[]{:S(2)}) collective-permute-start(bf16[384,256]{1,0:T(8,128)(2,1)S(1)} %get-tuple-element.29.own), channel_id=1, source_target_pairs={{0,16},{8,24},{16,32},{24,40},{32,48},{40,56},{48,64},{64,80},{72,... | collective-permute-start | bytes 589832 | tf_op jit(solution)/shard_map/ppermute | solution.py:340
  29.0 0.0 collective-permute-done.3.z1
  29.0 0.0 collective-permute-done.4.z2
  29.0 0.2 shard_map.125
  29.2 1.3 %collective-permute-start.5 = (bf16[256,128]{1,0:T(8,128)(2,1)S(1)}, bf16[256,128]{1,0:T(8,128)(2,1)S(1)}, u32[]{:S(2)}, u32[]{:S(2)}) collective-permute-start(bf16[256,128]{1,0:T(8,128)(2,1)S(1)} %get-tuple-element.24), channel_id=1, source_target_pairs={{0,8},{8,16},{16,24},{24,0},{32,40},{40,48},{48,56},{56,32},{64,72... | collective-permute-start | bytes 196616 | tf_op jit(solution)/shard_map/ppermute | solution.py:340
  30.5 3.1 %collective-permute-start.6 = (bf16[256,128]{1,0:T(8,128)(2,1)S(1)}, bf16[256,128]{1,0:T(8,128)(2,1)S(1)}, u32[]{:S(2)}, u32[]{:S(2)}) collective-permute-start(bf16[256,128]{1,0:T(8,128)(2,1)S(1)} %get-tuple-element.25), channel_id=1, source_target_pairs={{0,16},{8,24},{16,0},{24,8},{32,48},{40,56},{48,32},{56,40},{64,80... | collective-permute-start | bytes 196616 | tf_op jit(solution)/shard_map/ppermute | solution.py:340
  33.5 4.9 %collective-permute-done.5.p1 = bf16[256,128]{1,0:T(8,128)(2,1)S(1)} collective-permute-done((bf16[256,128]{1,0:T(8,128)(2,1)S(1)}, bf16[256,128]{1,0:T(8,128)(2,1)S(1)}, u32[]{:S(2)}, u32[]{:S(2)}) %collective-permute-start.5) | collective-permute-done | bytes 65568 | tf_op jit(solution)/shard_map/ppermute | solution.py:340
  38.4 0.0 collective-permute-start.7
  38.4 0.0 copy-done.1
  38.4 4.4 %shard_map.123.intra = f32[384,1024]{1,0:T(8,128)S(1)} custom-call(s32[4]{0:T(128)S(1)} %copy-done.5, s32[4]{0:T(128)S(1)} %copy-done.6, bf16[384,1024]{1,0:T(8,128)(2,1)S(1)} %copy-done.3, bf16[384,1024]{1,0:T(8,128)(2,1)S(1)} %copy-done, bf16[384,1024]{1,0:T(8,128)(2,1)S(1)} %copy-done.1, f32[384,8]{1,0:T(8,128)S(1)} %get-tuple-element.17.cum, ...), custom_call_target="tpu_custom_call" | custom-call | tf_op jit(solution)/shard_map/pallas_call | solution.py:309
  42.9 0.0 copy-start.2
  42.9 0.0 collective-permute-done.6.p2
  42.9 1.4 %collective-permute-done.7.p3 = bf16[256,128]{1,0:T(8,128)(2,1)S(1)} collective-permute-done((bf16[256,128]{1,0:T(8,128)(2,1)S(1)}, bf16[256,128]{1,0:T(8,128)(2,1)S(1)}, u32[]{:S(2)}, u32[]{:S(2)}) %collective-permute-start.7) | collective-permute-done | bytes 65568 | tf_op jit(solution)/shard_map/ppermute | solution.py:340
  44.3 1.6 %shard_map.126 = (f32[384,1024]{1,0:T(8,128)S(1)}, f32[8,384]{1,0:T(8,128)S(1)}) custom-call(s32[4]{0:T(128)S(1)} %copy-done.5, s32[4]{0:T(128)S(1)} %copy-done.6, bf16[384,1024]{1,0:T(8,128)(2,1)S(1)} %copy-done.3, f32[384,1024]{1,0:T(8,128)S(1)} %shard_map.123.intra, bf16[256,128]{1,0:T(8,128)(2,1)S(1)} %get-tuple-element.23.p0, ...), custom_call_target="tpu_custom_call" | custom-call | tf_op jit(solution)/shard_map/pallas_call | solution.py:309
  45.9 0.0 collective-permute-start.8
  45.9 1.4 %collective-permute-start.18 = (bf16[384,256]{1,0:T(8,128)(2,1)S(1)}, bf16[384,256]{1,0:T(8,128)(2,1)S(1)}, u32[]{:S(2)}, u32[]{:S(2)}) collective-permute-start(bf16[384,256]{1,0:T(8,128)(2,1)S(1)} %get-tuple-element.29.own), channel_id=1, source_target_pairs={{0,24},{8,32},{16,40},{24,48},{32,56},{40,64},{64,88},{72,96},{80,... | collective-permute-start | bytes 589832 | tf_op jit(solution)/shard_map/ppermute | solution.py:340
  47.4 0.0 collective-permute-done.8
  47.4 1.7 %collective-permute-start.9 = (f32[8,384]{1,0:T(8,128)S(1)}, f32[8,384]{1,0:T(8,128)S(1)}, u32[]{:S(2)}, u32[]{:S(2)}) collective-permute-start(f32[8,384]{1,0:T(8,128)S(1)} %add.6), channel_id=1, source_target_pairs={{0,2},{1,3},{2,0},{3,1},{4,6},{5,7},{6,4},{7,5},{8,10},{9,11},{10,... | collective-permute-start | bytes 36872 | tf_op jit(solution)/shard_map/ppermute | solution.py:381
  49.1 0.0 collective-permute-done.11.rest_3_
  49.1 6.2 %collective-permute-start.12 = (bf16[384,256]{1,0:T(8,128)(2,1)S(1)}, bf16[384,256]{1,0:T(8,128)(2,1)S(1)}, u32[]{:S(2)}, u32[]{:S(2)}) collective-permute-start(bf16[384,256]{1,0:T(8,128)(2,1)S(1)} %collective-permute-done.11.rest_3_), channel_id=1, source_target_pairs={{32,40},{40,48},{48,56},{56,64},{96,104},{104,112},{112,120},{120,... | collective-permute-start | bytes 589832 | tf_op jit(solution)/shard_map/ppermute | solution.py:340
  55.2 0.0 collective-permute-done.16.rest_0_
  55.2 1.3 %collective-permute-start.13 = (bf16[384,256]{1,0:T(8,128)(2,1)S(1)}, bf16[384,256]{1,0:T(8,128)(2,1)S(1)}, u32[]{:S(2)}, u32[]{:S(2)}) collective-permute-start(bf16[384,256]{1,0:T(8,128)(2,1)S(1)} %collective-permute-done.11.rest_3_), channel_id=1, source_target_pairs={{32,48},{40,56},{48,64},{96,112},{104,120},{112,128},{160,176},{16... | collective-permute-start | bytes 589832 | tf_op jit(solution)/shard_map/ppermute | solution.py:340
  56.5 0.0 collective-permute-done.17.rest_1_
  56.5 1.3 %collective-permute-start.14 = (bf16[384,256]{1,0:T(8,128)(2,1)S(1)}, bf16[384,256]{1,0:T(8,128)(2,1)S(1)}, u32[]{:S(2)}, u32[]{:S(2)}) collective-permute-start(bf16[384,256]{1,0:T(8,128)(2,1)S(1)} %collective-permute-done.11.rest_3_), channel_id=1, source_target_pairs={{32,56},{40,64},{96,120},{104,128},{160,184},{168,192},{224,248},{... | collective-permute-start | bytes 589832 | tf_op jit(solution)/shard_map/ppermute | solution.py:340
  57.8 0.0 collective-permute-done.9
  57.9 0.7 collective-permute-start.15
  58.5 0.0 collective-permute-done.18.rest_2_
  58.6 3.2 %collective-permute-start.10 = (f32[8,384]{1,0:T(8,128)S(1)}, f32[8,384]{1,0:T(8,128)S(1)}, u32[]{:S(2)}, u32[]{:S(2)}) collective-permute-start(f32[8,384]{1,0:T(8,128)S(1)} %add.7.squares), channel_id=1, source_target_pairs={{0,4},{1,5},{2,6},{3,7},{4,0},{5,1},{6,2},{7,3},{8,12},{9,13},{10,... | collective-permute-start | bytes 36872 | tf_op jit(solution)/shard_map/ppermute | solution.py:381
  61.7 13.3 %shard_map.128 = (f32[8,384,128]{2,1,0:T(8,128)S(1)}, f32[8,384,256]{2,1,0:T(8,128)S(1)}) custom-call(s32[4]{0:T(128)S(1)} %copy-done.5, s32[4]{0:T(128)S(1)} %copy-done.6, bf16[384,1024]{1,0:T(8,128)(2,1)S(1)} %copy-done.2, bf16[384,256]{1,0:T(8,128)(2,1)S(1)} %get-tuple-element.29.own, bf16[384,256]{1,0:T(8,128)(2,1)S(1)} %collective-permute-done.16.rest_0_, ...), custom_call_target="tpu_custom_call" | custom-call | tf_op jit(solution)/shard_map/pallas_call | solution.py:309
  75.0 0.0 collective-permute-done.10.others
  75.0 1.6 %shard_map.127 = bf16[384,1024]{1,0:T(8,128)(2,1)} custom-call(f32[384,1024]{1,0:T(8,128)S(1)} %get-tuple-element.27.heads, bf16[384,1024]{1,0:T(8,128)(2,1)S(1)} %copy-done.4, f32[1,1024]{1,0:T(1,128)S(1)} %bitcast.2, f32[8,384]{1,0:T(8,128)S(1)} %add.7.squares, f32[8,384]{1,0:T(8,128)S(1)} %collective-permute-done.10.others), custom_call_target="tpu_custom_call" | custom-call | tf_op jit(solution)/shard_map/pallas_call | solution.py:309
  76.6 0.0 collective-permute-done.12.rest_0_
  76.7 0.0 collective-permute-done.13.rest_1_
  76.7 0.0 collective-permute-done.14.rest_2_
  76.7 0.0 collective-permute-done.15.rest_3_
  76.7 9.3 %shard_map.129 = bf16[384,1024]{1,0:T(8,128)(2,1)} custom-call(s32[4]{0:T(128)S(1)} %copy-done.5, s32[4]{0:T(128)S(1)} %copy-done.6, bf16[384,1024]{1,0:T(8,128)(2,1)S(1)} %copy-done.2, bf16[384,256]{1,0:T(8,128)(2,1)S(1)} %get-tuple-element.29.own, bf16[384,256]{1,0:T(8,128)(2,1)S(1)} %collective-permute-done.12.rest_0_, ...), custom_call_target="tpu_custom_call" | custom-call | tf_op jit(solution)/shard_map/pallas_call | solution.py:309
  (16 shorter events, 0.0 us)
Async XLA Ops:
  0.6 37.8 %copy-start = (bf16[384,1024]{1,0:T(8,128)(2,1)S(1)}, bf16[384,1024]{1,0:T(8,128)(2,1)}, u32[]{:S(2)}) copy-start(bf16[384,1024]{1,0:T(8,128)(2,1)} %key.1) | copy-start | bytes 2359300
  0.6 37.8 %copy-start.1 = (bf16[384,1024]{1,0:T(8,128)(2,1)S(1)}, bf16[384,1024]{1,0:T(8,128)(2,1)}, u32[]{:S(2)}) copy-start(bf16[384,1024]{1,0:T(8,128)(2,1)} %value.1) | copy-start | bytes 2359300
  0.7 37.8 %copy-start.5 = (s32[4]{0:T(128)S(1)}, s32[4]{0:T(128)}, u32[]{:S(2)}) copy-start(s32[4]{0:T(128)} %starts.7) | copy-start | bytes 52
  0.7 37.8 %copy-start.6 = (s32[4]{0:T(128)S(1)}, s32[4]{0:T(128)}, u32[]{:S(2)}) copy-start(s32[4]{0:T(128)} %lengths.7) | copy-start | bytes 52
  0.7 37.8 %copy-start.3 = (bf16[384,1024]{1,0:T(8,128)(2,1)S(1)}, bf16[384,1024]{1,0:T(8,128)(2,1)}, u32[]{:S(2)}) copy-start(bf16[384,1024]{1,0:T(8,128)(2,1)} %query.5) | copy-start | bytes 2359300
  4.0 4.7 %collective-permute-start = (bf16[272,128]{1,0:T(8,128)(2,1)S(1)}, bf16[272,128]{1,0:T(8,128)(2,1)S(1)}, u32[]{:S(2)}, u32[]{:S(2)}) collective-permute-start(bf16[272,128]{1,0:T(8,128)(2,1)S(1)} %get-tuple-element.20), channel_id=1, source_target_pairs={{0,8},{8,16},{16,24},{24,0},{32,40},{40,48},{48,56},{56,32},{64,72... | collective-permute-start | bytes 208904 | tf_op jit(solution)/shard_map/ppermute | solution.py:340
  4.6 6.1 %collective-permute-start.1 = (bf16[272,128]{1,0:T(8,128)(2,1)S(1)}, bf16[272,128]{1,0:T(8,128)(2,1)S(1)}, u32[]{:S(2)}, u32[]{:S(2)}) collective-permute-start(bf16[272,128]{1,0:T(8,128)(2,1)S(1)} %get-tuple-element.21), channel_id=1, source_target_pairs={{0,16},{8,24},{16,0},{24,8},{32,48},{40,56},{48,32},{56,40},{64,80... | collective-permute-start | bytes 208904 | tf_op jit(solution)/shard_map/ppermute | solution.py:340
  7.0 5.5 %collective-permute-start.2 = (bf16[272,128]{1,0:T(8,128)(2,1)S(1)}, bf16[272,128]{1,0:T(8,128)(2,1)S(1)}, u32[]{:S(2)}, u32[]{:S(2)}) collective-permute-start(bf16[272,128]{1,0:T(8,128)(2,1)S(1)} %get-tuple-element.22), channel_id=1, source_target_pairs={{0,24},{8,0},{16,8},{24,16},{32,56},{40,32},{48,40},{56,48},{64,88... | collective-permute-start | bytes 208904 | tf_op jit(solution)/shard_map/ppermute | solution.py:340
  12.6 16.4 %collective-permute-start.3 = (bf16[272,128]{1,0:T(8,128)(2,1)S(1)}, bf16[272,128]{1,0:T(8,128)(2,1)S(1)}, u32[]{:S(2)}, u32[]{:S(2)}) collective-permute-start(bf16[272,128]{1,0:T(8,128)(2,1)S(1)} %shard_map.124), channel_id=1, source_target_pairs={{0,32},{8,40},{16,48},{24,56},{32,64},{40,72},{48,80},{56,88},{64,... | collective-permute-start | bytes 208904 | tf_op jit(solution)/shard_map/ppermute | solution.py:340
  16.4 12.6 %collective-permute-start.4 = (bf16[272,128]{1,0:T(8,128)(2,1)S(1)}, bf16[272,128]{1,0:T(8,128)(2,1)S(1)}, u32[]{:S(2)}, u32[]{:S(2)}) collective-permute-start(bf16[272,128]{1,0:T(8,128)(2,1)S(1)} %shard_map.124), channel_id=1, source_target_pairs={{0,64},{8,72},{16,80},{24,88},{64,128},{72,136},{80,144},{88,152},... | collective-permute-start | bytes 208904 | tf_op jit(solution)/shard_map/ppermute | solution.py:340
  17.1 31.9 %collective-permute-start.11 = (bf16[384,256]{1,0:T(8,128)(2,1)S(1)}, bf16[384,256]{1,0:T(8,128)(2,1)S(1)}, u32[]{:S(2)}, u32[]{:S(2)}) collective-permute-start(bf16[384,256]{1,0:T(8,128)(2,1)S(1)} %get-tuple-element.29.own), channel_id=1, source_target_pairs={{0,32},{8,40},{16,48},{24,56},{32,64},{64,96},{72,104},{80,112},{8... | collective-permute-start | bytes 589832 | tf_op jit(solution)/shard_map/ppermute | solution.py:340
  18.4 36.8 %collective-permute-start.16 = (bf16[384,256]{1,0:T(8,128)(2,1)S(1)}, bf16[384,256]{1,0:T(8,128)(2,1)S(1)}, u32[]{:S(2)}, u32[]{:S(2)}) collective-permute-start(bf16[384,256]{1,0:T(8,128)(2,1)S(1)} %get-tuple-element.29.own), channel_id=1, source_target_pairs={{0,8},{8,16},{16,24},{24,32},{32,40},{40,48},{48,56},{56,64},{64,7... | collective-permute-start | bytes 589832 | tf_op jit(solution)/shard_map/ppermute | solution.py:340
  27.7 28.8 %collective-permute-start.17 = (bf16[384,256]{1,0:T(8,128)(2,1)S(1)}, bf16[384,256]{1,0:T(8,128)(2,1)S(1)}, u32[]{:S(2)}, u32[]{:S(2)}) collective-permute-start(bf16[384,256]{1,0:T(8,128)(2,1)S(1)} %get-tuple-element.29.own), channel_id=1, source_target_pairs={{0,16},{8,24},{16,32},{24,40},{32,48},{40,56},{48,64},{64,80},{72,... | collective-permute-start | bytes 589832 | tf_op jit(solution)/shard_map/ppermute | solution.py:340
  29.2 9.2 %collective-permute-start.5 = (bf16[256,128]{1,0:T(8,128)(2,1)S(1)}, bf16[256,128]{1,0:T(8,128)(2,1)S(1)}, u32[]{:S(2)}, u32[]{:S(2)}) collective-permute-start(bf16[256,128]{1,0:T(8,128)(2,1)S(1)} %get-tuple-element.24), channel_id=1, source_target_pairs={{0,8},{8,16},{16,24},{24,0},{32,40},{40,48},{48,56},{56,32},{64,72... | collective-permute-start | bytes 196616 | tf_op jit(solution)/shard_map/ppermute | solution.py:340
  30.5 12.4 %collective-permute-start.6 = (bf16[256,128]{1,0:T(8,128)(2,1)S(1)}, bf16[256,128]{1,0:T(8,128)(2,1)S(1)}, u32[]{:S(2)}, u32[]{:S(2)}) collective-permute-start(bf16[256,128]{1,0:T(8,128)(2,1)S(1)} %get-tuple-element.25), channel_id=1, source_target_pairs={{0,16},{8,24},{16,0},{24,8},{32,48},{40,56},{48,32},{56,40},{64,80... | collective-permute-start | bytes 196616 | tf_op jit(solution)/shard_map/ppermute | solution.py:340
  38.4 5.9 %collective-permute-start.7 = (bf16[256,128]{1,0:T(8,128)(2,1)S(1)}, bf16[256,128]{1,0:T(8,128)(2,1)S(1)}, u32[]{:S(2)}, u32[]{:S(2)}) collective-permute-start(bf16[256,128]{1,0:T(8,128)(2,1)S(1)} %get-tuple-element.26), channel_id=1, source_target_pairs={{0,24},{8,0},{16,8},{24,16},{32,56},{40,32},{48,40},{56,48},{64,88... | collective-permute-start | bytes 196616 | tf_op jit(solution)/shard_map/ppermute | solution.py:340
  42.9 18.8 %copy-start.2 = (bf16[384,1024]{1,0:T(8,128)(2,1)S(1)}, bf16[384,1024]{1,0:T(8,128)(2,1)}, u32[]{:S(2)}) copy-start(bf16[384,1024]{1,0:T(8,128)(2,1)} %query.7) | copy-start | bytes 2359300
  45.9 29.1 %copy-start.4 = (bf16[384,1024]{1,0:T(8,128)(2,1)S(1)}, bf16[384,1024]{1,0:T(8,128)(2,1)}, u32[]{:S(2)}) copy-start(bf16[384,1024]{1,0:T(8,128)(2,1)} %gate.1) | copy-start | bytes 2359300
  45.9 29.1 %copy-start.7 = (f32[1024]{0:T(1024)S(1)}, f32[1024]{0:T(1024)}, u32[]{:S(2)}) copy-start(f32[1024]{0:T(1024)} %param.16) | copy-start | bytes 12292
  45.9 1.5 %collective-permute-start.8 = (f32[8,384]{1,0:T(8,128)S(1)}, f32[8,384]{1,0:T(8,128)S(1)}, u32[]{:S(2)}, u32[]{:S(2)}) collective-permute-start(f32[8,384]{1,0:T(8,128)S(1)} %get-tuple-element.28), channel_id=1, source_target_pairs={{0,1},{1,0},{2,3},{3,2},{4,5},{5,4},{6,7},{7,6},{8,9},{9,8},{10,11... | collective-permute-start | bytes 36872 | tf_op jit(solution)/shard_map/ppermute | solution.py:381
  45.9 12.6 %collective-permute-start.18 = (bf16[384,256]{1,0:T(8,128)(2,1)S(1)}, bf16[384,256]{1,0:T(8,128)(2,1)S(1)}, u32[]{:S(2)}, u32[]{:S(2)}) collective-permute-start(bf16[384,256]{1,0:T(8,128)(2,1)S(1)} %get-tuple-element.29.own), channel_id=1, source_target_pairs={{0,24},{8,32},{16,40},{24,48},{32,56},{40,64},{64,88},{72,96},{80,... | collective-permute-start | bytes 589832 | tf_op jit(solution)/shard_map/ppermute | solution.py:340
  47.4 10.4 %collective-permute-start.9 = (f32[8,384]{1,0:T(8,128)S(1)}, f32[8,384]{1,0:T(8,128)S(1)}, u32[]{:S(2)}, u32[]{:S(2)}) collective-permute-start(f32[8,384]{1,0:T(8,128)S(1)} %add.6), channel_id=1, source_target_pairs={{0,2},{1,3},{2,0},{3,1},{4,6},{5,7},{6,4},{7,5},{8,10},{9,11},{10,... | collective-permute-start | bytes 36872 | tf_op jit(solution)/shard_map/ppermute | solution.py:381
  49.1 27.6 %collective-permute-start.12 = (bf16[384,256]{1,0:T(8,128)(2,1)S(1)}, bf16[384,256]{1,0:T(8,128)(2,1)S(1)}, u32[]{:S(2)}, u32[]{:S(2)}) collective-permute-start(bf16[384,256]{1,0:T(8,128)(2,1)S(1)} %collective-permute-done.11.rest_3_), channel_id=1, source_target_pairs={{32,40},{40,48},{48,56},{56,64},{96,104},{104,112},{112,120},{120,... | collective-permute-start | bytes 589832 | tf_op jit(solution)/shard_map/ppermute | solution.py:340
  55.2 21.4 %collective-permute-start.13 = (bf16[384,256]{1,0:T(8,128)(2,1)S(1)}, bf16[384,256]{1,0:T(8,128)(2,1)S(1)}, u32[]{:S(2)}, u32[]{:S(2)}) collective-permute-start(bf16[384,256]{1,0:T(8,128)(2,1)S(1)} %collective-permute-done.11.rest_3_), channel_id=1, source_target_pairs={{32,48},{40,56},{48,64},{96,112},{104,120},{112,128},{160,176},{16... | collective-permute-start | bytes 589832 | tf_op jit(solution)/shard_map/ppermute | solution.py:340
  56.5 20.1 %collective-permute-start.14 = (bf16[384,256]{1,0:T(8,128)(2,1)S(1)}, bf16[384,256]{1,0:T(8,128)(2,1)S(1)}, u32[]{:S(2)}, u32[]{:S(2)}) collective-permute-start(bf16[384,256]{1,0:T(8,128)(2,1)S(1)} %collective-permute-done.11.rest_3_), channel_id=1, source_target_pairs={{32,56},{40,64},{96,120},{104,128},{160,184},{168,192},{224,248},{... | collective-permute-start | bytes 589832 | tf_op jit(solution)/shard_map/ppermute | solution.py:340
  57.9 18.8 %collective-permute-start.15 = (bf16[384,256]{1,0:T(8,128)(2,1)S(1)}, bf16[384,256]{1,0:T(8,128)(2,1)S(1)}, u32[]{:S(2)}, u32[]{:S(2)}) collective-permute-start(bf16[384,256]{1,0:T(8,128)(2,1)S(1)} %collective-permute-done.11.rest_3_), channel_id=1, source_target_pairs={{32,64},{96,128},{160,192},{33,65},{97,129},{161,193},{34,66},{98,... | collective-permute-start | bytes 589832 | tf_op jit(solution)/shard_map/ppermute | solution.py:340
  58.6 16.5 %collective-permute-start.10 = (f32[8,384]{1,0:T(8,128)S(1)}, f32[8,384]{1,0:T(8,128)S(1)}, u32[]{:S(2)}, u32[]{:S(2)}) collective-permute-start(f32[8,384]{1,0:T(8,128)S(1)} %add.7.squares), channel_id=1, source_target_pairs={{0,4},{1,5},{2,6},{3,7},{4,0},{5,1},{6,2},{7,3},{8,12},{9,13},{10,... | collective-permute-start | bytes 36872 | tf_op jit(solution)/shard_map/ppermute | solution.py:381
